TPU v7x, 32 devices: a whole 2x2x4 slice. The times are simulated.
32 devices in a mesh: group: 4 (over z), patch: 8 (over y, x, core).
Axes of the slice: x: 2, y: 2, z: 4, core: 2. Of those that a mesh axis runs over, the one named last changes fastest.
Arguments:
- volume: float32 [4096, 8, 1024], P(('group', 'patch')), may hold values from 0.02 to 18, as said below
- block_place: int32 [4096], P(('group', 'patch')), may hold values from 0 to 4095, as said below
- measured: float32 [2, 512, 384], P(None, 'patch'), may hold values from 0.5 to 5.5
- live_rays: int32 [2, 512], replicated, may hold values from 24 to 48
Outputs:
- final_volume: float32 [4096, 8, 1024], P(('group', 'patch'))
- last_residual: float32 [4, 128, 384], P('group', 'patch')
Inputs may be any that keep to these rules, and one draw needn't show every extreme that they name: block_place lists the block positions of the 64 x 64 grid in the order of a Hilbert curve over that grid, begun at a drawn point of the curve (continuing from its end to its start) and turned or mirrored by one of the grid's eight symmetries; each position appears once. `volume`: positive.
All inputs are finite; a program needn't handle non-finite values.
Results may differ from a plain program's by a relative error of at most 0.0007.
Values may be sent and summed in bfloat16 or wider, within the bound.
A program may use at most 192 MiB of HBM per device.

v0:
```python
import math

import jax
import jax.numpy as jnp
import numpy as np
from jax import lax
from jax.experimental import pallas as pl
from jax.experimental.pallas import tpu as pltpu
from jax.sharding import PartitionSpec as P

IMG_BLK = 64
BLK_SIDE = 32
RAYS_TILE = 48
NTILE = 64
ANG_SUB = 8
SUBSETS = 2

spread = 1.5
relax = 0.9

SUB = 8
NQ = (BLK_SIDE // SUB) ** 2
R = 16
VOX = BLK_SIDE * BLK_SIDE
RAYS = NTILE * RAYS_TILE
LANES = 128
PAD = 32
SPAN = 128
TALL = RAYS + SPAN
VMEM_LIMIT = 60 * 1024 * 1024


def angles(subset):
    return [math.pi * (a * SUBSETS + subset) / (ANG_SUB * SUBSETS) for a in range(ANG_SUB)]


def geometry(subset):
    v = np.arange(VOX)
    col = (v % BLK_SIDE) + 0.5 - BLK_SIDE / 2
    row = (v // BLK_SIDE) + 0.5 - BLK_SIDE / 2
    q_of = (v // BLK_SIDE // SUB) * (BLK_SIDE // SUB) + (v % BLK_SIDE) // SUB
    base = np.zeros((ANG_SUB, VOX), np.float64)
    first = np.zeros((ANG_SUB, NQ), np.int64)
    for a, theta in enumerate(angles(subset)):
        off = col * math.cos(theta) + row * math.sin(theta)
        for q in range(NQ):
            mine = q_of == q
            first[a, q] = math.floor(off[mine].min() - spread)
            base[a, mine] = off[mine] - first[a, q]
    return base.astype(np.float32), first.astype(np.int32)


def fill_grid(base_ref, e_scr):
    ray = lax.broadcasted_iota(jnp.int32, (R, VOX), 0).astype(jnp.float32)
    for a in range(ANG_SUB):
        e_scr[a * R:(a + 1) * R, :] = (base_ref[a:a + 1, :] - ray) * (1.0 / spread)


def make_footprint(e_scr, f_scr, frac_ref, b):
    for a in range(ANG_SUB):
        t = e_scr[a * R:(a + 1) * R, :] + frac_ref[b, a]
        bump = jnp.maximum(1.0 - t * t, 0.0)
        f_scr[a * R:(a + 1) * R, :] = (bump * bump).astype(jnp.bfloat16)


TILES = RAYS // SPAN


def list_tiles(win_ref, tiles):
    def step(i, n):
        hit = win_ref[i]
        tiles[n] = i
        return n + hit

    n = lax.fori_loop(0, ANG_SUB * TILES, step, 0)
    tiles[n] = tiles[jnp.maximum(n - 1, 0)]
    return (n + 1) // 2


def over_tiles(tiles, half_count, body):
    def pair(i, c):
        for j in range(2):
            at = tiles[2 * i + j]
            body(at // TILES, lax.rem(at, TILES))
        return c

    lax.fori_loop(0, half_count, pair, 0)


def aligned(x, m):
    return pl.multiple_of(x, m)


def forward_kernel(nb, lo_ref, frac_ref, win_ref, first_ref, vol_ref, base_ref, out_ref,
                   e_scr, f_even, f_odd, m_scr, acc, tiles):
    f_bufs = (f_even, f_odd)
    step = pl.program_id(0)

    @pl.when(step == 0)
    def _():
        fill_grid(base_ref, e_scr)
        v = lax.broadcasted_iota(jnp.int32, (LANES, VOX), 1)
        line = lax.broadcasted_iota(jnp.int32, (LANES, VOX), 0)
        q_of = (v // (BLK_SIDE * SUB)) * (BLK_SIDE // SUB) + (v % BLK_SIDE) // SUB
        m_scr[...] = jnp.where(q_of == line // 8, 1.0, 0.0).astype(jnp.bfloat16)
        zero = jnp.zeros((2 * SPAN, LANES), jnp.float32)

        tiles[ANG_SUB * TILES + 1] = list_tiles(win_ref, tiles)

        def clear(a, i):
            acc[pl.ds(aligned(a * TALL + i * SPAN, SPAN), 2 * SPAN), :] = zero

        over_tiles(tiles, tiles[ANG_SUB * TILES + 1], clear)

    for i in range(nb):
        b = step * nb + i
        f_scr = f_bufs[i % 2]
        make_footprint(e_scr, f_scr, frac_ref, b)
        rounded = vol_ref[i].astype(jnp.bfloat16)
        spreadv = jnp.tile(rounded, (NQ, 1)) * m_scr[...]
        part = lax.dot_general(f_scr[...], spreadv, (((1,), (1,)), ((), ())),
                               preferred_element_type=jnp.float32)
        for a in range(ANG_SUB):
            at = pl.ds(a * TALL + PAD + lo_ref[b, a], R)
            acc[at, :] += part[a * R:(a + 1) * R, :]

    @pl.when(step == pl.num_programs(0) - 1)
    def _():
        out_ref[...] = jnp.zeros_like(out_ref)
        span = SPAN
        lane_q = lax.broadcasted_iota(jnp.int32, (span, LANES), 1) // 8
        row_j = lax.broadcasted_iota(jnp.int32, (span, LANES), 0) % 16
        pick = lane_q == row_j

        def merge(a, i):
            k = i * span
            total = jnp.zeros((span, LANES), jnp.float32)
            for q in range(NQ):
                src = a * TALL + PAD + k - first_ref[a, q]
                total = jnp.where(lane_q == q, acc[pl.ds(src, span), :], total)
            for s in (64, 32, 16, 8):
                total = total + pltpu.roll(total, s, 1)
            total = jnp.where(pick, total, 0.0)
            out = jnp.sum(total.reshape(span // 16, 16, LANES), axis=1)
            out_ref[pl.ds(aligned(a * (RAYS // 16) + i * 8, 8), 8), :] = out

        over_tiles(tiles, tiles[ANG_SUB * TILES + 1], merge)


def backward_kernel(nb, lo_ref, frac_ref, win_ref, first_ref, vol_ref, base_ref, res_ref, out_ref,
                    e_scr, f_even, f_odd, rb, dd, tiles):
    f_bufs = (f_even, f_odd)
    step = pl.program_id(0)

    @pl.when(step == 0)
    def _():
        fill_grid(base_ref, e_scr)
        span = SPAN
        lane_q = lax.broadcasted_iota(jnp.int32, (span, LANES), 1) // 8
        row_j = lax.broadcasted_iota(jnp.int32, (span, LANES), 0) % 16
        pick = lane_q == row_j
        fold = jnp.where(
            lax.broadcasted_iota(jnp.int32, (LANES, LANES), 0) % 8
            == lax.broadcasted_iota(jnp.int32, (LANES, LANES), 1) % 8, 1.0, 0.0).astype(jnp.bfloat16)

        count = list_tiles(win_ref, tiles)

        def widen(a, i):
            rows = res_ref[pl.ds(aligned(a * (RAYS // 16) + i * 8, 8), 8), :]
            wide = jnp.broadcast_to(rows[:, None, :], (8, 16, LANES)).reshape(span, LANES)
            wide = jnp.where(pick, wide, 0.0).astype(jnp.bfloat16)
            rb[pl.ds(aligned(a * TALL + PAD + i * span, 8), span), :] = jnp.dot(
                wide, fold, preferred_element_type=jnp.float32)

        def shift(a, i):
            k = i * span
            total = jnp.zeros((span, LANES), jnp.float32)
            for q in range(NQ):
                src = a * TALL + PAD + k + first_ref[a, q]
                total = jnp.where(lane_q == q, rb[pl.ds(src, span), :], total)
            dd[pl.ds(aligned(a * RAYS + k, span), span), :] = total

        over_tiles(tiles, count, widen)
        over_tiles(tiles, count, shift)

    width = SUB * BLK_SIDE
    group = BLK_SIDE // SUB
    lane = lax.broadcasted_iota(jnp.int32, (8, width), 1)
    col_group = (lane % BLK_SIDE) // SUB

    for i in range(nb):
        b = step * nb + i
        f_scr = f_bufs[i % 2]
        make_footprint(e_scr, f_scr, frac_ref, b)
        rows = jnp.concatenate(
            [dd[pl.ds(a * RAYS + lo_ref[b, a], R), :] for a in range(ANG_SUB)], axis=0)
        turned = jnp.transpose(rows)
        ones = jnp.ones((8, ANG_SUB * R), jnp.float32)
        for g in range(group):
            lhs = jnp.concatenate([turned[g * 32:(g + 1) * 32], ones], axis=0).astype(jnp.bfloat16)
            at = slice(g * width, (g + 1) * width)
            part = jnp.dot(lhs, f_scr[:, at], preferred_element_type=jnp.float32)
            back = part[0:8]
            for j in range(1, group):
                back = jnp.where(col_group == j, part[j * 8:(j + 1) * 8], back)
            col_sum = part[32:40]
            out_ref[i, :, at] = jnp.maximum(vol_ref[i, :, at] + relax * back / col_sum, 0.0)


def ray_sum_kernel(c_ref, s_ref, k_ref, out_ref):
    side = IMG_BLK * BLK_SIDE
    half = side * 0.5
    for u in range(c_ref.shape[0]):
        cs = c_ref[u] * (1.0 / spread)
        sn = s_ref[u] * (1.0 / spread)
        inv = 1.0 / cs
        ray = k_ref[u] * (1.0 / spread)

        def row(i, total):
            y = i.astype(jnp.float32) + (0.5 - half)
            w = ray - y * sn
            mid = jnp.clip(jnp.floor(w * inv) + 0.5, 2.5 - half, half - 2.5)
            t0 = mid * cs - w
            for t in (t0 - 2 * cs, t0 - cs, t0, t0 + cs, t0 + 2 * cs):
                bump = jnp.maximum(1.0 - t * t, 0.0)
                total = total + bump * bump
            return total

        out_ref[u] = lax.fori_loop(0, side, row, jnp.zeros(out_ref.shape[1:], jnp.float32), unroll=8)


def exchange_kernel(part_ref, mine_ref, on_ref, rs_ref, full_ref, own_ref,
                    half, inbox, sums, stage, gathered, send_sem, recv_sem,
                    pair_send, pair_recv, out_send, out_recv, back_send, back_recv):
    g, p = lax.axis_index("group"), lax.axis_index("patch")
    groups, pairs = inbox.shape[1], inbox.shape[0]
    n = groups * pairs
    parity, column = lax.rem(p, 2), p // 2
    me = column * groups + g
    partner = (g, column * 2 + 1 - parity)
    mesh_id = pl.DeviceIdType.MESH

    def peer(d):
        at = lax.rem(me + d, n)
        return at // groups, lax.rem(at, groups)

    barrier = pltpu.get_barrier_semaphore()
    pl.semaphore_signal(barrier, inc=1, device_id=partner, device_id_type=mesh_id)

    def greet(d, c):
        pc, pg = peer(d)
        pl.semaphore_signal(barrier, inc=1, device_id=(pg, pc * 2 + parity), device_id_type=mesh_id)
        return c

    lax.fori_loop(1, n, greet, 0)
    pl.semaphore_wait(barrier, n)

    swap = pltpu.make_async_remote_copy(
        src_ref=part_ref.at[:, 1 - parity], dst_ref=half, send_sem=pair_send, recv_sem=pair_recv,
        device_id=partner, device_id_type=mesh_id)
    swap.start()
    swap.wait()
    for i in range(pairs):
        sums[i] = part_ref[i, parity] + half[i]

    def to_owner(d):
        pc, pg = peer(d)
        return pltpu.make_async_remote_copy(
            src_ref=sums.at[pc, pg], dst_ref=inbox.at[column, g], send_sem=send_sem.at[d],
            recv_sem=recv_sem.at[d], device_id=(pg, pc * 2 + parity), device_id_type=mesh_id)

    def go(d, c):
        to_owner(d).start()
        return c

    def done(d, c):
        to_owner(d).wait()
        return c

    lax.fori_loop(1, n, go, 0)
    inbox[column, g] = sums[column, g]
    lax.fori_loop(1, n, done, 0)
    total = jnp.zeros(mine_ref.shape, jnp.float32)
    for i in range(pairs):
        for j in range(groups):
            total = total + inbox[i, j]
    residual = (mine_ref[...] - total / rs_ref[...]) * on_ref[...]
    own_ref[...] = residual
    stage[...] = residual.astype(jnp.bfloat16)

    def to_all(d):
        pc, pg = peer(d)
        return pltpu.make_async_remote_copy(
            src_ref=stage, dst_ref=gathered.at[column, parity, g], send_sem=out_send.at[d],
            recv_sem=out_recv.at[d], device_id=(pg, pc * 2 + parity), device_id_type=mesh_id)

    def go_all(d, c):
        to_all(d).start()
        return c

    def done_all(d, c):
        to_all(d).wait()
        return c

    lax.fori_loop(1, n, go_all, 0)
    gathered[column, parity, g] = stage[...]
    lax.fori_loop(1, n, done_all, 0)
    share = pltpu.make_async_remote_copy(
        src_ref=gathered.at[:, parity], dst_ref=gathered.at[:, parity], send_sem=back_send,
        recv_sem=back_recv, device_id=partner, device_id_type=mesh_id)
    share.start()
    share.wait()
    for i in range(pairs):
        full_ref[i] = gathered[i].astype(jnp.float32)


def exchange(partial, mine, on, rs, groups, patches):
    lines = mine.shape[0]
    pairs = patches // 2
    shape = (pairs, 2, groups, lines, LANES)
    n = pairs * groups
    dma = pltpu.SemaphoreType.DMA
    vmem = pl.BlockSpec(memory_space=pltpu.VMEM)
    full, own = pl.pallas_call(
        exchange_kernel,
        in_specs=[vmem] * 4,
        out_specs=[vmem] * 2,
        out_shape=[jax.ShapeDtypeStruct(shape, jnp.float32),
                   jax.ShapeDtypeStruct((lines, LANES), jnp.float32)],
        scratch_shapes=[pltpu.VMEM((pairs, groups, lines, LANES), jnp.float32),
                        pltpu.VMEM((pairs, groups, lines, LANES), jnp.float32),
                        pltpu.VMEM((pairs, groups, lines, LANES), jnp.float32),
                        pltpu.VMEM((lines, LANES), jnp.bfloat16),
                        pltpu.VMEM(shape, jnp.bfloat16),
                        dma((n,)), dma((n,)), dma, dma, dma((n,)), dma((n,)), dma, dma],
        compiler_params=pltpu.CompilerParams(collective_id=0, has_side_effects=True),
        name="exchange",
    )(partial.reshape(shape), mine, on, rs)
    return full.reshape(partial.shape), own


def smem():
    return pl.BlockSpec(memory_space=pltpu.SMEM)


def forward(volume, lo, frac, win, base, first):
    blocks, slices, _ = volume.shape
    nb = 8
    lines = ANG_SUB * RAYS // 16
    return pl.pallas_call(
        lambda *refs: forward_kernel(nb, *refs),
        grid=(blocks // nb,),
        in_specs=[smem(), smem(), smem(), smem(),
                  pl.BlockSpec((nb, slices, VOX), lambda i: (i, 0, 0)),
                  pl.BlockSpec((ANG_SUB, VOX), lambda i: (0, 0))],
        out_specs=pl.BlockSpec((lines, LANES), lambda i: (0, 0)),
        out_shape=jax.ShapeDtypeStruct((lines, LANES), jnp.float32),
        scratch_shapes=[pltpu.VMEM((ANG_SUB * R, VOX), jnp.float32),
                        pltpu.VMEM((ANG_SUB * R, VOX), jnp.bfloat16),
                        pltpu.VMEM((ANG_SUB * R, VOX), jnp.bfloat16),
                        pltpu.VMEM((LANES, VOX), jnp.bfloat16),
                        pltpu.VMEM((ANG_SUB * TALL, LANES), jnp.float32),
                        pltpu.SMEM((ANG_SUB * TILES + 2,), jnp.int32)],
        compiler_params=pltpu.CompilerParams(vmem_limit_bytes=VMEM_LIMIT),
        name="forward",
    )(lo, frac, win, first, volume, base)


def backward(volume, residual, lo, frac, win, base, first):
    blocks, slices, _ = volume.shape
    nb = 8
    return pl.pallas_call(
        lambda *refs: backward_kernel(nb, *refs),
        grid=(blocks // nb,),
        in_specs=[smem(), smem(), smem(), smem(),
                  pl.BlockSpec((nb, slices, VOX), lambda i: (i, 0, 0)),
                  pl.BlockSpec((ANG_SUB, VOX), lambda i: (0, 0)),
                  pl.BlockSpec(residual.shape, lambda i: (0, 0))],
        out_specs=pl.BlockSpec((nb, slices, VOX), lambda i: (i, 0, 0)),
        out_shape=jax.ShapeDtypeStruct(volume.shape, jnp.float32),
        scratch_shapes=[pltpu.VMEM((ANG_SUB * R, VOX), jnp.float32),
                        pltpu.VMEM((ANG_SUB * R, VOX), jnp.bfloat16),
                        pltpu.VMEM((ANG_SUB * R, VOX), jnp.bfloat16),
                        pltpu.VMEM((ANG_SUB * TALL, LANES), jnp.float32),
                        pltpu.VMEM((ANG_SUB * RAYS, LANES), jnp.float32),
                        pltpu.SMEM((ANG_SUB * TILES + 2,), jnp.int32)],
        compiler_params=pltpu.CompilerParams(vmem_limit_bytes=VMEM_LIMIT),
        name="backward",
    )(lo, frac, win, first, volume, base, residual)


def own_ray_sums(first_row, rows):
    count = rows * RAYS_TILE
    padded = -(-count // 1024) * 1024
    idx = jnp.minimum(jnp.arange(padded, dtype=jnp.int32), count - 1)
    row = first_row + idx // RAYS_TILE
    ray = ((row % NTILE) * RAYS_TILE + idx % RAYS_TILE).astype(jnp.float32) + (0.5 - RAYS * 0.5)
    angle = row // NTILE
    big, small = [], []
    for subset in range(SUBSETS):
        th = angles(subset)
        pairs = [sorted((math.cos(t), math.sin(t)), key=abs) for t in th]
        sign = jnp.zeros((padded,), jnp.float32)
        b, s = sign, sign
        for a in range(ANG_SUB):
            b = jnp.where(angle == a, np.float32(pairs[a][1]), b)
            s = jnp.where(angle == a, np.float32(pairs[a][0]), s)
        big.append(b)
        small.append(s)
    shape = (SUBSETS, padded // LANES, LANES)
    big = jnp.stack(big).reshape(shape)
    small = jnp.stack(small).reshape(shape)
    rays = jnp.broadcast_to(ray.reshape(1, padded // LANES, LANES), shape)
    sums = pl.pallas_call(
        ray_sum_kernel,
        out_shape=jax.ShapeDtypeStruct(shape, jnp.float32),
        name="raysum",
    )(big, small, rays)
    return sums.reshape(SUBSETS, padded)[:, :count]


def placing(place, subset):
    half = IMG_BLK * BLK_SIDE * 0.5
    x = (place % IMG_BLK).astype(jnp.float32) * BLK_SIDE + (BLK_SIDE * 0.5 - half)
    y = (place // IMG_BLK).astype(jnp.float32) * BLK_SIDE + (BLK_SIDE * 0.5 - half)
    cosine = np.cos(np.array(angles(subset))).astype(np.float32)
    sine = np.sin(np.array(angles(subset))).astype(np.float32)
    z = x[:, None] * cosine + y[:, None] * sine + (RAYS * 0.5 - 0.5)
    low = jnp.floor(z)
    lo = low.astype(jnp.int32)
    tile = jnp.arange(TILES, dtype=jnp.int32)
    touched = jnp.any(((lo - PAD) // SPAN)[:, :, None] == tile, axis=0)
    touched |= jnp.any(((lo + R + PAD) // SPAN)[:, :, None] == tile, axis=0)
    win = touched.reshape(-1).astype(jnp.int32)
    return lo, (z - low) * (1.0 / spread), win


def shards(volume, block_place, measured, live_rays):
    groups = lax.axis_size("group")
    patches = lax.axis_size("patch")
    group_index = lax.axis_index("group")
    patch_index = lax.axis_index("patch")
    slices = volume.shape[1]
    slab_rows = ANG_SUB * NTILE // patches
    rows = slab_rows // groups
    first_row = patch_index * slab_rows + group_index * rows
    lines = rows * RAYS_TILE * slices // LANES
    per = LANES // slices
    sums = own_ray_sums(first_row, rows)
    estimate = volume
    own_residual = None
    for subset in range(SUBSETS):
        base, first = geometry(subset)
        lo, frac, win = placing(block_place, subset)
        partial = forward(estimate, lo, frac, win, base, first)
        mine = lax.dynamic_slice_in_dim(measured[subset], group_index * rows, rows, 0)
        live = lax.dynamic_slice_in_dim(live_rays[subset], first_row, rows, 0)
        on = jnp.arange(RAYS_TILE, dtype=jnp.int32)[None, :] < live[:, None]
        on = jnp.broadcast_to(on[:, :, None], (rows, RAYS_TILE, slices)).reshape(lines, LANES)
        rs = jnp.maximum(sums[subset], 1.0).reshape(lines, per, 1)
        rs = jnp.broadcast_to(rs, (lines, per, slices)).reshape(lines, LANES)
        full, own = exchange(partial, mine.reshape(lines, LANES), on.astype(jnp.float32), rs, groups, patches)
        own_residual = own.reshape(rows, RAYS_TILE * slices)
        estimate = backward(estimate, full, lo, frac, win, base, first)
    return (estimate, own_residual[None])


def solution(mesh):
    return jax.shard_map(
        shards,
        mesh=mesh,
        in_specs=(
            P(("group", "patch"), None, None),
            P(("group", "patch")),
            P(None, "patch", None),
            P(),
        ),
        out_specs=(P(("group", "patch"), None, None), P("group", "patch", None)),
        check_vma=False,
    )
```

profile of v0, /device:TPU:1, one launch (start us, length us, event | category | flops | bytes accessed | tf_op | source)
XLA Modules:
  0.0 235.6 jit_solution(9925105976498644310)
XLA Ops:
  0.6 0.7 fusion.37
  1.3 0.6 broadcast_in_dim.129.k_ref
  1.9 0.8 fusion.39
  2.7 0.1 fusion.33
  2.8 0.1 fusion.14
  2.8 0.1 fusion.15
  3.0 0.6 pad_maximum_fusion.1.s_ref
  3.6 0.6 pad_maximum_fusion.c_ref
  4.2 30.7 %raysum.1 = f32[2,8,128]{2,1,0:T(8,128)} custom-call(f32[2,8,128]{2,1,0:T(8,128)} %pad_maximum_fusion.c_ref, f32[2,8,128]{2,1,0:T(8,128)} %pad_maximum_fusion.1.s_ref, f32[2,8,128]{2,1,0:T(8,128)} %broadcast_in_dim.129.k_ref), custom_call_target="tpu_custom_call" | custom-call | tf_op jit(solution)/shard_map/raysum/pallas_call | solution.py:414
  34.9 0.7 copy.28
  35.6 0.1 max.23
  35.7 0.1 copy.24
  35.8 0.1 max.21
  35.8 0.1 copy.22
  35.9 0.7 copy.23.rs_ref
  36.6 0.7 copy.25.rs_ref
  37.3 1.0 fusion.38
  38.3 0.6 reshape.624.mine_ref
  38.9 0.6 reshape.619.mine_ref
  39.5 1.5 fusion.5
  41.0 1.0 add_select_fusion
  42.1 0.1 copy.20
  42.1 0.4 fusion.2
  42.5 0.7 reshape.628.refs_2_
  43.2 0.1 copy.19
  43.3 0.4 fusion
  43.7 0.7 reshape.627.refs_2_
  44.4 0.2 broadcast_in_dim.131
  44.5 0.8 convert_element_type.53.on_ref
  45.3 0.2 broadcast_in_dim.112
  45.5 0.8 convert_element_type.50.on_ref
  46.3 35.9 %forward.2 = f32[1536,128]{1,0:T(8,128)} custom-call(s32[128,8]{1,0:T(8,128)} %get-tuple-element.17.refs_0_, f32[128,8]{1,0:T(8,128)} %get-tuple-element.16.refs_1_, s32[192]{0:T(256)} %reshape.628.refs_2_, s32[8,16]{1,0:T(8,128)} %constant.207.clone.refs_3_, f32[128,8,1024]{2,1,0:T(8,128)} %refs_4_.3, f32[8,1024]{1,0:T(8,128)} %constant.208.clone.refs_5_), custom_call_target="tpu_custom_call" | custom-call | tf_op jit(solution)/shard_map/forward/pallas_call | solution.py:350
  82.1 28.9 %exchange.2 = (f32[4,2,4,48,128]{4,3,2,1,0:T(8,128)}, f32[48,128]{1,0:T(8,128)}) custom-call(f32[4,2,4,48,128]{4,3,2,1,0:T(8,128)} %bitcast.16, f32[48,128]{1,0:T(8,128)} %reshape.619.mine_ref, f32[48,128]{1,0:T(8,128)} %convert_element_type.50.on_ref, f32[48,128]{1,0:T(8,128)} %copy.23.rs_ref), custom_call_target="tpu_custom_call" | custom-call | tf_op jit(solution)/shard_map/exchange/pallas_call | solution.py:324
  111.1 29.6 %backward.2.refs_4_ = f32[128,8,1024]{2,1,0:T(8,128)} custom-call(s32[128,8]{1,0:T(8,128)} %get-tuple-element.17.refs_0_, f32[128,8]{1,0:T(8,128)} %get-tuple-element.16.refs_1_, s32[192]{0:T(256)} %reshape.628.refs_2_, s32[8,16]{1,0:T(8,128)} %constant.207.clone.refs_3_, f32[128,8,1024]{2,1,0:T(8,128)} %refs_4_.3, f32[8,1024]{1,0:T(8,128)} %constant.208.clone.refs_5_, ...), custom_call_target="tpu_custom_call" | custom-call | tf_op jit(solution)/shard_map/backward/pallas_call | solution.py:372
  140.7 36.0 %forward.3 = f32[1536,128]{1,0:T(8,128)} custom-call(s32[128,8]{1,0:T(8,128)} %get-tuple-element.24.refs_0_, f32[128,8]{1,0:T(8,128)} %get-tuple-element.25.refs_1_, s32[192]{0:T(256)} %reshape.627.refs_2_, s32[8,16]{1,0:T(8,128)} %constant.211.clone.refs_3_, f32[128,8,1024]{2,1,0:T(8,128)} %backward.2.refs_4_, f32[8,1024]{1,0:T(8,128)} %constant.212.clone.refs_5_), custom_call_target="tpu_custom_call" | custom-call | tf_op jit(solution)/shard_map/forward/pallas_call | solution.py:350
  176.7 28.6 %exchange.3 = (f32[4,2,4,48,128]{4,3,2,1,0:T(8,128)}, f32[48,128]{1,0:T(8,128)}) custom-call(f32[4,2,4,48,128]{4,3,2,1,0:T(8,128)} %bitcast.17, f32[48,128]{1,0:T(8,128)} %reshape.624.mine_ref, f32[48,128]{1,0:T(8,128)} %convert_element_type.53.on_ref, f32[48,128]{1,0:T(8,128)} %copy.25.rs_ref), custom_call_target="tpu_custom_call" | custom-call | tf_op jit(solution)/shard_map/exchange/pallas_call | solution.py:324
  205.3 0.0 copy-start
  205.3 29.7 %backward.3 = f32[128,8,1024]{2,1,0:T(8,128)} custom-call(s32[128,8]{1,0:T(8,128)} %get-tuple-element.24.refs_0_, f32[128,8]{1,0:T(8,128)} %get-tuple-element.25.refs_1_, s32[192]{0:T(256)} %reshape.627.refs_2_, s32[8,16]{1,0:T(8,128)} %constant.211.clone.refs_3_, f32[128,8,1024]{2,1,0:T(8,128)} %backward.2.refs_4_, f32[8,1024]{1,0:T(8,128)} %constant.212.clone.refs_5_, ...), custom_call_target="tpu_custom_call" | custom-call | tf_op jit(solution)/shard_map/backward/pallas_call | solution.py:372
  235.0 0.0 copy-done
  235.0 0.6 broadcast_in_dim_reshape.3
  (11 shorter events, 0.2 us)
Async XLA Ops:
  205.3 29.7 %copy-start = (f32[48,128]{1,0:T(8,128)S(1)}, f32[48,128]{1,0:T(8,128)}, u32[]{:S(2)}) copy-start(f32[48,128]{1,0:T(8,128)} %get-tuple-element.7) | copy-start | bytes 73732
where the time goes:
time: 239 us; the launch traced here: 236 us
  Pallas kernels  219 us (92%)
  local copies, waits for them, and re-layouts  10.1 us (4%)
  other arithmetic  5.41 us (2%)
    pallas_call x2, Pallas kernels, forward(): pl.pallas_call(lambda *refs: forward_kernel(nb, *refs), grid=(blocks // n...  71.9 us
    pallas_call x2, Pallas kernels, backward(): pl.pallas_call(lambda *refs: backward_kernel(nb, *refs), grid=(blocks //...  59.3 us
    pallas_call x2, Pallas kernels, exchange(): pl.pallas_call(exchange_kernel, in_specs=[vmem] * 4, out_specs=[vmem] * 2...  57.5 us
    pallas_call x1, Pallas kernels, own_ray_sums(): pl.pallas_call(ray_sum_kernel, out_shape=jax.ShapeDtypeStruct(shape, jnp....  30.7 us

commit v1 on v0

--- a/solution.py
+++ b/solution.py
@@ -56,11 +56,10 @@
         e_scr[a * R:(a + 1) * R, :] = (base_ref[a:a + 1, :] - ray) * (1.0 / spread)
 
 
-def make_footprint(e_scr, f_scr, frac_ref, b):
-    for a in range(ANG_SUB):
-        t = e_scr[a * R:(a + 1) * R, :] + frac_ref[b, a]
-        bump = jnp.maximum(1.0 - t * t, 0.0)
-        f_scr[a * R:(a + 1) * R, :] = (bump * bump).astype(jnp.bfloat16)
+def footprint(t):
+    t = t.astype(jnp.bfloat16)
+    bump = jnp.maximum(1.0 - t * t, 0.0)
+    return bump * bump
 
 
 TILES = RAYS // SPAN
@@ -72,7 +71,7 @@
         tiles[n] = i
         return n + hit
 
-    n = lax.fori_loop(0, ANG_SUB * TILES, step, 0)
+    n = lax.fori_loop(0, ANG_SUB * TILES, step, 0, unroll=16)
     tiles[n] = tiles[jnp.maximum(n - 1, 0)]
     return (n + 1) // 2
 
@@ -91,18 +90,11 @@
     return pl.multiple_of(x, m)
 
 
-def forward_kernel(nb, lo_ref, frac_ref, win_ref, first_ref, vol_ref, base_ref, out_ref,
-                   e_scr, f_even, f_odd, m_scr, acc, tiles):
-    f_bufs = (f_even, f_odd)
+def forward_kernel(nb, lo_ref, win_ref, first_ref, vol_ref, frac_ref, grid_ref, out_ref, fold_scr, acc, tiles):
     step = pl.program_id(0)
 
     @pl.when(step == 0)
     def _():
-        fill_grid(base_ref, e_scr)
-        v = lax.broadcasted_iota(jnp.int32, (LANES, VOX), 1)
-        line = lax.broadcasted_iota(jnp.int32, (LANES, VOX), 0)
-        q_of = (v // (BLK_SIDE * SUB)) * (BLK_SIDE // SUB) + (v % BLK_SIDE) // SUB
-        m_scr[...] = jnp.where(q_of == line // 8, 1.0, 0.0).astype(jnp.bfloat16)
         zero = jnp.zeros((2 * SPAN, LANES), jnp.float32)
 
         tiles[ANG_SUB * TILES + 1] = list_tiles(win_ref, tiles)
@@ -112,14 +104,20 @@
 
         over_tiles(tiles, tiles[ANG_SUB * TILES + 1], clear)
 
+    width = SUB * BLK_SIDE
+    group = BLK_SIDE // SUB
+    slices = vol_ref.shape[1]
+    col_group = (lax.broadcasted_iota(jnp.int32, (group * slices, width), 1) % BLK_SIDE) // SUB
+    mine = col_group == lax.broadcasted_iota(jnp.int32, (group * slices, width), 0) // slices
     for i in range(nb):
         b = step * nb + i
-        f_scr = f_bufs[i % 2]
-        make_footprint(e_scr, f_scr, frac_ref, b)
-        rounded = vol_ref[i].astype(jnp.bfloat16)
-        spreadv = jnp.tile(rounded, (NQ, 1)) * m_scr[...]
-        part = lax.dot_general(f_scr[...], spreadv, (((1,), (1,)), ((), ())),
-                               preferred_element_type=jnp.float32)
+        parts = []
+        for g in range(group):
+            at = slice(g * width, (g + 1) * width)
+            f = footprint(grid_ref[at, :] + frac_ref[i:i + 1, :])
+            wide = jnp.where(mine, jnp.tile(vol_ref[i, :, at], (group, 1)), 0.0)
+            parts.append(jnp.dot(wide.astype(jnp.bfloat16), f, preferred_element_type=jnp.float32))
+        part = jnp.transpose(jnp.concatenate(parts, axis=0))
         for a in range(ANG_SUB):
             at = pl.ds(a * TALL + PAD + lo_ref[b, a], R)
             acc[at, :] += part[a * R:(a + 1) * R, :]
@@ -129,8 +127,7 @@
         out_ref[...] = jnp.zeros_like(out_ref)
         span = SPAN
         lane_q = lax.broadcasted_iota(jnp.int32, (span, LANES), 1) // 8
-        row_j = lax.broadcasted_iota(jnp.int32, (span, LANES), 0) % 16
-        pick = lane_q == row_j
+        line_q = lax.broadcasted_iota(jnp.int32, (span // 16, LANES), 1) // 8
 
         def merge(a, i):
             k = i * span
@@ -140,16 +137,17 @@
                 total = jnp.where(lane_q == q, acc[pl.ds(src, span), :], total)
             for s in (64, 32, 16, 8):
                 total = total + pltpu.roll(total, s, 1)
-            total = jnp.where(pick, total, 0.0)
-            out = jnp.sum(total.reshape(span // 16, 16, LANES), axis=1)
+            fold_scr[...] = total
+            out = fold_scr[pl.ds(0, span // 16, stride=16), :]
+            for r in range(1, 16):
+                out = jnp.where(line_q == r, fold_scr[pl.ds(r, span // 16, stride=16), :], out)
             out_ref[pl.ds(aligned(a * (RAYS // 16) + i * 8, 8), 8), :] = out
 
         over_tiles(tiles, tiles[ANG_SUB * TILES + 1], merge)
 
 
 def backward_kernel(nb, lo_ref, frac_ref, win_ref, first_ref, vol_ref, base_ref, res_ref, out_ref,
-                    e_scr, f_even, f_odd, rb, dd, tiles):
-    f_bufs = (f_even, f_odd)
+                    e_scr, rb, dd, tiles):
     step = pl.program_id(0)
 
     @pl.when(step == 0)
@@ -190,8 +188,6 @@
 
     for i in range(nb):
         b = step * nb + i
-        f_scr = f_bufs[i % 2]
-        make_footprint(e_scr, f_scr, frac_ref, b)
         rows = jnp.concatenate(
             [dd[pl.ds(a * RAYS + lo_ref[b, a], R), :] for a in range(ANG_SUB)], axis=0)
         turned = jnp.transpose(rows)
@@ -199,7 +195,9 @@
         for g in range(group):
             lhs = jnp.concatenate([turned[g * 32:(g + 1) * 32], ones], axis=0).astype(jnp.bfloat16)
             at = slice(g * width, (g + 1) * width)
-            part = jnp.dot(lhs, f_scr[:, at], preferred_element_type=jnp.float32)
+            f = jnp.concatenate(
+                [footprint(e_scr[a * R:(a + 1) * R, at] + frac_ref[b, a]) for a in range(ANG_SUB)], axis=0)
+            part = jnp.dot(lhs, f, preferred_element_type=jnp.float32)
             back = part[0:8]
             for j in range(1, group):
                 back = jnp.where(col_group == j, part[j * 8:(j + 1) * 8], back)
@@ -347,23 +345,22 @@
     blocks, slices, _ = volume.shape
     nb = 8
     lines = ANG_SUB * RAYS // 16
+    grid = (np.repeat(base, R, axis=0) - np.tile(np.arange(R), ANG_SUB)[:, None]) * (1.0 / spread)
     return pl.pallas_call(
         lambda *refs: forward_kernel(nb, *refs),
         grid=(blocks // nb,),
-        in_specs=[smem(), smem(), smem(), smem(),
+        in_specs=[smem(), smem(), smem(),
                   pl.BlockSpec((nb, slices, VOX), lambda i: (i, 0, 0)),
-                  pl.BlockSpec((ANG_SUB, VOX), lambda i: (0, 0))],
+                  pl.BlockSpec((nb, LANES), lambda i: (i, 0)),
+                  pl.BlockSpec((VOX, LANES), lambda i: (0, 0))],
         out_specs=pl.BlockSpec((lines, LANES), lambda i: (0, 0)),
         out_shape=jax.ShapeDtypeStruct((lines, LANES), jnp.float32),
-        scratch_shapes=[pltpu.VMEM((ANG_SUB * R, VOX), jnp.float32),
-                        pltpu.VMEM((ANG_SUB * R, VOX), jnp.bfloat16),
-                        pltpu.VMEM((ANG_SUB * R, VOX), jnp.bfloat16),
-                        pltpu.VMEM((LANES, VOX), jnp.bfloat16),
+        scratch_shapes=[pltpu.VMEM((SPAN, LANES), jnp.float32),
                         pltpu.VMEM((ANG_SUB * TALL, LANES), jnp.float32),
                         pltpu.SMEM((ANG_SUB * TILES + 2,), jnp.int32)],
         compiler_params=pltpu.CompilerParams(vmem_limit_bytes=VMEM_LIMIT),
         name="forward",
-    )(lo, frac, win, first, volume, base)
+    )(lo, win, first, volume, jnp.repeat(frac, R, axis=1), grid.T.astype(np.float32))
 
 
 def backward(volume, residual, lo, frac, win, base, first):
@@ -379,8 +376,6 @@
         out_specs=pl.BlockSpec((nb, slices, VOX), lambda i: (i, 0, 0)),
         out_shape=jax.ShapeDtypeStruct(volume.shape, jnp.float32),
         scratch_shapes=[pltpu.VMEM((ANG_SUB * R, VOX), jnp.float32),
-                        pltpu.VMEM((ANG_SUB * R, VOX), jnp.bfloat16),
-                        pltpu.VMEM((ANG_SUB * R, VOX), jnp.bfloat16),
                         pltpu.VMEM((ANG_SUB * TALL, LANES), jnp.float32),
                         pltpu.VMEM((ANG_SUB * RAYS, LANES), jnp.float32),
                         pltpu.SMEM((ANG_SUB * TILES + 2,), jnp.int32)],

time: 239 us -> 220 us (0.921)
  Pallas kernels: 219 us -> 199 us
    pallas_call x2, Pallas kernels: 71.9 us -> 56.1 us  [forward(): pl.pallas_call(lambda *refs: forward_kernel(nb, *refs), grid=(blocks // n...]
    pallas_call x2, Pallas kernels: 59.3 us -> 52.6 us  [backward(): pl.pallas_call(lambda *refs: backward_kernel(nb, *refs), grid=(blocks //...]
where the time goes in v1:
time: 220 us; the launch traced here: 217 us
  Pallas kernels  199 us (90%)
  local copies, waits for them, and re-layouts  11.7 us (5%)
  other arithmetic  5.33 us (2%)
    pallas_call x2, Pallas kernels, exchange(): pl.pallas_call(exchange_kernel, in_specs=[vmem] * 4, out_specs=[vmem] * 2...  59.7 us
    pallas_call x2, Pallas kernels, forward(): pl.pallas_call(lambda *refs: forward_kernel(nb, *refs), grid=(blocks // n...  56.1 us
    pallas_call x2, Pallas kernels, backward(): pl.pallas_call(lambda *refs: backward_kernel(nb, *refs), grid=(blocks //...  52.6 us
    pallas_call x1, Pallas kernels, own_ray_sums(): pl.pallas_call(ray_sum_kernel, out_shape=jax.ShapeDtypeStruct(shape, jnp....  30.7 us

profile of v1, /device:TPU:1, one launch (start us, length us, event | category | flops | bytes accessed | tf_op | source)
XLA Modules:
  0.0 216.9 jit_solution(6264274044020977849)
XLA Ops:
  0.6 0.7 fusion.37
  1.3 0.6 broadcast_in_dim.136.k_ref
  1.9 0.8 fusion.39
  2.7 0.1 fusion.33
  2.8 0.1 fusion.14
  2.8 0.1 fusion.15
  3.0 0.6 pad_maximum_fusion.1.s_ref
  3.6 0.6 pad_maximum_fusion.c_ref
  4.2 30.7 %raysum.1 = f32[2,8,128]{2,1,0:T(8,128)} custom-call(f32[2,8,128]{2,1,0:T(8,128)} %pad_maximum_fusion.c_ref, f32[2,8,128]{2,1,0:T(8,128)} %pad_maximum_fusion.1.s_ref, f32[2,8,128]{2,1,0:T(8,128)} %broadcast_in_dim.136.k_ref), custom_call_target="tpu_custom_call" | custom-call | tf_op jit(solution)/shard_map/raysum/pallas_call | solution.py:409
  34.9 0.7 copy.38
  35.6 0.1 max.23
  35.7 0.1 copy.34
  35.8 0.1 max.21
  35.8 0.1 copy.30
  35.9 0.7 copy.31.rs_ref
  36.6 0.7 copy.35.rs_ref
  37.3 1.0 fusion.38
  38.3 0.6 reshape.632.mine_ref
  38.9 0.6 reshape.626.mine_ref
  39.5 1.5 fusion.5
  41.0 0.0 copy-start
  41.0 0.0 copy-start.1
  41.0 0.1 copy.32
  41.1 0.7 copy.33.refs_4_
  41.8 0.7 copy.29.refs_4_
  42.5 1.0 add_select_fusion
  43.6 0.1 copy.26
  43.6 0.4 fusion.2
  44.0 0.7 reshape.636.refs_1_.refs_2_
  44.7 0.1 copy.25
  44.8 0.4 fusion
  45.2 0.7 reshape.635.refs_1_.refs_2_
  45.9 0.2 broadcast_in_dim.139
  46.0 0.8 convert_element_type.53.on_ref
  46.8 0.2 broadcast_in_dim.119
  47.0 0.8 convert_element_type.50.on_ref
  47.8 28.3 %forward.2 = f32[1536,128]{1,0:T(8,128)} custom-call(s32[128,8]{1,0:T(8,128)} %get-tuple-element.17.refs_0_, s32[192]{0:T(256)} %reshape.636.refs_1_.refs_2_, s32[8,16]{1,0:T(8,128)} %constant.211.clone.refs_2_.refs_3_, f32[128,8,1024]{2,1,0:T(8,128)} %refs_4_.1, f32[128,128]{1,0:T(8,128)} %copy.29.refs_4_, f32[1024,128]{1,0:T(8,128)} %constant.212.clone.refs_5_), custom_call_target="tpu_custom_call" | custom-call | tf_op jit(solution)/shard_map/forward/pallas_call | solution.py:349
  76.0 0.0 copy-done
  76.0 0.0 copy-done.1
  76.1 30.0 %exchange.2 = (f32[4,2,4,48,128]{4,3,2,1,0:T(8,128)}, f32[48,128]{1,0:T(8,128)}) custom-call(f32[4,2,4,48,128]{4,3,2,1,0:T(8,128)} %bitcast.18, f32[48,128]{1,0:T(8,128)} %reshape.626.mine_ref, f32[48,128]{1,0:T(8,128)} %convert_element_type.50.on_ref, f32[48,128]{1,0:T(8,128)} %copy.31.rs_ref), custom_call_target="tpu_custom_call" | custom-call | tf_op jit(solution)/shard_map/exchange/pallas_call | solution.py:322
  106.1 26.4 %backward.2.refs_3_.refs_4_ = f32[128,8,1024]{2,1,0:T(8,128)} custom-call(s32[128,8]{1,0:T(8,128)} %get-tuple-element.17.refs_0_, f32[128,8]{1,0:T(8,128)} %copy-done.1, s32[192]{0:T(256)} %reshape.636.refs_1_.refs_2_, s32[8,16]{1,0:T(8,128)} %constant.211.clone.refs_2_.refs_3_, f32[128,8,1024]{2,1,0:T(8,128)} %refs_4_.1, ...), custom_call_target="tpu_custom_call" | custom-call | tf_op jit(solution)/shard_map/backward/pallas_call | solution.py:369
  132.5 27.9 %forward.3 = f32[1536,128]{1,0:T(8,128)} custom-call(s32[128,8]{1,0:T(8,128)} %get-tuple-element.24.refs_0_, s32[192]{0:T(256)} %reshape.635.refs_1_.refs_2_, s32[8,16]{1,0:T(8,128)} %constant.216.clone.refs_2_.refs_3_, f32[128,8,1024]{2,1,0:T(8,128)} %backward.2.refs_3_.refs_4_, f32[128,128]{1,0:T(8,128)} %copy.33.refs_4_, f32[1024,128]{1,0:T(8,128)} %constant.217.clone.refs_5_), custom_call_target="tpu_custom_call" | custom-call | tf_op jit(solution)/shard_map/forward/pallas_call | solution.py:349
  160.4 29.7 %exchange.3 = (f32[4,2,4,48,128]{4,3,2,1,0:T(8,128)}, f32[48,128]{1,0:T(8,128)}) custom-call(f32[4,2,4,48,128]{4,3,2,1,0:T(8,128)} %bitcast.19, f32[48,128]{1,0:T(8,128)} %reshape.632.mine_ref, f32[48,128]{1,0:T(8,128)} %convert_element_type.53.on_ref, f32[48,128]{1,0:T(8,128)} %copy.35.rs_ref), custom_call_target="tpu_custom_call" | custom-call | tf_op jit(solution)/shard_map/exchange/pallas_call | solution.py:322
  190.1 0.0 copy-start.2
  190.1 26.2 %backward.3 = f32[128,8,1024]{2,1,0:T(8,128)} custom-call(s32[128,8]{1,0:T(8,128)} %get-tuple-element.24.refs_0_, f32[128,8]{1,0:T(8,128)} %copy-done, s32[192]{0:T(256)} %reshape.635.refs_1_.refs_2_, s32[8,16]{1,0:T(8,128)} %constant.216.clone.refs_2_.refs_3_, f32[128,8,1024]{2,1,0:T(8,128)} %backward.2.refs_3_.refs_4_, f32[8,1024]{1,0:T(8,128)} %constant.218.clone.refs_5_, ...), custom_call_target="tpu_custom_call" | custom-call | tf_op jit(solution)/shard_map/backward/pallas_call | solution.py:369
  216.3 0.0 copy-done.2
  216.3 0.6 broadcast_in_dim_reshape.3
  (14 shorter events, 0.3 us)
Async XLA Ops:
  41.0 35.1 %copy-start = (f32[128,8]{1,0:T(8,128)}, f32[128,8]{1,0:T(8,128)S(1)}, u32[]{:S(2)}) copy-start(f32[128,8]{1,0:T(8,128)S(1)} %get-tuple-element.25.refs_1_) | copy-start | bytes 12292
  41.0 35.1 %copy-start.1 = (f32[128,8]{1,0:T(8,128)}, f32[128,8]{1,0:T(8,128)S(1)}, u32[]{:S(2)}) copy-start(f32[128,8]{1,0:T(8,128)S(1)} %get-tuple-element.16.refs_1_) | copy-start | bytes 12292
  190.1 26.2 %copy-start.2 = (f32[48,128]{1,0:T(8,128)S(1)}, f32[48,128]{1,0:T(8,128)}, u32[]{:S(2)}) copy-start(f32[48,128]{1,0:T(8,128)} %get-tuple-element.7) | copy-start | bytes 73732

commit v2 on v1

v2 whole, which is shorter than its diff:
```python
import math

import jax
import jax.numpy as jnp
import numpy as np
from jax import lax
from jax.experimental import pallas as pl
from jax.experimental.pallas import tpu as pltpu
from jax.sharding import PartitionSpec as P

IMG_BLK = 64
BLK_SIDE = 32
RAYS_TILE = 48
NTILE = 64
ANG_SUB = 8
SUBSETS = 2

spread = 1.5
relax = 0.9

SUB = 8
NQ = (BLK_SIDE // SUB) ** 2
R = 16
VOX = BLK_SIDE * BLK_SIDE
RAYS = NTILE * RAYS_TILE
LANES = 128
PAD = 32
SPAN = 128
TALL = RAYS + SPAN
VMEM_LIMIT = 60 * 1024 * 1024


def angles(subset):
    return [math.pi * (a * SUBSETS + subset) / (ANG_SUB * SUBSETS) for a in range(ANG_SUB)]


def geometry(subset):
    v = np.arange(VOX)
    col = (v % BLK_SIDE) + 0.5 - BLK_SIDE / 2
    row = (v // BLK_SIDE) + 0.5 - BLK_SIDE / 2
    q_of = (v // BLK_SIDE // SUB) * (BLK_SIDE // SUB) + (v % BLK_SIDE) // SUB
    base = np.zeros((ANG_SUB, VOX), np.float64)
    first = np.zeros((ANG_SUB, NQ), np.int64)
    for a, theta in enumerate(angles(subset)):
        off = col * math.cos(theta) + row * math.sin(theta)
        for q in range(NQ):
            mine = q_of == q
            first[a, q] = math.floor(off[mine].min() - spread)
            base[a, mine] = off[mine] - first[a, q]
    return base.astype(np.float32), first.astype(np.int32)


def fill_grid(base_ref, e_scr):
    ray = lax.broadcasted_iota(jnp.int32, (R, VOX), 0).astype(jnp.float32)
    for a in range(ANG_SUB):
        e_scr[a * R:(a + 1) * R, :] = (base_ref[a:a + 1, :] - ray) * (1.0 / spread)


def footprint(t):
    t = t.astype(jnp.bfloat16)
    bump = jnp.maximum(1.0 - t * t, 0.0)
    return bump * bump


TILES = RAYS // SPAN


def list_tiles(subset, win_ref, tiles):
    def angle(a, n):
        for i in range(TILES):
            hit = win_ref[subset, a, i]
            tiles[n] = a * TILES + i
            n = n + hit
        return n

    n = lax.fori_loop(0, ANG_SUB, angle, 0)
    tiles[n] = tiles[jnp.maximum(n - 1, 0)]
    return (n + 1) // 2


def over_tiles(tiles, half_count, body):
    def pair(i, c):
        for j in range(2):
            at = tiles[2 * i + j]
            body(at // TILES, lax.rem(at, TILES), j)
        return c

    lax.fori_loop(0, half_count, pair, 0)


def aligned(x, m):
    return pl.multiple_of(x, m)


def forward_kernel(nb, subset, lo_ref, frac_ref, win_ref, first_ref, vol_ref, grid_ref, out_ref,
                   fold_scr, acc, tiles):
    step = pl.program_id(0)

    @pl.when(step == 0)
    def _():
        zero = jnp.zeros((2 * SPAN, LANES), jnp.float32)

        tiles[ANG_SUB * TILES + 1] = list_tiles(subset, win_ref, tiles)

        def clear(a, i, j):
            acc[pl.ds(aligned(a * TALL + i * SPAN, SPAN), 2 * SPAN), :] = zero

        over_tiles(tiles, tiles[ANG_SUB * TILES + 1], clear)

    width = SUB * BLK_SIDE
    group = BLK_SIDE // SUB
    slices = vol_ref.shape[1]
    col_group = (lax.broadcasted_iota(jnp.int32, (group * slices, width), 1) % BLK_SIDE) // SUB
    mine = col_group == lax.broadcasted_iota(jnp.int32, (group * slices, width), 0) // slices
    angle = lax.broadcasted_iota(jnp.int32, (1, LANES), 1) // R
    for i in range(nb):
        b = step * nb + i
        frac = jnp.zeros((1, LANES), jnp.float32)
        for a in range(ANG_SUB):
            frac = jnp.where(angle == a, frac_ref[subset, a, b], frac)
        parts = []
        for g in range(group):
            at = slice(g * width, (g + 1) * width)
            f = footprint(grid_ref[at, :] + frac)
            wide = jnp.where(mine, jnp.tile(vol_ref[i, :, at], (group, 1)), 0.0)
            parts.append(jnp.dot(wide.astype(jnp.bfloat16), f, preferred_element_type=jnp.float32))
        part = jnp.transpose(jnp.concatenate(parts, axis=0))
        for a in range(ANG_SUB):
            at = pl.ds(a * TALL + PAD + lo_ref[subset, a, b], R)
            acc[at, :] += part[a * R:(a + 1) * R, :]

    @pl.when(step == pl.num_programs(0) - 1)
    def _():
        out_ref[...] = jnp.zeros_like(out_ref)
        span = SPAN
        lane_q = lax.broadcasted_iota(jnp.int32, (span, LANES), 1) // 8
        line_q = lax.broadcasted_iota(jnp.int32, (span // 16, LANES), 1) // 8

        def merge(a, i, j):
            k = i * span
            total = jnp.zeros((span, LANES), jnp.float32)
            for q in range(NQ):
                src = a * TALL + PAD + k - first_ref[a, q]
                total = jnp.where(lane_q == q, acc[pl.ds(src, span), :], total)
            fold_scr[j] = total
            rows = [fold_scr[j, pl.ds(r, span // 16, stride=16), :] for r in range(16)]
            for half in (8, 4, 2, 1):
                low = line_q % (2 * half) < half
                rows = [jnp.where(low, rows[r] + pltpu.roll(rows[r], LANES - half * 8, 1),
                                  rows[r + half] + pltpu.roll(rows[r + half], half * 8, 1))
                        for r in range(half)]
            out_ref[pl.ds(aligned(a * (RAYS // 16) + i * 8, 8), 8), :] = rows[0]

        over_tiles(tiles, tiles[ANG_SUB * TILES + 1], merge)


def backward_kernel(nb, subset, lo_ref, frac_ref, win_ref, first_ref, vol_ref, base_ref, res_ref, out_ref,
                    e_scr, rb, dd, tiles):
    step = pl.program_id(0)

    @pl.when(step == 0)
    def _():
        fill_grid(base_ref, e_scr)
        span = SPAN
        lane_q = lax.broadcasted_iota(jnp.int32, (span, LANES), 1) // 8
        row_j = lax.broadcasted_iota(jnp.int32, (span, LANES), 0) % 16
        pick = lane_q == row_j
        fold = jnp.where(
            lax.broadcasted_iota(jnp.int32, (LANES, LANES), 0) % 8
            == lax.broadcasted_iota(jnp.int32, (LANES, LANES), 1) % 8, 1.0, 0.0).astype(jnp.bfloat16)

        count = list_tiles(subset, win_ref, tiles)

        def widen(a, i, j):
            rows = res_ref[pl.ds(aligned(a * (RAYS // 16) + i * 8, 8), 8), :]
            wide = jnp.broadcast_to(rows[:, None, :], (8, 16, LANES)).reshape(span, LANES)
            wide = jnp.where(pick, wide, 0.0).astype(jnp.bfloat16)
            rb[pl.ds(aligned(a * TALL + PAD + i * span, 8), span), :] = jnp.dot(
                wide, fold, preferred_element_type=jnp.float32)

        def shift(a, i, j):
            k = i * span
            total = jnp.zeros((span, LANES), jnp.float32)
            for q in range(NQ):
                src = a * TALL + PAD + k + first_ref[a, q]
                total = jnp.where(lane_q == q, rb[pl.ds(src, span), :], total)
            dd[pl.ds(aligned(a * RAYS + k, span), span), :] = total

        over_tiles(tiles, count, widen)
        over_tiles(tiles, count, shift)

    width = SUB * BLK_SIDE
    group = BLK_SIDE // SUB
    lane = lax.broadcasted_iota(jnp.int32, (8, width), 1)
    col_group = (lane % BLK_SIDE) // SUB

    for i in range(nb):
        b = step * nb + i
        rows = jnp.concatenate(
            [dd[pl.ds(a * RAYS + lo_ref[subset, a, b], R), :] for a in range(ANG_SUB)], axis=0)
        turned = jnp.transpose(rows)
        ones = jnp.ones((8, ANG_SUB * R), jnp.float32)
        for g in range(group):
            lhs = jnp.concatenate([turned[g * 32:(g + 1) * 32], ones], axis=0).astype(jnp.bfloat16)
            at = slice(g * width, (g + 1) * width)
            f = jnp.concatenate(
                [footprint(e_scr[a * R:(a + 1) * R, at] + frac_ref[subset, a, b]) for a in range(ANG_SUB)], axis=0)
            part = jnp.dot(lhs, f, preferred_element_type=jnp.float32)
            back = part[0:8]
            for j in range(1, group):
                back = jnp.where(col_group == j, part[j * 8:(j + 1) * 8], back)
            col_sum = part[32:40]
            out_ref[i, :, at] = jnp.maximum(vol_ref[i, :, at] + relax * back / col_sum, 0.0)


def ray_sums(shape, big, small, inv, ray):
    side = IMG_BLK * BLK_SIDE
    half = side * 0.5
    count = side // 8
    part = lax.broadcasted_iota(jnp.int32, shape, 1) % 8
    start = (part * count).astype(jnp.float32) + (0.5 - half)
    start = ray - start * small

    def row(i, total):
        w = start - i.astype(jnp.float32) * small
        mid = jnp.clip(jnp.floor(w * inv) + 0.5, 2.5 - half, half - 2.5)
        t0 = mid * big - w
        for t in (t0 - 2 * big, t0 - big, t0, t0 + big, t0 + 2 * big):
            bump = jnp.maximum(1.0 - t * t, 0.0)
            total = total + bump * bump
        return total

    total = lax.fori_loop(0, count, row, jnp.zeros(shape, jnp.float32), unroll=4)
    for d in (1, 2, 4):
        total = total + jnp.where(part // d % 2 == 0, pltpu.roll(total, LANES - d, 1), pltpu.roll(total, d, 1))
    return total


def exchange_kernel(subset, part_ref, live_ref, table_ref, meas_ref, full_ref, own_ref,
                    half, inbox, sums, lines_scr, halves, meas, stage, gathered,
                    meas_sem, pair_send, pair_recv, send_sem, recv_sem, rs_send, rs_recv,
                    out_send, out_recv, back_send, back_recv):
    g, p = lax.axis_index("group"), lax.axis_index("patch")
    pairs, groups = inbox.shape[0], inbox.shape[1]
    n = groups * pairs
    lines = stage.shape[0]
    rows = own_ref.shape[0]
    parity, column = lax.rem(p, 2), p // 2
    partner = (g, column * 2 + 1 - parity)
    mesh_id = pl.DeviceIdType.MESH

    def peer(d):
        return lax.rem(column + d // groups, pairs), lax.rem(g + lax.rem(d, groups), groups)

    def source(d):
        return (lax.rem(column + pairs - d // groups, pairs),
                lax.rem(g + groups - lax.rem(d, groups), groups))

    barrier = pltpu.get_barrier_semaphore()
    pl.semaphore_signal(barrier, inc=1, device_id=partner, device_id_type=mesh_id)

    def greet(d, c):
        pc, pg = peer(d)
        pl.semaphore_signal(barrier, inc=1, device_id=(pg, pc * 2 + parity), device_id_type=mesh_id)
        return c

    lax.fori_loop(1, n, greet, 0)
    read = pltpu.make_async_copy(meas_ref.at[subset, pl.ds(g * rows, rows)], meas, meas_sem)
    read.start()
    pl.semaphore_wait(barrier, n)

    def swap(d):
        pc = lax.rem(column + d, pairs)
        return pltpu.make_async_remote_copy(
            src_ref=part_ref.at[pc, 1 - parity], dst_ref=half.at[pc], send_sem=pair_send.at[d],
            recv_sem=pair_recv.at[d], device_id=partner, device_id_type=mesh_id)

    def to_owner(d):
        pc, pg = peer(d)
        return pltpu.make_async_remote_copy(
            src_ref=sums.at[pc, pg], dst_ref=inbox.at[column, g], send_sem=send_sem.at[d],
            recv_sem=recv_sem.at[d], device_id=(pg, pc * 2 + parity), device_id_type=mesh_id)

    def go_swap(d, c):
        swap(d).start()
        return c

    def go_column(i, c):
        pc = lax.rem(column + i, pairs)
        swap(i).wait_recv()
        sums[pc] = part_ref[pc, parity] + half[pc]

        def go(d, c):
            to_owner(d).start()
            return c

        return lax.fori_loop(jnp.maximum(i * groups, 1), (i + 1) * groups, go, c)

    lax.fori_loop(0, pairs, go_swap, 0)
    lax.fori_loop(0, pairs, go_column, 0)

    first_row = (p * groups + g) * rows
    mine = p // pairs
    line = lax.broadcasted_iota(jnp.int32, halves.shape[1:], 0)
    lane = lax.broadcasted_iota(jnp.int32, halves.shape[1:], 1)
    ray = lax.rem(first_row, NTILE) * RAYS_TILE + mine * (lines * 8) + line * 16 + lane // 8
    ray = (ray.astype(jnp.float32) + (0.5 - RAYS * 0.5)) * (1.0 / spread)
    a = first_row // NTILE
    halves[mine] = ray_sums(
        halves.shape[1:], table_ref[subset, 0, a], table_ref[subset, 1, a], table_ref[subset, 2, a], ray)
    trade = pltpu.make_async_remote_copy(
        src_ref=halves.at[mine], dst_ref=halves.at[mine], send_sem=rs_send, recv_sem=rs_recv,
        device_id=(g, lax.rem(p + pairs, 2 * pairs)), device_id_type=mesh_id)
    trade.start()

    def got(d, c):
        to_owner(d).wait_recv()
        return c

    inbox[column, g] = sums[column, g]
    lax.fori_loop(1, n, got, 0)
    total = jnp.zeros(stage.shape, jnp.float32)
    for i in range(pairs):
        for j in range(groups):
            total = total + inbox[i, j]
    lines_scr[...] = total
    read.wait()
    trade.wait()
    at = lax.broadcasted_iota(jnp.int32, (rows, LANES), 0)
    live = jnp.zeros((rows, LANES), jnp.int32)
    for r in range(rows):
        live = jnp.where(at == r, live_ref[subset, first_row + r], live)
    ray = lax.broadcasted_iota(jnp.int32, (rows, LANES), 1) // 8
    wide = lines // rows
    residuals = []
    for c in range(wide):
        sums_c = jnp.concatenate(
            [halves[h, pl.ds(c, rows // 2, stride=wide), :] for h in range(2)], axis=0)
        level = lines_scr[pl.ds(c, rows, stride=wide), :] / jnp.maximum(sums_c, 1.0)
        differ = meas[:, c * LANES:(c + 1) * LANES] - level
        residual = jnp.where(ray + c * 16 < live, differ, 0.0)
        own_ref[:, c * LANES:(c + 1) * LANES] = residual
        residuals.append(residual)
    for c in range(wide):
        lines_scr[pl.ds(c, rows, stride=wide), :] = residuals[c]
    stage[...] = lines_scr[...].astype(jnp.bfloat16)

    def to_all(d):
        pc, pg = peer(d)
        return pltpu.make_async_remote_copy(
            src_ref=stage, dst_ref=gathered.at[column, parity, g], send_sem=out_send.at[d],
            recv_sem=out_recv.at[d], device_id=(pg, pc * 2 + parity), device_id_type=mesh_id)

    def share(d):
        pc, pg = source(d)
        return pltpu.make_async_remote_copy(
            src_ref=gathered.at[pc, parity, pg], dst_ref=gathered.at[pc, parity, pg], send_sem=back_send.at[d],
            recv_sem=back_recv.at[d], device_id=partner, device_id_type=mesh_id)

    def go_all(d, c):
        to_all(d).start()
        return c

    def pass_on(d, c):
        to_all(d).wait_recv()
        share(d).start()
        return c

    def finish(d, c):
        share(d).wait()
        return c

    def sent(d, c):
        to_owner(d).wait_send()
        to_all(d).wait_send()
        return c

    def swapped(d, c):
        swap(d).wait_send()
        return c

    lax.fori_loop(1, n, go_all, 0)
    gathered[column, parity, g] = stage[...]
    share(0).start()
    lax.fori_loop(1, n, pass_on, 0)
    lax.fori_loop(0, n, finish, 0)
    lax.fori_loop(1, n, sent, 0)
    lax.fori_loop(0, pairs, swapped, 0)
    for i in range(pairs):
        full_ref[i] = gathered[i].astype(jnp.float32)


def exchange(subset, partial, live, table, measured, rows, groups, patches):
    pairs = patches // 2
    lines = rows * measured.shape[2] // LANES
    shape = (pairs, 2, groups, lines, LANES)
    n = pairs * groups
    dma = pltpu.SemaphoreType.DMA
    vmem = pl.BlockSpec(memory_space=pltpu.VMEM)
    full, own = pl.pallas_call(
        lambda *refs: exchange_kernel(subset, *refs),
        in_specs=[vmem, smem(), smem(), pl.BlockSpec(memory_space=pl.ANY)],
        out_specs=[vmem] * 2,
        out_shape=[jax.ShapeDtypeStruct(shape, jnp.float32),
                   jax.ShapeDtypeStruct((rows, measured.shape[2]), jnp.float32)],
        scratch_shapes=[pltpu.VMEM((pairs, groups, lines, LANES), jnp.float32),
                        pltpu.VMEM((pairs, groups, lines, LANES), jnp.float32),
                        pltpu.VMEM((pairs, groups, lines, LANES), jnp.float32),
                        pltpu.VMEM((lines, LANES), jnp.float32),
                        pltpu.VMEM((2, lines // 2, LANES), jnp.float32),
                        pltpu.VMEM((rows, measured.shape[2]), jnp.float32),
                        pltpu.VMEM((lines, LANES), jnp.bfloat16),
                        pltpu.VMEM(shape, jnp.bfloat16),
                        dma, dma((pairs,)), dma((pairs,)), dma((n,)), dma((n,)), dma, dma,
                        dma((n,)), dma((n,)), dma((n,)), dma((n,))],
        compiler_params=pltpu.CompilerParams(collective_id=subset, has_side_effects=True),
        name="exchange",
    )(partial.reshape(shape), live, table, measured)
    return full.reshape(partial.shape), own


def smem():
    return pl.BlockSpec(memory_space=pltpu.SMEM)


def forward(subset, volume, lo, frac, win, base, first):
    blocks, slices, _ = volume.shape
    nb = 8
    lines = ANG_SUB * RAYS // 16
    grid = (np.repeat(base, R, axis=0) - np.tile(np.arange(R), ANG_SUB)[:, None]) * (1.0 / spread)
    return pl.pallas_call(
        lambda *refs: forward_kernel(nb, subset, *refs),
        grid=(blocks // nb,),
        in_specs=[smem(), smem(), smem(), smem(),
                  pl.BlockSpec((nb, slices, VOX), lambda i: (i, 0, 0)),
                  pl.BlockSpec((VOX, LANES), lambda i: (0, 0))],
        out_specs=pl.BlockSpec((lines, LANES), lambda i: (0, 0)),
        out_shape=jax.ShapeDtypeStruct((lines, LANES), jnp.float32),
        scratch_shapes=[pltpu.VMEM((2, SPAN, LANES), jnp.float32),
                        pltpu.VMEM((ANG_SUB * TALL, LANES), jnp.float32),
                        pltpu.SMEM((ANG_SUB * TILES + 2,), jnp.int32)],
        compiler_params=pltpu.CompilerParams(vmem_limit_bytes=VMEM_LIMIT),
        name="forward",
    )(lo, frac, win, first, volume, grid.T.astype(np.float32))


def backward(subset, volume, residual, lo, frac, win, base, first):
    blocks, slices, _ = volume.shape
    nb = 8
    return pl.pallas_call(
        lambda *refs: backward_kernel(nb, subset, *refs),
        grid=(blocks // nb,),
        in_specs=[smem(), smem(), smem(), smem(),
                  pl.BlockSpec((nb, slices, VOX), lambda i: (i, 0, 0)),
                  pl.BlockSpec((ANG_SUB, VOX), lambda i: (0, 0)),
                  pl.BlockSpec(residual.shape, lambda i: (0, 0))],
        out_specs=pl.BlockSpec((nb, slices, VOX), lambda i: (i, 0, 0)),
        out_shape=jax.ShapeDtypeStruct(volume.shape, jnp.float32),
        scratch_shapes=[pltpu.VMEM((ANG_SUB * R, VOX), jnp.float32),
                        pltpu.VMEM((ANG_SUB * TALL, LANES), jnp.float32),
                        pltpu.VMEM((ANG_SUB * RAYS, LANES), jnp.float32),
                        pltpu.SMEM((ANG_SUB * TILES + 2,), jnp.int32)],
        compiler_params=pltpu.CompilerParams(vmem_limit_bytes=VMEM_LIMIT),
        name="backward",
    )(lo, frac, win, first, volume, base, residual)


def ray_table():
    table = np.zeros((SUBSETS, 3, ANG_SUB), np.float64)
    for subset in range(SUBSETS):
        for a, t in enumerate(angles(subset)):
            small, big = sorted((abs(math.cos(t)), abs(math.sin(t))))
            table[subset, :, a] = big / spread, small / spread, spread / big
    return table.astype(np.float32)


def placing(place):
    half = IMG_BLK * BLK_SIDE * 0.5
    x = (place % IMG_BLK).astype(jnp.float32) * BLK_SIDE + (BLK_SIDE * 0.5 - half)
    y = (place // IMG_BLK).astype(jnp.float32) * BLK_SIDE + (BLK_SIDE * 0.5 - half)
    theta = np.array([angles(subset) for subset in range(SUBSETS)])
    cosine = np.cos(theta).astype(np.float32)[:, :, None]
    sine = np.sin(theta).astype(np.float32)[:, :, None]
    z = x * cosine + y * sine + (RAYS * 0.5 - 0.5)
    low = jnp.floor(z)
    lo = low.astype(jnp.int32)
    tile = jnp.arange(TILES, dtype=jnp.int32)[:, None]
    near = ((lo - PAD) // SPAN)[:, :, None, :] == tile
    near |= ((lo + R + PAD) // SPAN)[:, :, None, :] == tile
    return lo, (z - low) * (1.0 / spread), jnp.any(near, axis=3).astype(jnp.int32)


def shards(volume, block_place, measured, live_rays):
    groups = lax.axis_size("group")
    patches = lax.axis_size("patch")
    rows = ANG_SUB * NTILE // patches // groups
    lo, frac, win = placing(block_place)
    table = ray_table()
    estimate = volume
    own = None
    for subset in range(SUBSETS):
        base, first = geometry(subset)
        partial = forward(subset, estimate, lo, frac, win, base, first)
        full, own = exchange(subset, partial, live_rays, table, measured, rows, groups, patches)
        estimate = backward(subset, estimate, full, lo, frac, win, base, first)
    return (estimate, own[None])


def solution(mesh):
    return jax.shard_map(
        shards,
        mesh=mesh,
        in_specs=(
            P(("group", "patch"), None, None),
            P(("group", "patch")),
            P(None, "patch", None),
            P(),
        ),
        out_specs=(P(("group", "patch"), None, None), P("group", "patch", None)),
        check_vma=False,
    )
```

time: 220 us -> 170 us (0.77)
  Pallas kernels: 199 us -> 161 us
  local copies, waits for them, and re-layouts: 11.7 us -> 0.61 us
    pallas_call x7 -> x6, Pallas kernels: 199 us -> 161 us  [the longest x2 57.9 us: exchange(): pl.pallas_call(lambda *refs: exchange_kernel(subset, *refs), in_specs=[vm...]
    reshape x8 -> x0, local copies, waits for them, and re-layouts: 4.06 us -> none  [the longest x2 1.46 us: forward(): jnp.repeat(frac, R, axis=1)]
    convert_element_type x4 -> x0, local copies, waits for them, and re-layouts: 2.93 us -> none  [the longest x2 1.6 us: shards(): on.astype(jnp.float32)]
where the time goes in v2:
time: 170 us; the launch traced here: 166 us
  Pallas kernels  161 us (95%)
  other arithmetic  3.79 us (2%)
    pallas_call x2, Pallas kernels, exchange(): pl.pallas_call(lambda *refs: exchange_kernel(subset, *refs), in_specs=[vm...  57.9 us
    pallas_call x2, Pallas kernels, forward(): pl.pallas_call(lambda *refs: forward_kernel(nb, subset, *refs), grid=(blo...  54.1 us
    pallas_call x2, Pallas kernels, backward(): pl.pallas_call(lambda *refs: backward_kernel(nb, subset, *refs), grid=(bl...  49.3 us

profile of v2, /device:TPU:1, one launch (start us, length us, event | category | flops | bytes accessed | tf_op | source)
XLA Modules:
  0.0 166.4 jit_solution(14413060127653765686)
XLA Ops:
  0.6 0.7 fusion.9
  1.3 1.4 fusion.2
  2.7 0.8 add_select_fusion.1
  3.5 0.4 fusion.1
  3.8 0.6 convert_element_type.15.refs_2_
  4.4 26.8 %forward.2 = f32[1536,128]{1,0:T(8,128)} custom-call(s32[2,8,128]{2,1,0:T(8,128)} %get-tuple-element.11.refs_0_, f32[2,8,128]{2,1,0:T(8,128)} %get-tuple-element.10.refs_1_, s32[2,8,24]{2,1,0:T(8,128)} %convert_element_type.15.refs_2_, s32[8,16]{1,0:T(8,128)} %constant.84.clone.refs_3_, f32[128,8,1024]{2,1,0:T(8,128)} %refs_4_.3, ...), custom_call_target="tpu_custom_call" | custom-call | tf_op jit(solution)/shard_map/forward/pallas_call | solution.py:431
  31.2 29.8 %exchange.2 = (f32[4,2,4,48,128]{4,3,2,1,0:T(8,128)}, f32[16,384]{1,0:T(8,128)}) custom-call(f32[4,2,4,48,128]{4,3,2,1,0:T(8,128)} %bitcast.6, s32[2,512]{1,0:T(2,128)} %refs_1_.3, f32[2,3,8]{2,1,0:T(4,128)} %constant.86.clone.refs_2_, f32[2,64,384]{2,1,0:T(8,128)} %refs_3_.7), custom_call_target="tpu_custom_call" | custom-call | tf_op jit(solution)/shard_map/exchange/pallas_call | solution.py:400
  61.0 24.4 %backward.2.refs_4_ = f32[128,8,1024]{2,1,0:T(8,128)} custom-call(s32[2,8,128]{2,1,0:T(8,128)} %get-tuple-element.11.refs_0_, f32[2,8,128]{2,1,0:T(8,128)} %get-tuple-element.10.refs_1_, s32[2,8,24]{2,1,0:T(8,128)} %convert_element_type.15.refs_2_, s32[8,16]{1,0:T(8,128)} %constant.84.clone.refs_3_, f32[128,8,1024]{2,1,0:T(8,128)} %refs_4_.3, ...), custom_call_target="tpu_custom_call" | custom-call | tf_op jit(solution)/shard_map/backward/pallas_call | solution.py:450
  85.4 27.4 %forward.3 = f32[1536,128]{1,0:T(8,128)} custom-call(s32[2,8,128]{2,1,0:T(8,128)} %get-tuple-element.11.refs_0_, f32[2,8,128]{2,1,0:T(8,128)} %get-tuple-element.10.refs_1_, s32[2,8,24]{2,1,0:T(8,128)} %convert_element_type.15.refs_2_, s32[8,16]{1,0:T(8,128)} %constant.88.clone.refs_3_, f32[128,8,1024]{2,1,0:T(8,128)} %backward.2.refs_4_, ...), custom_call_target="tpu_custom_call" | custom-call | tf_op jit(solution)/shard_map/forward/pallas_call | solution.py:431
  112.8 28.1 %exchange.3 = (f32[4,2,4,48,128]{4,3,2,1,0:T(8,128)}, f32[16,384]{1,0:T(8,128)}) custom-call(f32[4,2,4,48,128]{4,3,2,1,0:T(8,128)} %bitcast.5, s32[2,512]{1,0:T(2,128)} %refs_1_.3, f32[2,3,8]{2,1,0:T(4,128)} %constant.86.clone.refs_2_, f32[2,64,384]{2,1,0:T(8,128)} %refs_3_.7), custom_call_target="tpu_custom_call" | custom-call | tf_op jit(solution)/shard_map/exchange/pallas_call | solution.py:400
  140.9 0.0 copy-start
  140.9 24.9 %backward.3 = f32[128,8,1024]{2,1,0:T(8,128)} custom-call(s32[2,8,128]{2,1,0:T(8,128)} %get-tuple-element.11.refs_0_, f32[2,8,128]{2,1,0:T(8,128)} %get-tuple-element.10.refs_1_, s32[2,8,24]{2,1,0:T(8,128)} %convert_element_type.15.refs_2_, s32[8,16]{1,0:T(8,128)} %constant.88.clone.refs_3_, f32[128,8,1024]{2,1,0:T(8,128)} %backward.2.refs_4_, ...), custom_call_target="tpu_custom_call" | custom-call | tf_op jit(solution)/shard_map/backward/pallas_call | solution.py:450
  165.8 0.0 copy-done
  165.8 0.6 copy.16
Async XLA Ops:
  140.9 24.9 %copy-start = (f32[16,384]{1,0:T(8,128)S(1)}, f32[16,384]{1,0:T(8,128)}, u32[]{:S(2)}) copy-start(f32[16,384]{1,0:T(8,128)} %get-tuple-element.7) | copy-start | bytes 73732

commit v3 on v2

--- a/solution.py
+++ b/solution.py
@@ -65,47 +65,96 @@
 TILES = RAYS // SPAN
 
 
-def list_tiles(subset, win_ref, tiles):
+WIDE = 4
+
+
+def list_tiles(subset, win_ref, tiles, starts):
     def angle(a, n):
+        starts[a] = n
         for i in range(TILES):
-            hit = win_ref[subset, a, i]
+            hit = win_ref[0, (subset * ANG_SUB + a) * TILES + i]
             tiles[n] = a * TILES + i
             n = n + hit
         return n
 
-    n = lax.fori_loop(0, ANG_SUB, angle, 0)
-    tiles[n] = tiles[jnp.maximum(n - 1, 0)]
-    return (n + 1) // 2
-
-
-def over_tiles(tiles, half_count, body):
-    def pair(i, c):
-        for j in range(2):
-            at = tiles[2 * i + j]
-            body(at // TILES, lax.rem(at, TILES), j)
-        return c
-
-    lax.fori_loop(0, half_count, pair, 0)
+    starts[ANG_SUB] = lax.fori_loop(0, ANG_SUB, angle, 0)
+
+
+def over_tiles(tiles, starts, body):
+    n = starts[ANG_SUB]
+
+    def some(i, c):
+        for j in range(WIDE):
+            t = jnp.minimum(WIDE * i + j, n - 1)
+            body(t, tiles[t])
+        return c
+
+    lax.fori_loop(0, (n + WIDE - 1) // WIDE, some, 0)
+
+
+def over_angle(a, tiles, starts, body):
+    def one(t, c):
+        body(t, tiles[t] - a * TILES)
+        return c
+
+    lax.fori_loop(starts[a], starts[a + 1], one, 0)
+
+
+def shifted(ref, base, offsets, lane_q):
+    fine = [o % 8 for o in offsets]
+    coarse = [o // 8 for o in offsets]
+    low, high = min(coarse), max(coarse)
+
+    def member(values, value):
+        hits = [lane_q == q for q, v in enumerate(values) if v == value]
+        mask = hits[0]
+        for h in hits[1:]:
+            mask = mask | h
+        return mask
+
+    rows = None
+    for f in sorted(set(fine)):
+        part = ref[pl.ds(base + 8 * low + f, SPAN + 8 * (high - low)), :]
+        rows = part if rows is None else jnp.where(member(fine, f), part, rows)
+    out = None
+    for c in sorted(set(coarse)):
+        part = rows[8 * (c - low):8 * (c - low) + SPAN]
+        out = part if out is None else jnp.where(member(coarse, c), part, out)
+    return out
+
+
+def spread_lanes(x, lane_q):
+    rows = [x]
+    for half in (8, 4, 2, 1):
+        low = lane_q % (2 * half) < half
+        turned = [pltpu.roll(x, half * 8, 1) for x in rows]
+        rows = ([jnp.where(low, x, y) for x, y in zip(rows, turned)]
+                + [jnp.where(low, y, x) for x, y in zip(rows, turned)])
+    return [rows[int(format(r, "04b")[::-1], 2)] for r in range(16)]
+
+
+def sixteenth(base, r, tall):
+    return pl.ds(base + 8 * r, 8) if tall else pl.ds(base + r, 8, stride=16)
 
 
 def aligned(x, m):
     return pl.multiple_of(x, m)
 
 
-def forward_kernel(nb, subset, lo_ref, frac_ref, win_ref, first_ref, vol_ref, grid_ref, out_ref,
-                   fold_scr, acc, tiles):
+def forward_kernel(nb, subset, first, tall, lo_ref, frac_ref, win_ref, vol_ref, grid_ref, out_ref,
+                   tot, acc, tiles, starts):
     step = pl.program_id(0)
 
     @pl.when(step == 0)
     def _():
         zero = jnp.zeros((2 * SPAN, LANES), jnp.float32)
 
-        tiles[ANG_SUB * TILES + 1] = list_tiles(subset, win_ref, tiles)
-
-        def clear(a, i, j):
-            acc[pl.ds(aligned(a * TALL + i * SPAN, SPAN), 2 * SPAN), :] = zero
-
-        over_tiles(tiles, tiles[ANG_SUB * TILES + 1], clear)
+        list_tiles(subset, win_ref, tiles, starts)
+
+        def clear(t, at):
+            acc[pl.ds(aligned(at // TILES * TALL + lax.rem(at, TILES) * SPAN, SPAN), 2 * SPAN), :] = zero
+
+        over_tiles(tiles, starts, clear)
 
     width = SUB * BLK_SIDE
     group = BLK_SIDE // SUB
@@ -132,62 +181,53 @@
     @pl.when(step == pl.num_programs(0) - 1)
     def _():
         out_ref[...] = jnp.zeros_like(out_ref)
-        span = SPAN
-        lane_q = lax.broadcasted_iota(jnp.int32, (span, LANES), 1) // 8
-        line_q = lax.broadcasted_iota(jnp.int32, (span // 16, LANES), 1) // 8
-
-        def merge(a, i, j):
-            k = i * span
-            total = jnp.zeros((span, LANES), jnp.float32)
-            for q in range(NQ):
-                src = a * TALL + PAD + k - first_ref[a, q]
-                total = jnp.where(lane_q == q, acc[pl.ds(src, span), :], total)
-            fold_scr[j] = total
-            rows = [fold_scr[j, pl.ds(r, span // 16, stride=16), :] for r in range(16)]
-            for half in (8, 4, 2, 1):
-                low = line_q % (2 * half) < half
-                rows = [jnp.where(low, rows[r] + pltpu.roll(rows[r], LANES - half * 8, 1),
-                                  rows[r + half] + pltpu.roll(rows[r + half], half * 8, 1))
-                        for r in range(half)]
-            out_ref[pl.ds(aligned(a * (RAYS // 16) + i * 8, 8), 8), :] = rows[0]
-
-        over_tiles(tiles, tiles[ANG_SUB * TILES + 1], merge)
-
-
-def backward_kernel(nb, subset, lo_ref, frac_ref, win_ref, first_ref, vol_ref, base_ref, res_ref, out_ref,
-                    e_scr, rb, dd, tiles):
+        lane_q = lax.broadcasted_iota(jnp.int32, (1, LANES), 1) // 8
+
+        for a in range(ANG_SUB):
+            def merge(t, i, a=a):
+                base = aligned(a * TALL + PAD + i * SPAN, 32)
+                tot[pl.ds(aligned(t * SPAN, SPAN), SPAN), :] = shifted(
+                    acc, base, [-int(o) for o in first[a]], lane_q)
+
+            over_angle(a, tiles, starts, merge)
+
+        def fold(t, at):
+            rows = [tot[sixteenth(aligned(t * SPAN, SPAN), r, tall), :] for r in range(16)]
+            for half in (1, 2, 4, 8):
+                low = lane_q % (2 * half) < half
+                rows = [jnp.where(low, x, y) + pltpu.roll(jnp.where(low, y, x), half * 8, 1)
+                        for x, y in zip(rows[0::2], rows[1::2])]
+            out_ref[pl.ds(aligned(at * 8, 8), 8), :] = rows[0]
+
+        over_tiles(tiles, starts, fold)
+
+
+def backward_kernel(nb, subset, first, tall, lo_ref, frac_ref, win_ref, vol_ref, base_ref, res_ref, own_ref, out_ref, last_ref,
+                    e_scr, rb, dd, tiles, starts):
     step = pl.program_id(0)
 
     @pl.when(step == 0)
     def _():
         fill_grid(base_ref, e_scr)
-        span = SPAN
-        lane_q = lax.broadcasted_iota(jnp.int32, (span, LANES), 1) // 8
-        row_j = lax.broadcasted_iota(jnp.int32, (span, LANES), 0) % 16
-        pick = lane_q == row_j
-        fold = jnp.where(
-            lax.broadcasted_iota(jnp.int32, (LANES, LANES), 0) % 8
-            == lax.broadcasted_iota(jnp.int32, (LANES, LANES), 1) % 8, 1.0, 0.0).astype(jnp.bfloat16)
-
-        count = list_tiles(subset, win_ref, tiles)
-
-        def widen(a, i, j):
-            rows = res_ref[pl.ds(aligned(a * (RAYS // 16) + i * 8, 8), 8), :]
-            wide = jnp.broadcast_to(rows[:, None, :], (8, 16, LANES)).reshape(span, LANES)
-            wide = jnp.where(pick, wide, 0.0).astype(jnp.bfloat16)
-            rb[pl.ds(aligned(a * TALL + PAD + i * span, 8), span), :] = jnp.dot(
-                wide, fold, preferred_element_type=jnp.float32)
-
-        def shift(a, i, j):
-            k = i * span
-            total = jnp.zeros((span, LANES), jnp.float32)
-            for q in range(NQ):
-                src = a * TALL + PAD + k + first_ref[a, q]
-                total = jnp.where(lane_q == q, rb[pl.ds(src, span), :], total)
-            dd[pl.ds(aligned(a * RAYS + k, span), span), :] = total
-
-        over_tiles(tiles, count, widen)
-        over_tiles(tiles, count, shift)
+        lane_q = lax.broadcasted_iota(jnp.int32, (1, LANES), 1) // 8
+        last_ref[...] = own_ref[...]
+        list_tiles(subset, win_ref, tiles, starts)
+
+        def widen(t, at):
+            rows = spread_lanes(res_ref[pl.ds(aligned(at * 8, 8), 8), :], lane_q)
+            base = aligned(at // TILES * TALL + PAD + lax.rem(at, TILES) * SPAN, 32)
+            for r in range(16):
+                rb[sixteenth(base, r, tall), :] = rows[r]
+
+        over_tiles(tiles, starts, widen)
+
+        for a in range(ANG_SUB):
+            def shift(t, i, a=a):
+                base = aligned(a * TALL + PAD + i * SPAN, 32)
+                dd[pl.ds(aligned(a * RAYS + i * SPAN, SPAN), SPAN), :] = shifted(
+                    rb, base, [int(o) for o in first[a]], lane_q)
+
+            over_angle(a, tiles, starts, shift)
 
     width = SUB * BLK_SIDE
     group = BLK_SIDE // SUB
@@ -236,8 +276,14 @@
     return total
 
 
-def exchange_kernel(subset, part_ref, live_ref, table_ref, meas_ref, full_ref, own_ref,
-                    half, inbox, sums, lines_scr, halves, meas, stage, gathered,
+def ray_at(line, lane, tall):
+    if tall:
+        return line // 8 * LANES + lane // 8 * 8 + line % 8
+    return line * 16 + lane // 8
+
+
+def exchange_kernel(subset, tall, part_ref, live_ref, table_ref, meas_ref, full_ref, own_ref,
+                    half, inbox, sums, lines_scr, flat, halves, meas, stage, gathered,
                     meas_sem, pair_send, pair_recv, send_sem, recv_sem, rs_send, rs_recv,
                     out_send, out_recv, back_send, back_recv):
     g, p = lax.axis_index("group"), lax.axis_index("patch")
@@ -303,7 +349,7 @@
     mine = p // pairs
     line = lax.broadcasted_iota(jnp.int32, halves.shape[1:], 0)
     lane = lax.broadcasted_iota(jnp.int32, halves.shape[1:], 1)
-    ray = lax.rem(first_row, NTILE) * RAYS_TILE + mine * (lines * 8) + line * 16 + lane // 8
+    ray = lax.rem(first_row, NTILE) * RAYS_TILE + mine * (lines * 8) + ray_at(line, lane, tall)
     ray = (ray.astype(jnp.float32) + (0.5 - RAYS * 0.5)) * (1.0 / spread)
     a = first_row // NTILE
     halves[mine] = ray_sums(
@@ -317,33 +363,46 @@
         to_owner(d).wait_recv()
         return c
 
+    read.wait()
+    wide = lines // rows
+    lane_q = lax.broadcasted_iota(jnp.int32, (1, LANES), 1) // 8
+
+    def retile(forth):
+        def one(i, c):
+            at = pl.ds(aligned(i * 8, 8), 8)
+            for r, x in enumerate(spread_lanes(lines_scr[at, :], lane_q)):
+                flat[sixteenth(0, r, not forth), :] = x
+            out = flat[sixteenth(0, 0, forth), :]
+            for r in range(1, 16):
+                out = jnp.where(lane_q == r, flat[sixteenth(0, r, forth), :], out)
+            lines_scr[at, :] = out
+            return c
+
+        if tall:
+            lax.fori_loop(0, lines // 8, one, 0)
+
+    for c in range(wide):
+        lines_scr[pl.ds(c, rows, stride=wide), :] = meas[:, c * LANES:(c + 1) * LANES]
+    retile(True)
+
     inbox[column, g] = sums[column, g]
     lax.fori_loop(1, n, got, 0)
     total = jnp.zeros(stage.shape, jnp.float32)
     for i in range(pairs):
         for j in range(groups):
             total = total + inbox[i, j]
-    lines_scr[...] = total
-    read.wait()
+    ray = ray_at(lax.broadcasted_iota(jnp.int32, stage.shape, 0),
+                 lax.broadcasted_iota(jnp.int32, stage.shape, 1), tall)
+    row = ray // RAYS_TILE
+    live = jnp.zeros(stage.shape, jnp.int32)
+    for r in range(rows):
+        live = jnp.where(row == r, live_ref[subset, first_row + r], live)
     trade.wait()
-    at = lax.broadcasted_iota(jnp.int32, (rows, LANES), 0)
-    live = jnp.zeros((rows, LANES), jnp.int32)
-    for r in range(rows):
-        live = jnp.where(at == r, live_ref[subset, first_row + r], live)
-    ray = lax.broadcasted_iota(jnp.int32, (rows, LANES), 1) // 8
-    wide = lines // rows
-    residuals = []
-    for c in range(wide):
-        sums_c = jnp.concatenate(
-            [halves[h, pl.ds(c, rows // 2, stride=wide), :] for h in range(2)], axis=0)
-        level = lines_scr[pl.ds(c, rows, stride=wide), :] / jnp.maximum(sums_c, 1.0)
-        differ = meas[:, c * LANES:(c + 1) * LANES] - level
-        residual = jnp.where(ray + c * 16 < live, differ, 0.0)
-        own_ref[:, c * LANES:(c + 1) * LANES] = residual
-        residuals.append(residual)
-    for c in range(wide):
-        lines_scr[pl.ds(c, rows, stride=wide), :] = residuals[c]
-    stage[...] = lines_scr[...].astype(jnp.bfloat16)
+    sums_of = jnp.concatenate([halves[0], halves[1]], axis=0)
+    differ = lines_scr[...] - total / jnp.maximum(sums_of, 1.0)
+    residual = jnp.where(ray - row * RAYS_TILE < live, differ, 0.0)
+    lines_scr[...] = residual
+    stage[...] = residual.astype(jnp.bfloat16)
 
     def to_all(d):
         pc, pg = peer(d)
@@ -382,6 +441,9 @@
     lax.fori_loop(1, n, go_all, 0)
     gathered[column, parity, g] = stage[...]
     share(0).start()
+    retile(False)
+    for c in range(wide):
+        own_ref[:, c * LANES:(c + 1) * LANES] = lines_scr[pl.ds(c, rows, stride=wide), :]
     lax.fori_loop(1, n, pass_on, 0)
     lax.fori_loop(0, n, finish, 0)
     lax.fori_loop(1, n, sent, 0)
@@ -390,7 +452,7 @@
         full_ref[i] = gathered[i].astype(jnp.float32)
 
 
-def exchange(subset, partial, live, table, measured, rows, groups, patches):
+def exchange(subset, tall, partial, live, table, measured, rows, groups, patches):
     pairs = patches // 2
     lines = rows * measured.shape[2] // LANES
     shape = (pairs, 2, groups, lines, LANES)
@@ -398,7 +460,7 @@
     dma = pltpu.SemaphoreType.DMA
     vmem = pl.BlockSpec(memory_space=pltpu.VMEM)
     full, own = pl.pallas_call(
-        lambda *refs: exchange_kernel(subset, *refs),
+        lambda *refs: exchange_kernel(subset, tall, *refs),
         in_specs=[vmem, smem(), smem(), pl.BlockSpec(memory_space=pl.ANY)],
         out_specs=[vmem] * 2,
         out_shape=[jax.ShapeDtypeStruct(shape, jnp.float32),
@@ -407,6 +469,7 @@
                         pltpu.VMEM((pairs, groups, lines, LANES), jnp.float32),
                         pltpu.VMEM((pairs, groups, lines, LANES), jnp.float32),
                         pltpu.VMEM((lines, LANES), jnp.float32),
+                        pltpu.VMEM((SPAN, LANES), jnp.float32),
                         pltpu.VMEM((2, lines // 2, LANES), jnp.float32),
                         pltpu.VMEM((rows, measured.shape[2]), jnp.float32),
                         pltpu.VMEM((lines, LANES), jnp.bfloat16),
@@ -423,46 +486,51 @@
     return pl.BlockSpec(memory_space=pltpu.SMEM)
 
 
-def forward(subset, volume, lo, frac, win, base, first):
+def forward(subset, tall, volume, lo, frac, win, base, first):
     blocks, slices, _ = volume.shape
     nb = 8
     lines = ANG_SUB * RAYS // 16
     grid = (np.repeat(base, R, axis=0) - np.tile(np.arange(R), ANG_SUB)[:, None]) * (1.0 / spread)
     return pl.pallas_call(
-        lambda *refs: forward_kernel(nb, subset, *refs),
+        lambda *refs: forward_kernel(nb, subset, first, tall, *refs),
         grid=(blocks // nb,),
-        in_specs=[smem(), smem(), smem(), smem(),
+        in_specs=[smem(), smem(), smem(),
                   pl.BlockSpec((nb, slices, VOX), lambda i: (i, 0, 0)),
                   pl.BlockSpec((VOX, LANES), lambda i: (0, 0))],
         out_specs=pl.BlockSpec((lines, LANES), lambda i: (0, 0)),
         out_shape=jax.ShapeDtypeStruct((lines, LANES), jnp.float32),
-        scratch_shapes=[pltpu.VMEM((2, SPAN, LANES), jnp.float32),
+        scratch_shapes=[pltpu.VMEM((ANG_SUB * RAYS, LANES), jnp.float32),
                         pltpu.VMEM((ANG_SUB * TALL, LANES), jnp.float32),
-                        pltpu.SMEM((ANG_SUB * TILES + 2,), jnp.int32)],
+                        pltpu.SMEM((ANG_SUB * TILES + 1,), jnp.int32),
+                        pltpu.SMEM((ANG_SUB + 1,), jnp.int32)],
         compiler_params=pltpu.CompilerParams(vmem_limit_bytes=VMEM_LIMIT),
         name="forward",
-    )(lo, frac, win, first, volume, grid.T.astype(np.float32))
-
-
-def backward(subset, volume, residual, lo, frac, win, base, first):
+    )(lo, frac, win, volume, grid.T.astype(np.float32))
+
+
+def backward(subset, tall, volume, residual, own, lo, frac, win, base, first):
     blocks, slices, _ = volume.shape
     nb = 8
     return pl.pallas_call(
-        lambda *refs: backward_kernel(nb, subset, *refs),
+        lambda *refs: backward_kernel(nb, subset, first, tall, *refs),
         grid=(blocks // nb,),
-        in_specs=[smem(), smem(), smem(), smem(),
+        in_specs=[smem(), smem(), smem(),
                   pl.BlockSpec((nb, slices, VOX), lambda i: (i, 0, 0)),
                   pl.BlockSpec((ANG_SUB, VOX), lambda i: (0, 0)),
-                  pl.BlockSpec(residual.shape, lambda i: (0, 0))],
-        out_specs=pl.BlockSpec((nb, slices, VOX), lambda i: (i, 0, 0)),
-        out_shape=jax.ShapeDtypeStruct(volume.shape, jnp.float32),
+                  pl.BlockSpec(residual.shape, lambda i: (0, 0)),
+                  pl.BlockSpec(own.shape, lambda i: (0, 0))],
+        out_specs=[pl.BlockSpec((nb, slices, VOX), lambda i: (i, 0, 0)),
+                   pl.BlockSpec(own.shape, lambda i: (0, 0))],
+        out_shape=[jax.ShapeDtypeStruct(volume.shape, jnp.float32),
+                   jax.ShapeDtypeStruct(own.shape, jnp.float32)],
         scratch_shapes=[pltpu.VMEM((ANG_SUB * R, VOX), jnp.float32),
                         pltpu.VMEM((ANG_SUB * TALL, LANES), jnp.float32),
                         pltpu.VMEM((ANG_SUB * RAYS, LANES), jnp.float32),
-                        pltpu.SMEM((ANG_SUB * TILES + 2,), jnp.int32)],
+                        pltpu.SMEM((ANG_SUB * TILES + 1,), jnp.int32),
+                        pltpu.SMEM((ANG_SUB + 1,), jnp.int32)],
         compiler_params=pltpu.CompilerParams(vmem_limit_bytes=VMEM_LIMIT),
         name="backward",
-    )(lo, frac, win, first, volume, base, residual)
+    )(lo, frac, win, volume, base, residual, own)
 
 
 def ray_table():
@@ -474,20 +542,42 @@
     return table.astype(np.float32)
 
 
-def placing(place):
+def placing_kernel(place_ref, lo_ref, frac_ref, win_ref):
     half = IMG_BLK * BLK_SIDE * 0.5
+    shape = lo_ref.shape[1:]
+    place = jnp.broadcast_to(place_ref[...], shape)
     x = (place % IMG_BLK).astype(jnp.float32) * BLK_SIDE + (BLK_SIDE * 0.5 - half)
     y = (place // IMG_BLK).astype(jnp.float32) * BLK_SIDE + (BLK_SIDE * 0.5 - half)
-    theta = np.array([angles(subset) for subset in range(SUBSETS)])
-    cosine = np.cos(theta).astype(np.float32)[:, :, None]
-    sine = np.sin(theta).astype(np.float32)[:, :, None]
-    z = x * cosine + y * sine + (RAYS * 0.5 - 0.5)
-    low = jnp.floor(z)
-    lo = low.astype(jnp.int32)
-    tile = jnp.arange(TILES, dtype=jnp.int32)[:, None]
-    near = ((lo - PAD) // SPAN)[:, :, None, :] == tile
-    near |= ((lo + R + PAD) // SPAN)[:, :, None, :] == tile
-    return lo, (z - low) * (1.0 / spread), jnp.any(near, axis=3).astype(jnp.int32)
+    angle = lax.broadcasted_iota(jnp.int32, shape, 0)
+    tile = lax.broadcasted_iota(jnp.int32, (TILES, shape[1]), 0)
+    near = []
+    for subset in range(SUBSETS):
+        cosine = sine = jnp.zeros(shape, jnp.float32)
+        for a, theta in enumerate(angles(subset)):
+            cosine = jnp.where(angle == a, np.float32(math.cos(theta)), cosine)
+            sine = jnp.where(angle == a, np.float32(math.sin(theta)), sine)
+        z = x * cosine + y * sine + (RAYS * 0.5 - 0.5)
+        low = jnp.floor(z)
+        lo = low.astype(jnp.int32)
+        lo_ref[subset] = lo
+        frac_ref[subset] = (z - low) * (1.0 / spread)
+        ends = (lo - PAD) // SPAN, (lo + R + PAD) // SPAN
+        for a in range(ANG_SUB):
+            hit = (ends[0][a:a + 1] == tile) | (ends[1][a:a + 1] == tile)
+            near.append(jnp.where(hit, 1.0, 0.0))
+    count = lax.dot_general(jnp.ones((8, shape[1]), jnp.bfloat16), jnp.concatenate(near, axis=0).astype(jnp.bfloat16),
+                            (((1,), (1,)), ((), ())), preferred_element_type=jnp.float32)
+    win_ref[...] = jnp.where(count[0:1] > 0.0, 1, 0)
+
+
+def placing(place):
+    shape = (SUBSETS, ANG_SUB, place.shape[0])
+    return pl.pallas_call(
+        placing_kernel,
+        out_shape=[jax.ShapeDtypeStruct(shape, jnp.int32), jax.ShapeDtypeStruct(shape, jnp.float32),
+                   jax.ShapeDtypeStruct((1, SUBSETS * ANG_SUB * TILES), jnp.int32)],
+        name="placing",
+    )(place.reshape(1, -1))
 
 
 def shards(volume, block_place, measured, live_rays):
@@ -496,13 +586,14 @@
     rows = ANG_SUB * NTILE // patches // groups
     lo, frac, win = placing(block_place)
     table = ray_table()
+    tall = rows * RAYS_TILE % (2 * LANES) == 0
     estimate = volume
     own = None
     for subset in range(SUBSETS):
         base, first = geometry(subset)
-        partial = forward(subset, estimate, lo, frac, win, base, first)
-        full, own = exchange(subset, partial, live_rays, table, measured, rows, groups, patches)
-        estimate = backward(subset, estimate, full, lo, frac, win, base, first)
+        partial = forward(subset, tall, estimate, lo, frac, win, base, first)
+        full, own = exchange(subset, tall, partial, live_rays, table, measured, rows, groups, patches)
+        estimate, own = backward(subset, tall, estimate, full, own, lo, frac, win, base, first)
     return (estimate, own[None])
 
 

time: 170 us -> 147 us (0.86); the launches traced: 166 us -> 145 us
  Pallas kernels: 161 us -> 145 us
  other arithmetic: 3.79 us -> 0 us
    pallas_call x6 -> x7, Pallas kernels: 161 us -> 145 us  [the longest x2 56.8 us: exchange(): pl.pallas_call(lambda *refs: exchange_kernel(subset, tall, *refs), in_spe...]
where the time goes in v3:
time: 147 us; the launch traced here: 145 us
  Pallas kernels  145 us (99%)
    pallas_call x2, Pallas kernels, exchange(): pl.pallas_call(lambda *refs: exchange_kernel(subset, tall, *refs), in_spe...  56.8 us
    pallas_call x2, Pallas kernels, backward(): pl.pallas_call(lambda *refs: backward_kernel(nb, subset, first, tall, *re...  43.4 us
    pallas_call x2, Pallas kernels, forward(): pl.pallas_call(lambda *refs: forward_kernel(nb, subset, first, tall, *ref...  43.2 us

profile of v3, /device:TPU:1, one launch (start us, length us, event | category | flops | bytes accessed | tf_op | source)
XLA Modules:
  0.0 145.5 jit_solution(11346114992748944728)
XLA Ops:
  0.6 1.4 placing.1
  2.1 21.5 %forward.2 = f32[1536,128]{1,0:T(8,128)} custom-call(s32[2,8,128]{2,1,0:T(8,128)} %get-tuple-element.12.refs_0_, f32[2,8,128]{2,1,0:T(8,128)} %get-tuple-element.13.refs_1_, s32[1,384]{1,0:T(1,128)} %get-tuple-element.14.refs_2_, f32[128,8,1024]{2,1,0:T(8,128)} %refs_3_.6, f32[1024,128]{1,0:T(8,128)} %constant.10.clone.refs_4_), custom_call_target="tpu_custom_call" | custom-call | tf_op jit(solution)/shard_map/forward/pallas_call | solution.py:494
  23.5 29.3 %exchange.2 = (f32[4,2,4,48,128]{4,3,2,1,0:T(8,128)}, f32[16,384]{1,0:T(8,128)}) custom-call(f32[4,2,4,48,128]{4,3,2,1,0:T(8,128)} %bitcast.7, s32[2,512]{1,0:T(2,128)} %refs_1_.3, f32[2,3,8]{2,1,0:T(4,128)} %constant.11.clone.refs_2_, f32[2,64,384]{2,1,0:T(8,128)} %refs_3_.7), custom_call_target="tpu_custom_call" | custom-call | tf_op jit(solution)/shard_map/exchange/pallas_call | solution.py:462
  52.9 21.6 %backward.2 = (f32[128,8,1024]{2,1,0:T(8,128)}, f32[16,384]{1,0:T(8,128)}) custom-call(s32[2,8,128]{2,1,0:T(8,128)} %get-tuple-element.12.refs_0_, f32[2,8,128]{2,1,0:T(8,128)} %get-tuple-element.13.refs_1_, s32[1,384]{1,0:T(1,128)} %get-tuple-element.14.refs_2_, f32[128,8,1024]{2,1,0:T(8,128)} %refs_3_.6, f32[8,1024]{1,0:T(8,128)} %constant.12.clone.refs_4_, ...), custom_call_target="tpu_custom_call" | custom-call | tf_op jit(solution)/shard_map/backward/pallas_call | solution.py:514
  74.5 21.7 %forward.3 = f32[1536,128]{1,0:T(8,128)} custom-call(s32[2,8,128]{2,1,0:T(8,128)} %get-tuple-element.12.refs_0_, f32[2,8,128]{2,1,0:T(8,128)} %get-tuple-element.13.refs_1_, s32[1,384]{1,0:T(1,128)} %get-tuple-element.14.refs_2_, f32[128,8,1024]{2,1,0:T(8,128)} %get-tuple-element.17.refs_3_, f32[1024,128]{1,0:T(8,128)} %constant.13.clone.refs_4_), custom_call_target="tpu_custom_call" | custom-call | tf_op jit(solution)/shard_map/forward/pallas_call | solution.py:494
  96.2 27.5 %exchange.3 = (f32[4,2,4,48,128]{4,3,2,1,0:T(8,128)}, f32[16,384]{1,0:T(8,128)}) custom-call(f32[4,2,4,48,128]{4,3,2,1,0:T(8,128)} %bitcast.6, s32[2,512]{1,0:T(2,128)} %refs_1_.3, f32[2,3,8]{2,1,0:T(4,128)} %constant.11.clone.refs_2_, f32[2,64,384]{2,1,0:T(8,128)} %refs_3_.7), custom_call_target="tpu_custom_call" | custom-call | tf_op jit(solution)/shard_map/exchange/pallas_call | solution.py:462
  123.7 21.8 %backward.3 = (f32[128,8,1024]{2,1,0:T(8,128)}, f32[16,384]{1,0:T(8,128)}) custom-call(s32[2,8,128]{2,1,0:T(8,128)} %get-tuple-element.12.refs_0_, f32[2,8,128]{2,1,0:T(8,128)} %get-tuple-element.13.refs_1_, s32[1,384]{1,0:T(1,128)} %get-tuple-element.14.refs_2_, f32[128,8,1024]{2,1,0:T(8,128)} %get-tuple-element.17.refs_3_, ...), custom_call_target="tpu_custom_call" | custom-call | tf_op jit(solution)/shard_map/backward/pallas_call | solution.py:514

commit v4 on v3

--- a/solution.py
+++ b/solution.py
@@ -25,6 +25,7 @@
 RAYS = NTILE * RAYS_TILE
 LANES = 128
 PAD = 32
+EARLY = 3
 SPAN = 128
 TALL = RAYS + SPAN
 VMEM_LIMIT = 60 * 1024 * 1024
@@ -203,7 +204,7 @@
 
 
 def backward_kernel(nb, subset, first, tall, lo_ref, frac_ref, win_ref, vol_ref, base_ref, res_ref, own_ref, out_ref, last_ref,
-                    e_scr, rb, dd, tiles, starts):
+                    e_scr, res, rb, dd, tiles, starts):
     step = pl.program_id(0)
 
     @pl.when(step == 0)
@@ -211,10 +212,11 @@
         fill_grid(base_ref, e_scr)
         lane_q = lax.broadcasted_iota(jnp.int32, (1, LANES), 1) // 8
         last_ref[...] = own_ref[...]
+        res[...] = res_ref[...].astype(jnp.float32)
         list_tiles(subset, win_ref, tiles, starts)
 
         def widen(t, at):
-            rows = spread_lanes(res_ref[pl.ds(aligned(at * 8, 8), 8), :], lane_q)
+            rows = spread_lanes(res[pl.ds(aligned(at * 8, 8), 8), :], lane_q)
             base = aligned(at // TILES * TALL + PAD + lax.rem(at, TILES) * SPAN, 32)
             for r in range(16):
                 rb[sixteenth(base, r, tall), :] = rows[r]
@@ -270,10 +272,15 @@
             total = total + bump * bump
         return total
 
-    total = lax.fori_loop(0, count, row, jnp.zeros(shape, jnp.float32), unroll=4)
-    for d in (1, 2, 4):
-        total = total + jnp.where(part // d % 2 == 0, pltpu.roll(total, LANES - d, 1), pltpu.roll(total, d, 1))
-    return total
+    def fold(total):
+        for d in (1, 2, 4):
+            total = total + jnp.where(
+                part // d % 2 == 0, pltpu.roll(total, LANES - d, 1), pltpu.roll(total, d, 1))
+        return total
+
+    early = count * EARLY // 8
+    first = lax.fori_loop(0, early, row, jnp.zeros(shape, jnp.float32), unroll=4)
+    return first, lambda total: fold(lax.fori_loop(early, count, row, total, unroll=4))
 
 
 def ray_at(line, lane, tall):
@@ -282,9 +289,9 @@
     return line * 16 + lane // 8
 
 
-def exchange_kernel(subset, tall, part_ref, live_ref, table_ref, meas_ref, full_ref, own_ref,
-                    half, inbox, sums, lines_scr, flat, halves, meas, stage, gathered,
-                    meas_sem, pair_send, pair_recv, send_sem, recv_sem, rs_send, rs_recv,
+def exchange_kernel(subset, tall, part_ref, live_ref, table_ref, meas_ref, gathered, own_ref,
+                    keep, half, inbox, sums, lines_scr, flat, halves, meas, stage,
+                    meas_sem, keep_sem, pair_send, pair_recv, send_sem, recv_sem, rs_send, rs_recv,
                     out_send, out_recv, back_send, back_recv):
     g, p = lax.axis_index("group"), lax.axis_index("patch")
     pairs, groups = inbox.shape[0], inbox.shape[1]
@@ -313,38 +320,8 @@
     lax.fori_loop(1, n, greet, 0)
     read = pltpu.make_async_copy(meas_ref.at[subset, pl.ds(g * rows, rows)], meas, meas_sem)
     read.start()
-    pl.semaphore_wait(barrier, n)
-
-    def swap(d):
-        pc = lax.rem(column + d, pairs)
-        return pltpu.make_async_remote_copy(
-            src_ref=part_ref.at[pc, 1 - parity], dst_ref=half.at[pc], send_sem=pair_send.at[d],
-            recv_sem=pair_recv.at[d], device_id=partner, device_id_type=mesh_id)
-
-    def to_owner(d):
-        pc, pg = peer(d)
-        return pltpu.make_async_remote_copy(
-            src_ref=sums.at[pc, pg], dst_ref=inbox.at[column, g], send_sem=send_sem.at[d],
-            recv_sem=recv_sem.at[d], device_id=(pg, pc * 2 + parity), device_id_type=mesh_id)
-
-    def go_swap(d, c):
-        swap(d).start()
-        return c
-
-    def go_column(i, c):
-        pc = lax.rem(column + i, pairs)
-        swap(i).wait_recv()
-        sums[pc] = part_ref[pc, parity] + half[pc]
-
-        def go(d, c):
-            to_owner(d).start()
-            return c
-
-        return lax.fori_loop(jnp.maximum(i * groups, 1), (i + 1) * groups, go, c)
-
-    lax.fori_loop(0, pairs, go_swap, 0)
-    lax.fori_loop(0, pairs, go_column, 0)
-
+    kept = pltpu.make_async_copy(part_ref.at[:, parity], keep, keep_sem)
+    kept.start()
     first_row = (p * groups + g) * rows
     mine = p // pairs
     line = lax.broadcasted_iota(jnp.int32, halves.shape[1:], 0)
@@ -352,8 +329,41 @@
     ray = lax.rem(first_row, NTILE) * RAYS_TILE + mine * (lines * 8) + ray_at(line, lane, tall)
     ray = (ray.astype(jnp.float32) + (0.5 - RAYS * 0.5)) * (1.0 / spread)
     a = first_row // NTILE
-    halves[mine] = ray_sums(
+    early, rest = ray_sums(
         halves.shape[1:], table_ref[subset, 0, a], table_ref[subset, 1, a], table_ref[subset, 2, a], ray)
+    pl.semaphore_wait(barrier, n)
+
+    def swap(d):
+        pc = lax.rem(column + d, pairs)
+        return pltpu.make_async_remote_copy(
+            src_ref=part_ref.at[pc, 1 - parity], dst_ref=half.at[pc], send_sem=pair_send.at[d],
+            recv_sem=pair_recv.at[d], device_id=partner, device_id_type=mesh_id)
+
+    def to_owner(d):
+        pc, pg = peer(d)
+        return pltpu.make_async_remote_copy(
+            src_ref=sums.at[pc, pg], dst_ref=inbox.at[column, g], send_sem=send_sem.at[d],
+            recv_sem=recv_sem.at[d], device_id=(pg, pc * 2 + parity), device_id_type=mesh_id)
+
+    def go_swap(d, c):
+        swap(d).start()
+        return c
+
+    def go_column(i, c):
+        pc = lax.rem(column + i, pairs)
+        swap(i).wait_recv()
+        sums[pc] = (keep[pc] + half[pc]).astype(sums.dtype)
+
+        def go(d, c):
+            to_owner(d).start()
+            return c
+
+        return lax.fori_loop(jnp.maximum(i * groups, 1), (i + 1) * groups, go, c)
+
+    lax.fori_loop(0, pairs, go_swap, 0)
+    kept.wait()
+    lax.fori_loop(0, pairs, go_column, 0)
+    halves[mine] = rest(early)
     trade = pltpu.make_async_remote_copy(
         src_ref=halves.at[mine], dst_ref=halves.at[mine], send_sem=rs_send, recv_sem=rs_recv,
         device_id=(g, lax.rem(p + pairs, 2 * pairs)), device_id_type=mesh_id)
@@ -390,7 +400,7 @@
     total = jnp.zeros(stage.shape, jnp.float32)
     for i in range(pairs):
         for j in range(groups):
-            total = total + inbox[i, j]
+            total = total + inbox[i, j].astype(jnp.float32)
     ray = ray_at(lax.broadcasted_iota(jnp.int32, stage.shape, 0),
                  lax.broadcasted_iota(jnp.int32, stage.shape, 1), tall)
     row = ray // RAYS_TILE
@@ -448,8 +458,6 @@
     lax.fori_loop(0, n, finish, 0)
     lax.fori_loop(1, n, sent, 0)
     lax.fori_loop(0, pairs, swapped, 0)
-    for i in range(pairs):
-        full_ref[i] = gathered[i].astype(jnp.float32)
 
 
 def exchange(subset, tall, partial, live, table, measured, rows, groups, patches):
@@ -457,24 +465,25 @@
     lines = rows * measured.shape[2] // LANES
     shape = (pairs, 2, groups, lines, LANES)
     n = pairs * groups
+    wire = jnp.bfloat16 if subset < SUBSETS - 1 else jnp.float32
     dma = pltpu.SemaphoreType.DMA
     vmem = pl.BlockSpec(memory_space=pltpu.VMEM)
     full, own = pl.pallas_call(
         lambda *refs: exchange_kernel(subset, tall, *refs),
-        in_specs=[vmem, smem(), smem(), pl.BlockSpec(memory_space=pl.ANY)],
+        in_specs=[pl.BlockSpec(memory_space=pl.ANY), smem(), smem(), pl.BlockSpec(memory_space=pl.ANY)],
         out_specs=[vmem] * 2,
-        out_shape=[jax.ShapeDtypeStruct(shape, jnp.float32),
+        out_shape=[jax.ShapeDtypeStruct(shape, jnp.bfloat16),
                    jax.ShapeDtypeStruct((rows, measured.shape[2]), jnp.float32)],
         scratch_shapes=[pltpu.VMEM((pairs, groups, lines, LANES), jnp.float32),
                         pltpu.VMEM((pairs, groups, lines, LANES), jnp.float32),
-                        pltpu.VMEM((pairs, groups, lines, LANES), jnp.float32),
+                        pltpu.VMEM((pairs, groups, lines, LANES), wire),
+                        pltpu.VMEM((pairs, groups, lines, LANES), wire),
                         pltpu.VMEM((lines, LANES), jnp.float32),
                         pltpu.VMEM((SPAN, LANES), jnp.float32),
                         pltpu.VMEM((2, lines // 2, LANES), jnp.float32),
                         pltpu.VMEM((rows, measured.shape[2]), jnp.float32),
                         pltpu.VMEM((lines, LANES), jnp.bfloat16),
-                        pltpu.VMEM(shape, jnp.bfloat16),
-                        dma, dma((pairs,)), dma((pairs,)), dma((n,)), dma((n,)), dma, dma,
+                        dma, dma, dma((pairs,)), dma((pairs,)), dma((n,)), dma((n,)), dma, dma,
                         dma((n,)), dma((n,)), dma((n,)), dma((n,))],
         compiler_params=pltpu.CompilerParams(collective_id=subset, has_side_effects=True),
         name="exchange",
@@ -524,6 +533,7 @@
         out_shape=[jax.ShapeDtypeStruct(volume.shape, jnp.float32),
                    jax.ShapeDtypeStruct(own.shape, jnp.float32)],
         scratch_shapes=[pltpu.VMEM((ANG_SUB * R, VOX), jnp.float32),
+                        pltpu.VMEM(residual.shape, jnp.float32),
                         pltpu.VMEM((ANG_SUB * TALL, LANES), jnp.float32),
                         pltpu.VMEM((ANG_SUB * RAYS, LANES), jnp.float32),
                         pltpu.SMEM((ANG_SUB * TILES + 1,), jnp.int32),

time: 147 us -> 142 us (0.966)
  Pallas kernels: 145 us -> 139 us
    pallas_call x2, Pallas kernels: 56.8 us -> 51.5 us  [exchange(): pl.pallas_call(lambda *refs: exchange_kernel(subset, tall, *refs), in_spe...]
where the time goes in v4:
time: 142 us; the launch traced here: 140 us
  Pallas kernels  139 us (98%)
    pallas_call x2, Pallas kernels, exchange(): pl.pallas_call(lambda *refs: exchange_kernel(subset, tall, *refs), in_spe...  51.5 us
    pallas_call x2, Pallas kernels, backward(): pl.pallas_call(lambda *refs: backward_kernel(nb, subset, first, tall, *re...  43.2 us
    pallas_call x2, Pallas kernels, forward(): pl.pallas_call(lambda *refs: forward_kernel(nb, subset, first, tall, *ref...  43.1 us

profile of v4, /device:TPU:1, one launch (start us, length us, event | category | flops | bytes accessed | tf_op | source)
XLA Modules:
  0.0 139.9 jit_solution(8649392276664132143)
XLA Ops:
  0.6 1.4 %placing.1 = (s32[2,8,128]{2,1,0:T(8,128)}, f32[2,8,128]{2,1,0:T(8,128)}, s32[1,384]{1,0:T(1,128)}) custom-call(s32[1,128]{1,0:T(1,128)} %bitcast.11), custom_call_target="tpu_custom_call" | custom-call | tf_op jit(solution)/shard_map/placing/pallas_call | solution.py:585
  2.1 21.5 %forward.2 = f32[1536,128]{1,0:T(8,128)} custom-call(s32[2,8,128]{2,1,0:T(8,128)} %get-tuple-element.12.refs_0_, f32[2,8,128]{2,1,0:T(8,128)} %get-tuple-element.13.refs_1_, s32[1,384]{1,0:T(1,128)} %get-tuple-element.14.refs_2_, f32[128,8,1024]{2,1,0:T(8,128)} %refs_3_.6, f32[1024,128]{1,0:T(8,128)} %constant.10.clone.refs_4_), custom_call_target="tpu_custom_call" | custom-call | tf_op jit(solution)/shard_map/forward/pallas_call | solution.py:503
  23.5 24.6 %exchange.2 = (bf16[4,2,4,48,128]{4,3,2,1,0:T(8,128)(2,1)}, f32[16,384]{1,0:T(8,128)}) custom-call(f32[4,2,4,48,128]{4,3,2,1,0:T(8,128)} %bitcast.7, s32[2,512]{1,0:T(2,128)} %refs_1_.3, f32[2,3,8]{2,1,0:T(4,128)} %constant.11.clone.refs_2_, f32[2,64,384]{2,1,0:T(8,128)} %refs_3_.7), custom_call_target="tpu_custom_call" | custom-call | tf_op jit(solution)/shard_map/exchange/pallas_call | solution.py:471
  48.1 21.5 %backward.2 = (f32[128,8,1024]{2,1,0:T(8,128)}, f32[16,384]{1,0:T(8,128)}) custom-call(s32[2,8,128]{2,1,0:T(8,128)} %get-tuple-element.12.refs_0_, f32[2,8,128]{2,1,0:T(8,128)} %get-tuple-element.13.refs_1_, s32[1,384]{1,0:T(1,128)} %get-tuple-element.14.refs_2_, f32[128,8,1024]{2,1,0:T(8,128)} %refs_3_.6, f32[8,1024]{1,0:T(8,128)} %constant.12.clone.refs_4_, ...), custom_call_target="tpu_custom_call" | custom-call | tf_op jit(solution)/shard_map/backward/pallas_call | solution.py:523
  69.6 21.6 %forward.3 = f32[1536,128]{1,0:T(8,128)} custom-call(s32[2,8,128]{2,1,0:T(8,128)} %get-tuple-element.12.refs_0_, f32[2,8,128]{2,1,0:T(8,128)} %get-tuple-element.13.refs_1_, s32[1,384]{1,0:T(1,128)} %get-tuple-element.14.refs_2_, f32[128,8,1024]{2,1,0:T(8,128)} %get-tuple-element.17.refs_3_, f32[1024,128]{1,0:T(8,128)} %constant.13.clone.refs_4_), custom_call_target="tpu_custom_call" | custom-call | tf_op jit(solution)/shard_map/forward/pallas_call | solution.py:503
  91.3 26.9 %exchange.3 = (bf16[4,2,4,48,128]{4,3,2,1,0:T(8,128)(2,1)}, f32[16,384]{1,0:T(8,128)}) custom-call(f32[4,2,4,48,128]{4,3,2,1,0:T(8,128)} %bitcast.6, s32[2,512]{1,0:T(2,128)} %refs_1_.3, f32[2,3,8]{2,1,0:T(4,128)} %constant.11.clone.refs_2_, f32[2,64,384]{2,1,0:T(8,128)} %refs_3_.7), custom_call_target="tpu_custom_call" | custom-call | tf_op jit(solution)/shard_map/exchange/pallas_call | solution.py:471
  118.2 21.7 %backward.3 = (f32[128,8,1024]{2,1,0:T(8,128)}, f32[16,384]{1,0:T(8,128)}) custom-call(s32[2,8,128]{2,1,0:T(8,128)} %get-tuple-element.12.refs_0_, f32[2,8,128]{2,1,0:T(8,128)} %get-tuple-element.13.refs_1_, s32[1,384]{1,0:T(1,128)} %get-tuple-element.14.refs_2_, f32[128,8,1024]{2,1,0:T(8,128)} %get-tuple-element.17.refs_3_, ...), custom_call_target="tpu_custom_call" | custom-call | tf_op jit(solution)/shard_map/backward/pallas_call | solution.py:523

commit v5 on v4

--- a/solution.py
+++ b/solution.py
@@ -25,6 +25,8 @@
 RAYS = NTILE * RAYS_TILE
 LANES = 128
 PAD = 32
+CHUNK = 32
+DEPTH = 2
 EARLY = 3
 SPAN = 128
 TALL = RAYS + SPAN
@@ -66,7 +68,7 @@
 TILES = RAYS // SPAN
 
 
-WIDE = 4
+WIDE = 16
 
 
 def list_tiles(subset, win_ref, tiles, starts):
@@ -142,20 +144,31 @@
     return pl.multiple_of(x, m)
 
 
-def forward_kernel(nb, subset, first, tall, lo_ref, frac_ref, win_ref, vol_ref, grid_ref, out_ref,
-                   tot, acc, tiles, starts):
-    step = pl.program_id(0)
-
-    @pl.when(step == 0)
-    def _():
-        zero = jnp.zeros((2 * SPAN, LANES), jnp.float32)
-
-        list_tiles(subset, win_ref, tiles, starts)
-
-        def clear(t, at):
-            acc[pl.ds(aligned(at // TILES * TALL + lax.rem(at, TILES) * SPAN, SPAN), 2 * SPAN), :] = zero
-
-        over_tiles(tiles, starts, clear)
+def chunk_of(ref, c):
+    return ref.at[pl.ds(c * CHUNK, CHUNK)]
+
+
+def forward_kernel(subset, first, tall, lo_ref, frac_ref, win_ref, vol_hbm, grid_hbm, out_ref,
+                   vol_ref, grid_ref, tot, acc, tiles, starts, grid_sem, vol_sem):
+    chunks = vol_ref.shape[0] // CHUNK
+
+    def fetch(c):
+        return pltpu.make_async_copy(chunk_of(vol_hbm, c), chunk_of(vol_ref, c), vol_sem.at[c])
+
+    grid_copy = pltpu.make_async_copy(grid_hbm, grid_ref, grid_sem)
+    grid_copy.start()
+    for c in range(min(DEPTH, chunks)):
+        fetch(c).start()
+
+    zero = jnp.zeros((2 * SPAN, LANES), jnp.float32)
+    list_tiles(subset, win_ref, tiles, starts)
+
+    def clear(t, at):
+        acc[pl.ds(aligned(at // TILES * TALL + lax.rem(at, TILES) * SPAN, SPAN), 2 * SPAN), :] = zero
+
+    over_tiles(tiles, starts, clear)
+    out_ref[...] = jnp.zeros_like(out_ref)
+    grid_copy.wait()
 
     width = SUB * BLK_SIDE
     group = BLK_SIDE // SUB
@@ -163,8 +176,18 @@
     col_group = (lax.broadcasted_iota(jnp.int32, (group * slices, width), 1) % BLK_SIDE) // SUB
     mine = col_group == lax.broadcasted_iota(jnp.int32, (group * slices, width), 0) // slices
     angle = lax.broadcasted_iota(jnp.int32, (1, LANES), 1) // R
-    for i in range(nb):
-        b = step * nb + i
+    def chunk(c, carry):
+        fetch(c).wait()
+
+        @pl.when(c + DEPTH < chunks)
+        def _():
+            fetch(c + DEPTH).start()
+
+        for i in range(CHUNK):
+            block(c * CHUNK + i)
+        return carry
+
+    def block(b):
         frac = jnp.zeros((1, LANES), jnp.float32)
         for a in range(ANG_SUB):
             frac = jnp.where(angle == a, frac_ref[subset, a, b], frac)
@@ -172,72 +195,76 @@
         for g in range(group):
             at = slice(g * width, (g + 1) * width)
             f = footprint(grid_ref[at, :] + frac)
-            wide = jnp.where(mine, jnp.tile(vol_ref[i, :, at], (group, 1)), 0.0)
+            wide = jnp.where(mine, jnp.tile(vol_ref[b, :, at], (group, 1)), 0.0)
             parts.append(jnp.dot(wide.astype(jnp.bfloat16), f, preferred_element_type=jnp.float32))
         part = jnp.transpose(jnp.concatenate(parts, axis=0))
         for a in range(ANG_SUB):
             at = pl.ds(a * TALL + PAD + lo_ref[subset, a, b], R)
             acc[at, :] += part[a * R:(a + 1) * R, :]
 
-    @pl.when(step == pl.num_programs(0) - 1)
-    def _():
-        out_ref[...] = jnp.zeros_like(out_ref)
-        lane_q = lax.broadcasted_iota(jnp.int32, (1, LANES), 1) // 8
-
-        for a in range(ANG_SUB):
-            def merge(t, i, a=a):
-                base = aligned(a * TALL + PAD + i * SPAN, 32)
-                tot[pl.ds(aligned(t * SPAN, SPAN), SPAN), :] = shifted(
-                    acc, base, [-int(o) for o in first[a]], lane_q)
-
-            over_angle(a, tiles, starts, merge)
-
-        def fold(t, at):
-            rows = [tot[sixteenth(aligned(t * SPAN, SPAN), r, tall), :] for r in range(16)]
-            for half in (1, 2, 4, 8):
-                low = lane_q % (2 * half) < half
-                rows = [jnp.where(low, x, y) + pltpu.roll(jnp.where(low, y, x), half * 8, 1)
-                        for x, y in zip(rows[0::2], rows[1::2])]
-            out_ref[pl.ds(aligned(at * 8, 8), 8), :] = rows[0]
-
-        over_tiles(tiles, starts, fold)
-
-
-def backward_kernel(nb, subset, first, tall, lo_ref, frac_ref, win_ref, vol_ref, base_ref, res_ref, own_ref, out_ref, last_ref,
-                    e_scr, res, rb, dd, tiles, starts):
-    step = pl.program_id(0)
-
-    @pl.when(step == 0)
-    def _():
-        fill_grid(base_ref, e_scr)
-        lane_q = lax.broadcasted_iota(jnp.int32, (1, LANES), 1) // 8
-        last_ref[...] = own_ref[...]
-        res[...] = res_ref[...].astype(jnp.float32)
-        list_tiles(subset, win_ref, tiles, starts)
-
-        def widen(t, at):
-            rows = spread_lanes(res[pl.ds(aligned(at * 8, 8), 8), :], lane_q)
-            base = aligned(at // TILES * TALL + PAD + lax.rem(at, TILES) * SPAN, 32)
-            for r in range(16):
-                rb[sixteenth(base, r, tall), :] = rows[r]
-
-        over_tiles(tiles, starts, widen)
-
-        for a in range(ANG_SUB):
-            def shift(t, i, a=a):
-                base = aligned(a * TALL + PAD + i * SPAN, 32)
-                dd[pl.ds(aligned(a * RAYS + i * SPAN, SPAN), SPAN), :] = shifted(
-                    rb, base, [int(o) for o in first[a]], lane_q)
-
-            over_angle(a, tiles, starts, shift)
+    lax.fori_loop(0, chunks, chunk, 0)
+    lane_q = lax.broadcasted_iota(jnp.int32, (1, LANES), 1) // 8
+
+    for a in range(ANG_SUB):
+        def merge(t, i, a=a):
+            base = aligned(a * TALL + PAD + i * SPAN, 32)
+            tot[pl.ds(aligned(t * SPAN, SPAN), SPAN), :] = shifted(
+                acc, base, [-int(o) for o in first[a]], lane_q)
+
+        over_angle(a, tiles, starts, merge)
+
+    def fold(t, at):
+        rows = [tot[sixteenth(aligned(t * SPAN, SPAN), r, tall), :] for r in range(16)]
+        for half in (1, 2, 4, 8):
+            low = lane_q % (2 * half) < half
+            rows = [jnp.where(low, x, y) + pltpu.roll(jnp.where(low, y, x), half * 8, 1)
+                    for x, y in zip(rows[0::2], rows[1::2])]
+        out_ref[pl.ds(aligned(at * 8, 8), 8), :] = rows[0]
+
+    over_tiles(tiles, starts, fold)
+
+
+def backward_kernel(subset, first, tall, lo_ref, frac_ref, win_ref, vol_hbm, base_ref, res_ref, own_ref,
+                    out_hbm, last_ref,
+                    vol_ref, out_ref, e_scr, res, rb, dd, tiles, starts, vol_sem, out_sem):
+    chunks = vol_ref.shape[0] // CHUNK
+
+    def fetch(c):
+        return pltpu.make_async_copy(chunk_of(vol_hbm, c), chunk_of(vol_ref, c), vol_sem.at[c])
+
+    def emit(c):
+        return pltpu.make_async_copy(chunk_of(out_ref, c), chunk_of(out_hbm, c), out_sem.at[c])
+
+    for c in range(min(DEPTH, chunks)):
+        fetch(c).start()
+    fill_grid(base_ref, e_scr)
+    lane_q = lax.broadcasted_iota(jnp.int32, (1, LANES), 1) // 8
+    last_ref[...] = own_ref[...]
+    res[...] = res_ref[...].astype(jnp.float32)
+    list_tiles(subset, win_ref, tiles, starts)
+
+    def widen(t, at):
+        rows = spread_lanes(res[pl.ds(aligned(at * 8, 8), 8), :], lane_q)
+        base = aligned(at // TILES * TALL + PAD + lax.rem(at, TILES) * SPAN, 32)
+        for r in range(16):
+            rb[sixteenth(base, r, tall), :] = rows[r]
+
+    over_tiles(tiles, starts, widen)
+
+    for a in range(ANG_SUB):
+        def shift(t, i, a=a):
+            base = aligned(a * TALL + PAD + i * SPAN, 32)
+            dd[pl.ds(aligned(a * RAYS + i * SPAN, SPAN), SPAN), :] = shifted(
+                rb, base, [int(o) for o in first[a]], lane_q)
+
+        over_angle(a, tiles, starts, shift)
 
     width = SUB * BLK_SIDE
     group = BLK_SIDE // SUB
     lane = lax.broadcasted_iota(jnp.int32, (8, width), 1)
     col_group = (lane % BLK_SIDE) // SUB
 
-    for i in range(nb):
-        b = step * nb + i
+    def block(b):
         rows = jnp.concatenate(
             [dd[pl.ds(a * RAYS + lo_ref[subset, a, b], R), :] for a in range(ANG_SUB)], axis=0)
         turned = jnp.transpose(rows)
@@ -252,7 +279,23 @@
             for j in range(1, group):
                 back = jnp.where(col_group == j, part[j * 8:(j + 1) * 8], back)
             col_sum = part[32:40]
-            out_ref[i, :, at] = jnp.maximum(vol_ref[i, :, at] + relax * back / col_sum, 0.0)
+            out_ref[b, :, at] = jnp.maximum(vol_ref[b, :, at] + relax * back / col_sum, 0.0)
+
+    def chunk(c, carry):
+        fetch(c).wait()
+
+        @pl.when(c + DEPTH < chunks)
+        def _():
+            fetch(c + DEPTH).start()
+
+        for i in range(CHUNK):
+            block(c * CHUNK + i)
+        emit(c).start()
+        return carry
+
+    lax.fori_loop(0, chunks, chunk, 0)
+    for c in range(chunks):
+        emit(c).wait()
 
 
 def ray_sums(shape, big, small, inv, ray):
@@ -496,48 +539,49 @@
 
 
 def forward(subset, tall, volume, lo, frac, win, base, first):
-    blocks, slices, _ = volume.shape
-    nb = 8
+    blocks = volume.shape[0]
     lines = ANG_SUB * RAYS // 16
     grid = (np.repeat(base, R, axis=0) - np.tile(np.arange(R), ANG_SUB)[:, None]) * (1.0 / spread)
+    vmem = pl.BlockSpec(memory_space=pltpu.VMEM)
+    hbm = pl.BlockSpec(memory_space=pl.ANY)
+    dma = pltpu.SemaphoreType.DMA
     return pl.pallas_call(
-        lambda *refs: forward_kernel(nb, subset, first, tall, *refs),
-        grid=(blocks // nb,),
-        in_specs=[smem(), smem(), smem(),
-                  pl.BlockSpec((nb, slices, VOX), lambda i: (i, 0, 0)),
-                  pl.BlockSpec((VOX, LANES), lambda i: (0, 0))],
-        out_specs=pl.BlockSpec((lines, LANES), lambda i: (0, 0)),
+        lambda *refs: forward_kernel(subset, first, tall, *refs),
+        in_specs=[smem(), smem(), smem(), hbm, hbm],
+        out_specs=vmem,
         out_shape=jax.ShapeDtypeStruct((lines, LANES), jnp.float32),
-        scratch_shapes=[pltpu.VMEM((ANG_SUB * RAYS, LANES), jnp.float32),
+        scratch_shapes=[pltpu.VMEM(volume.shape, jnp.float32),
+                        pltpu.VMEM((VOX, LANES), jnp.float32),
+                        pltpu.VMEM((ANG_SUB * RAYS, LANES), jnp.float32),
                         pltpu.VMEM((ANG_SUB * TALL, LANES), jnp.float32),
                         pltpu.SMEM((ANG_SUB * TILES + 1,), jnp.int32),
-                        pltpu.SMEM((ANG_SUB + 1,), jnp.int32)],
+                        pltpu.SMEM((ANG_SUB + 1,), jnp.int32),
+                        dma, dma((blocks // CHUNK,))],
         compiler_params=pltpu.CompilerParams(vmem_limit_bytes=VMEM_LIMIT),
         name="forward",
     )(lo, frac, win, volume, grid.T.astype(np.float32))
 
 
 def backward(subset, tall, volume, residual, own, lo, frac, win, base, first):
-    blocks, slices, _ = volume.shape
-    nb = 8
+    blocks = volume.shape[0]
+    vmem = pl.BlockSpec(memory_space=pltpu.VMEM)
+    hbm = pl.BlockSpec(memory_space=pl.ANY)
+    dma = pltpu.SemaphoreType.DMA
     return pl.pallas_call(
-        lambda *refs: backward_kernel(nb, subset, first, tall, *refs),
-        grid=(blocks // nb,),
-        in_specs=[smem(), smem(), smem(),
-                  pl.BlockSpec((nb, slices, VOX), lambda i: (i, 0, 0)),
-                  pl.BlockSpec((ANG_SUB, VOX), lambda i: (0, 0)),
-                  pl.BlockSpec(residual.shape, lambda i: (0, 0)),
-                  pl.BlockSpec(own.shape, lambda i: (0, 0))],
-        out_specs=[pl.BlockSpec((nb, slices, VOX), lambda i: (i, 0, 0)),
-                   pl.BlockSpec(own.shape, lambda i: (0, 0))],
+        lambda *refs: backward_kernel(subset, first, tall, *refs),
+        in_specs=[smem(), smem(), smem(), hbm, vmem, vmem, vmem],
+        out_specs=[hbm, vmem],
         out_shape=[jax.ShapeDtypeStruct(volume.shape, jnp.float32),
                    jax.ShapeDtypeStruct(own.shape, jnp.float32)],
-        scratch_shapes=[pltpu.VMEM((ANG_SUB * R, VOX), jnp.float32),
+        scratch_shapes=[pltpu.VMEM(volume.shape, jnp.float32),
+                        pltpu.VMEM(volume.shape, jnp.float32),
+                        pltpu.VMEM((ANG_SUB * R, VOX), jnp.float32),
                         pltpu.VMEM(residual.shape, jnp.float32),
                         pltpu.VMEM((ANG_SUB * TALL, LANES), jnp.float32),
                         pltpu.VMEM((ANG_SUB * RAYS, LANES), jnp.float32),
                         pltpu.SMEM((ANG_SUB * TILES + 1,), jnp.int32),
-                        pltpu.SMEM((ANG_SUB + 1,), jnp.int32)],
+                        pltpu.SMEM((ANG_SUB + 1,), jnp.int32),
+                        dma((blocks // CHUNK,)), dma((blocks // CHUNK,))],
         compiler_params=pltpu.CompilerParams(vmem_limit_bytes=VMEM_LIMIT),
         name="backward",
     )(lo, frac, win, volume, base, residual, own)

time: 142 us -> 117 us (0.82); the launches traced: 140 us -> 117 us
  Pallas kernels: 139 us -> 116 us
    pallas_call x4, Pallas kernels: 86.3 us -> 64.4 us  [the longest x2 32.3 us: backward(): pl.pallas_call(lambda *refs: backward_kernel(subset, first, tall, *refs),...]
where the time goes in v5:
time: 117 us
  Pallas kernels  116 us (99%)
    pallas_call x2, Pallas kernels, exchange(): pl.pallas_call(lambda *refs: exchange_kernel(subset, tall, *refs), in_spe...  50.6 us
    pallas_call x2, Pallas kernels, backward(): pl.pallas_call(lambda *refs: backward_kernel(subset, first, tall, *refs),...  32.3 us
    pallas_call x2, Pallas kernels, forward(): pl.pallas_call(lambda *refs: forward_kernel(subset, first, tall, *refs),...  32.1 us

profile of v5, /device:TPU:1, one launch (start us, length us, event | category | flops | bytes accessed | tf_op | source)
XLA Modules:
  0.0 117.2 jit_solution(10756885512277545138)
XLA Ops:
  0.6 1.4 %placing.1 = (s32[2,8,128]{2,1,0:T(8,128)}, f32[2,8,128]{2,1,0:T(8,128)}, s32[1,384]{1,0:T(1,128)}) custom-call(s32[1,128]{1,0:T(1,128)} %bitcast.11), custom_call_target="tpu_custom_call" | custom-call | tf_op jit(solution)/shard_map/placing/pallas_call | solution.py:629
  2.1 15.9 %forward.2 = f32[1536,128]{1,0:T(8,128)} custom-call(s32[2,8,128]{2,1,0:T(8,128)} %get-tuple-element.12.refs_0_, f32[2,8,128]{2,1,0:T(8,128)} %get-tuple-element.13.refs_1_, s32[1,384]{1,0:T(1,128)} %get-tuple-element.14.refs_2_, f32[128,8,1024]{2,1,0:T(8,128)} %refs_3_.6, f32[1024,128]{1,0:T(8,128)} %constant.10.clone.refs_4_), custom_call_target="tpu_custom_call" | custom-call | tf_op jit(solution)/shard_map/forward/pallas_call | solution.py:548
  18.0 24.7 %exchange.2 = (bf16[4,2,4,48,128]{4,3,2,1,0:T(8,128)(2,1)}, f32[16,384]{1,0:T(8,128)}) custom-call(f32[4,2,4,48,128]{4,3,2,1,0:T(8,128)} %bitcast.7, s32[2,512]{1,0:T(2,128)} %refs_1_.3, f32[2,3,8]{2,1,0:T(4,128)} %constant.11.clone.refs_2_, f32[2,64,384]{2,1,0:T(8,128)} %refs_3_.7), custom_call_target="tpu_custom_call" | custom-call | tf_op jit(solution)/shard_map/exchange/pallas_call | solution.py:514
  42.7 16.1 %backward.2 = (f32[128,8,1024]{2,1,0:T(8,128)}, f32[16,384]{1,0:T(8,128)}) custom-call(s32[2,8,128]{2,1,0:T(8,128)} %get-tuple-element.12.refs_0_, f32[2,8,128]{2,1,0:T(8,128)} %get-tuple-element.13.refs_1_, s32[1,384]{1,0:T(1,128)} %get-tuple-element.14.refs_2_, f32[128,8,1024]{2,1,0:T(8,128)} %refs_3_.6, f32[8,1024]{1,0:T(8,128)} %constant.12.clone.refs_4_, ...), custom_call_target="tpu_custom_call" | custom-call | tf_op jit(solution)/shard_map/backward/pallas_call | solution.py:570
  58.8 16.2 %forward.3 = f32[1536,128]{1,0:T(8,128)} custom-call(s32[2,8,128]{2,1,0:T(8,128)} %get-tuple-element.12.refs_0_, f32[2,8,128]{2,1,0:T(8,128)} %get-tuple-element.13.refs_1_, s32[1,384]{1,0:T(1,128)} %get-tuple-element.14.refs_2_, f32[128,8,1024]{2,1,0:T(8,128)} %get-tuple-element.17.refs_3_, f32[1024,128]{1,0:T(8,128)} %constant.13.clone.refs_4_), custom_call_target="tpu_custom_call" | custom-call | tf_op jit(solution)/shard_map/forward/pallas_call | solution.py:548
  75.0 25.9 %exchange.3 = (bf16[4,2,4,48,128]{4,3,2,1,0:T(8,128)(2,1)}, f32[16,384]{1,0:T(8,128)}) custom-call(f32[4,2,4,48,128]{4,3,2,1,0:T(8,128)} %bitcast.6, s32[2,512]{1,0:T(2,128)} %refs_1_.3, f32[2,3,8]{2,1,0:T(4,128)} %constant.11.clone.refs_2_, f32[2,64,384]{2,1,0:T(8,128)} %refs_3_.7), custom_call_target="tpu_custom_call" | custom-call | tf_op jit(solution)/shard_map/exchange/pallas_call | solution.py:514
  100.9 16.2 %backward.3 = (f32[128,8,1024]{2,1,0:T(8,128)}, f32[16,384]{1,0:T(8,128)}) custom-call(s32[2,8,128]{2,1,0:T(8,128)} %get-tuple-element.12.refs_0_, f32[2,8,128]{2,1,0:T(8,128)} %get-tuple-element.13.refs_1_, s32[1,384]{1,0:T(1,128)} %get-tuple-element.14.refs_2_, f32[128,8,1024]{2,1,0:T(8,128)} %get-tuple-element.17.refs_3_, ...), custom_call_target="tpu_custom_call" | custom-call | tf_op jit(solution)/shard_map/backward/pallas_call | solution.py:570

commit v6 on v5

--- a/solution.py
+++ b/solution.py
@@ -26,6 +26,8 @@
 LANES = 128
 PAD = 32
 CHUNK = 32
+MADE = 4
+MADE_EARLY = (3, 8)
 DEPTH = 2
 EARLY = 3
 SPAN = 128
@@ -144,13 +146,18 @@
     return pl.multiple_of(x, m)
 
 
+def size_of(ref):
+    return min(CHUNK, ref.shape[0] // 2)
+
+
 def chunk_of(ref, c):
-    return ref.at[pl.ds(c * CHUNK, CHUNK)]
+    return ref.at[pl.ds(c * size_of(ref), size_of(ref))]
 
 
 def forward_kernel(subset, first, tall, lo_ref, frac_ref, win_ref, vol_hbm, grid_hbm, out_ref,
                    vol_ref, grid_ref, tot, acc, tiles, starts, grid_sem, vol_sem):
-    chunks = vol_ref.shape[0] // CHUNK
+    size = size_of(vol_ref)
+    chunks = vol_ref.shape[0] // size
 
     def fetch(c):
         return pltpu.make_async_copy(chunk_of(vol_hbm, c), chunk_of(vol_ref, c), vol_sem.at[c])
@@ -183,8 +190,8 @@
         def _():
             fetch(c + DEPTH).start()
 
-        for i in range(CHUNK):
-            block(c * CHUNK + i)
+        for i in range(size):
+            block(c * size + i)
         return carry
 
     def block(b):
@@ -224,10 +231,11 @@
     over_tiles(tiles, starts, fold)
 
 
-def backward_kernel(subset, first, tall, lo_ref, frac_ref, win_ref, vol_hbm, base_ref, res_ref, own_ref,
+def backward_kernel(subset, first, tall, lo_ref, frac_ref, win_ref, vol_hbm, made_hbm, base_ref, res_ref, own_ref,
                     out_hbm, last_ref,
-                    vol_ref, out_ref, e_scr, res, rb, dd, tiles, starts, vol_sem, out_sem):
-    chunks = vol_ref.shape[0] // CHUNK
+                    vol_ref, out_ref, made, e_scr, res, rb, dd, tiles, starts, vol_sem, out_sem, made_sem):
+    size = size_of(vol_ref)
+    chunks = vol_ref.shape[0] // size
 
     def fetch(c):
         return pltpu.make_async_copy(chunk_of(vol_hbm, c), chunk_of(vol_ref, c), vol_sem.at[c])
@@ -235,8 +243,14 @@
     def emit(c):
         return pltpu.make_async_copy(chunk_of(out_ref, c), chunk_of(out_hbm, c), out_sem.at[c])
 
+    def load(c):
+        at = pl.ds(c * MADE, MADE)
+        return pltpu.make_async_copy(made_hbm.at[at], made.at[at], made_sem.at[c])
+
     for c in range(min(DEPTH, chunks)):
         fetch(c).start()
+    for c in range(made.shape[0] // MADE):
+        load(c).start()
     fill_grid(base_ref, e_scr)
     lane_q = lax.broadcasted_iota(jnp.int32, (1, LANES), 1) // 8
     last_ref[...] = own_ref[...]
@@ -264,7 +278,7 @@
     lane = lax.broadcasted_iota(jnp.int32, (8, width), 1)
     col_group = (lane % BLK_SIDE) // SUB
 
-    def block(b):
+    def block(b, ready):
         rows = jnp.concatenate(
             [dd[pl.ds(a * RAYS + lo_ref[subset, a, b], R), :] for a in range(ANG_SUB)], axis=0)
         turned = jnp.transpose(rows)
@@ -272,8 +286,11 @@
         for g in range(group):
             lhs = jnp.concatenate([turned[g * 32:(g + 1) * 32], ones], axis=0).astype(jnp.bfloat16)
             at = slice(g * width, (g + 1) * width)
-            f = jnp.concatenate(
-                [footprint(e_scr[a * R:(a + 1) * R, at] + frac_ref[subset, a, b]) for a in range(ANG_SUB)], axis=0)
+            if ready:
+                f = made[b - made.shape[0], :, at]
+            else:
+                f = jnp.concatenate([footprint(e_scr[a * R:(a + 1) * R, at] + frac_ref[subset, a, b])
+                                     for a in range(ANG_SUB)], axis=0)
             part = jnp.dot(lhs, f, preferred_element_type=jnp.float32)
             back = part[0:8]
             for j in range(1, group):
@@ -281,19 +298,22 @@
             col_sum = part[32:40]
             out_ref[b, :, at] = jnp.maximum(vol_ref[b, :, at] + relax * back / col_sum, 0.0)
 
-    def chunk(c, carry):
+    def chunk(c, carry, ready):
         fetch(c).wait()
 
         @pl.when(c + DEPTH < chunks)
         def _():
             fetch(c + DEPTH).start()
 
-        for i in range(CHUNK):
-            block(c * CHUNK + i)
+        for i in range(size):
+            block(c * size + i, ready)
         emit(c).start()
         return carry
 
-    lax.fori_loop(0, chunks, chunk, 0)
+    lax.fori_loop(0, chunks // 2, lambda c, carry: chunk(c, carry, False), 0)
+    for c in range(made.shape[0] // MADE):
+        load(c).wait()
+    lax.fori_loop(chunks // 2, chunks, lambda c, carry: chunk(c, carry, True), 0)
     for c in range(chunks):
         emit(c).wait()
 
@@ -332,10 +352,10 @@
     return line * 16 + lane // 8
 
 
-def exchange_kernel(subset, tall, part_ref, live_ref, table_ref, meas_ref, gathered, own_ref,
-                    keep, half, inbox, sums, lines_scr, flat, halves, meas, stage,
+def exchange_kernel(subset, tall, part_ref, live_ref, table_ref, frac_ref, meas_ref, base_ref, gathered, own_ref, made_hbm,
+                    keep, half, inbox, sums, lines_scr, flat, halves, meas, stage, e_scr, made,
                     meas_sem, keep_sem, pair_send, pair_recv, send_sem, recv_sem, rs_send, rs_recv,
-                    out_send, out_recv, back_send, back_recv):
+                    out_send, out_recv, back_send, back_recv, made_sem):
     g, p = lax.axis_index("group"), lax.axis_index("patch")
     pairs, groups = inbox.shape[0], inbox.shape[1]
     n = groups * pairs
@@ -374,7 +394,28 @@
     a = first_row // NTILE
     early, rest = ray_sums(
         halves.shape[1:], table_ref[subset, 0, a], table_ref[subset, 1, a], table_ref[subset, 2, a], ray)
+    fill_grid(base_ref, e_scr)
     pl.semaphore_wait(barrier, n)
+
+    def put(i):
+        slot = lax.rem(i, 2)
+        return pltpu.make_async_copy(made.at[slot], made_hbm.at[pl.ds(i * MADE, MADE)], made_sem.at[slot])
+
+    def make(i, c):
+        @pl.when(i >= 2)
+        def _():
+            put(i - 2).wait()
+
+        for k in range(MADE):
+            b = frac_ref.shape[2] // 2 + i * MADE + k
+            for a in range(ANG_SUB):
+                made[lax.rem(i, 2), k, a * R:(a + 1) * R, :] = footprint(
+                    e_scr[a * R:(a + 1) * R, :] + frac_ref[subset, a, b])
+        put(i).start()
+        return c
+
+    steps = made_hbm.shape[0] // MADE
+    early_steps = min(MADE_EARLY[subset], steps)
 
     def swap(d):
         pc = lax.rem(column + d, pairs)
@@ -411,6 +452,8 @@
         src_ref=halves.at[mine], dst_ref=halves.at[mine], send_sem=rs_send, recv_sem=rs_recv,
         device_id=(g, lax.rem(p + pairs, 2 * pairs)), device_id_type=mesh_id)
     trade.start()
+
+    lax.fori_loop(0, early_steps, make, 0)
 
     def got(d, c):
         to_owner(d).wait_recv()
@@ -494,6 +537,7 @@
     lax.fori_loop(1, n, go_all, 0)
     gathered[column, parity, g] = stage[...]
     share(0).start()
+    lax.fori_loop(early_steps, steps, make, 0)
     retile(False)
     for c in range(wide):
         own_ref[:, c * LANES:(c + 1) * LANES] = lines_scr[pl.ds(c, rows, stride=wide), :]
@@ -501,9 +545,11 @@
     lax.fori_loop(0, n, finish, 0)
     lax.fori_loop(1, n, sent, 0)
     lax.fori_loop(0, pairs, swapped, 0)
-
-
-def exchange(subset, tall, partial, live, table, measured, rows, groups, patches):
+    for i in range(max(steps - 2, 0), steps):
+        put(i).wait()
+
+
+def exchange(subset, tall, partial, live, table, frac, measured, base, rows, groups, patches):
     pairs = patches // 2
     lines = rows * measured.shape[2] // LANES
     shape = (pairs, 2, groups, lines, LANES)
@@ -511,12 +557,13 @@
     wire = jnp.bfloat16 if subset < SUBSETS - 1 else jnp.float32
     dma = pltpu.SemaphoreType.DMA
     vmem = pl.BlockSpec(memory_space=pltpu.VMEM)
-    full, own = pl.pallas_call(
+    full, own, made = pl.pallas_call(
         lambda *refs: exchange_kernel(subset, tall, *refs),
-        in_specs=[pl.BlockSpec(memory_space=pl.ANY), smem(), smem(), pl.BlockSpec(memory_space=pl.ANY)],
-        out_specs=[vmem] * 2,
+        in_specs=[pl.BlockSpec(memory_space=pl.ANY), smem(), smem(), smem(), pl.BlockSpec(memory_space=pl.ANY), vmem],
+        out_specs=[vmem, vmem, pl.BlockSpec(memory_space=pl.ANY)],
         out_shape=[jax.ShapeDtypeStruct(shape, jnp.bfloat16),
-                   jax.ShapeDtypeStruct((rows, measured.shape[2]), jnp.float32)],
+                   jax.ShapeDtypeStruct((rows, measured.shape[2]), jnp.float32),
+                   jax.ShapeDtypeStruct((frac.shape[2] // 2, LANES, VOX), jnp.bfloat16)],
         scratch_shapes=[pltpu.VMEM((pairs, groups, lines, LANES), jnp.float32),
                         pltpu.VMEM((pairs, groups, lines, LANES), jnp.float32),
                         pltpu.VMEM((pairs, groups, lines, LANES), wire),
@@ -526,12 +573,14 @@
                         pltpu.VMEM((2, lines // 2, LANES), jnp.float32),
                         pltpu.VMEM((rows, measured.shape[2]), jnp.float32),
                         pltpu.VMEM((lines, LANES), jnp.bfloat16),
+                        pltpu.VMEM((LANES, VOX), jnp.float32),
+                        pltpu.VMEM((2, MADE, LANES, VOX), jnp.bfloat16),
                         dma, dma, dma((pairs,)), dma((pairs,)), dma((n,)), dma((n,)), dma, dma,
-                        dma((n,)), dma((n,)), dma((n,)), dma((n,))],
+                        dma((n,)), dma((n,)), dma((n,)), dma((n,)), dma((2,))],
         compiler_params=pltpu.CompilerParams(collective_id=subset, has_side_effects=True),
         name="exchange",
-    )(partial.reshape(shape), live, table, measured)
-    return full.reshape(partial.shape), own
+    )(partial.reshape(shape), live, table, frac, measured, base)
+    return full.reshape(partial.shape), own, made
 
 
 def smem():
@@ -556,35 +605,37 @@
                         pltpu.VMEM((ANG_SUB * TALL, LANES), jnp.float32),
                         pltpu.SMEM((ANG_SUB * TILES + 1,), jnp.int32),
                         pltpu.SMEM((ANG_SUB + 1,), jnp.int32),
-                        dma, dma((blocks // CHUNK,))],
+                        dma, dma((blocks // min(CHUNK, blocks // 2),))],
         compiler_params=pltpu.CompilerParams(vmem_limit_bytes=VMEM_LIMIT),
         name="forward",
     )(lo, frac, win, volume, grid.T.astype(np.float32))
 
 
-def backward(subset, tall, volume, residual, own, lo, frac, win, base, first):
+def backward(subset, tall, volume, made, residual, own, lo, frac, win, base, first):
     blocks = volume.shape[0]
     vmem = pl.BlockSpec(memory_space=pltpu.VMEM)
     hbm = pl.BlockSpec(memory_space=pl.ANY)
     dma = pltpu.SemaphoreType.DMA
     return pl.pallas_call(
         lambda *refs: backward_kernel(subset, first, tall, *refs),
-        in_specs=[smem(), smem(), smem(), hbm, vmem, vmem, vmem],
+        in_specs=[smem(), smem(), smem(), hbm, hbm, vmem, vmem, vmem],
         out_specs=[hbm, vmem],
         out_shape=[jax.ShapeDtypeStruct(volume.shape, jnp.float32),
                    jax.ShapeDtypeStruct(own.shape, jnp.float32)],
         scratch_shapes=[pltpu.VMEM(volume.shape, jnp.float32),
                         pltpu.VMEM(volume.shape, jnp.float32),
+                        pltpu.VMEM(made.shape, jnp.bfloat16),
                         pltpu.VMEM((ANG_SUB * R, VOX), jnp.float32),
                         pltpu.VMEM(residual.shape, jnp.float32),
                         pltpu.VMEM((ANG_SUB * TALL, LANES), jnp.float32),
                         pltpu.VMEM((ANG_SUB * RAYS, LANES), jnp.float32),
                         pltpu.SMEM((ANG_SUB * TILES + 1,), jnp.int32),
                         pltpu.SMEM((ANG_SUB + 1,), jnp.int32),
-                        dma((blocks // CHUNK,)), dma((blocks // CHUNK,))],
+                        dma((blocks // min(CHUNK, blocks // 2),)), dma((blocks // min(CHUNK, blocks // 2),)),
+                        dma((made.shape[0] // MADE,))],
         compiler_params=pltpu.CompilerParams(vmem_limit_bytes=VMEM_LIMIT),
         name="backward",
-    )(lo, frac, win, volume, base, residual, own)
+    )(lo, frac, win, volume, made, base, residual, own)
 
 
 def ray_table():
@@ -646,8 +697,9 @@
     for subset in range(SUBSETS):
         base, first = geometry(subset)
         partial = forward(subset, tall, estimate, lo, frac, win, base, first)
-        full, own = exchange(subset, tall, partial, live_rays, table, measured, rows, groups, patches)
-        estimate, own = backward(subset, tall, estimate, full, own, lo, frac, win, base, first)
+        full, own, made = exchange(
+            subset, tall, partial, live_rays, table, frac, measured, base, rows, groups, patches)
+        estimate, own = backward(subset, tall, estimate, made, full, own, lo, frac, win, base, first)
     return (estimate, own[None])
 
 

time: 117 us -> 122 us (1.043)
  Pallas kernels: 116 us -> 120 us
    pallas_call x2, Pallas kernels: 50.6 us -> 54.1 us  [exchange(): pl.pallas_call(lambda *refs: exchange_kernel(subset, tall, *refs), in_spe...]
where the time goes in v6:
time: 122 us; the launch traced here: 121 us
  Pallas kernels  120 us (98%)
    pallas_call x2, Pallas kernels, exchange(): pl.pallas_call(lambda *refs: exchange_kernel(subset, tall, *refs), in_spe...  54.1 us
    pallas_call x2, Pallas kernels, backward(): pl.pallas_call(lambda *refs: backward_kernel(subset, first, tall, *refs),...  32.5 us
    pallas_call x2, Pallas kernels, forward(): pl.pallas_call(lambda *refs: forward_kernel(subset, first, tall, *refs),...  32.4 us

profile of v6, /device:TPU:1, one launch (start us, length us, event | category | flops | bytes accessed | tf_op | source)
XLA Modules:
  0.0 121.3 jit_solution(18067415823035782691)
XLA Ops:
  0.6 1.4 %placing.1 = (s32[2,8,128]{2,1,0:T(8,128)}, f32[2,8,128]{2,1,0:T(8,128)}, s32[1,384]{1,0:T(1,128)}) custom-call(s32[1,128]{1,0:T(1,128)} %bitcast.11), custom_call_target="tpu_custom_call" | custom-call | tf_op jit(solution)/shard_map/placing/pallas_call | solution.py:680
  2.0 16.2 %forward.2 = f32[1536,128]{1,0:T(8,128)} custom-call(s32[2,8,128]{2,1,0:T(8,128)} %get-tuple-element.14.refs_0_, f32[2,8,128]{2,1,0:T(8,128)} %get-tuple-element.15.refs_1_.refs_3_, s32[1,384]{1,0:T(1,128)} %get-tuple-element.16.refs_2_, f32[128,8,1024]{2,1,0:T(8,128)} %refs_3_.3, f32[1024,128]{1,0:T(8,128)} %constant.10.clone.refs_4_), custom_call_target="tpu_custom_call" | custom-call | tf_op jit(solution)/shard_map/forward/pallas_call | solution.py:597
  18.2 28.7 %exchange.2 = (bf16[4,2,4,48,128]{4,3,2,1,0:T(8,128)(2,1)}, f32[16,384]{1,0:T(8,128)}, bf16[64,128,1024]{2,1,0:T(8,128)(2,1)}) custom-call(f32[4,2,4,48,128]{4,3,2,1,0:T(8,128)} %bitcast.7, s32[2,512]{1,0:T(2,128)} %refs_1_.3, f32[2,3,8]{2,1,0:T(4,128)} %constant.11.clone.refs_2_, f32[2,8,128]{2,1,0:T(8,128)} %get-tuple-element.15.refs_1_.refs_3_, ...), custom_call_target="tpu_custom_call" | custom-call | tf_op jit(solution)/shard_map/exchange/pallas_call | solution.py:560
  46.9 16.2 %backward.2 = (f32[128,8,1024]{2,1,0:T(8,128)}, f32[16,384]{1,0:T(8,128)}) custom-call(s32[2,8,128]{2,1,0:T(8,128)} %get-tuple-element.14.refs_0_, f32[2,8,128]{2,1,0:T(8,128)} %get-tuple-element.15.refs_1_.refs_3_, s32[1,384]{1,0:T(1,128)} %get-tuple-element.16.refs_2_, f32[128,8,1024]{2,1,0:T(8,128)} %refs_3_.3, ...), custom_call_target="tpu_custom_call" | custom-call | tf_op jit(solution)/shard_map/backward/pallas_call | solution.py:619
  63.2 16.2 %forward.3 = f32[1536,128]{1,0:T(8,128)} custom-call(s32[2,8,128]{2,1,0:T(8,128)} %get-tuple-element.14.refs_0_, f32[2,8,128]{2,1,0:T(8,128)} %get-tuple-element.15.refs_1_.refs_3_, s32[1,384]{1,0:T(1,128)} %get-tuple-element.16.refs_2_, f32[128,8,1024]{2,1,0:T(8,128)} %get-tuple-element.20.refs_3_, f32[1024,128]{1,0:T(8,128)} %constant.13.clone.refs_4_), custom_call_target="tpu_custom_call" | custom-call | tf_op jit(solution)/shard_map/forward/pallas_call | solution.py:597
  79.4 25.4 %exchange.3 = (bf16[4,2,4,48,128]{4,3,2,1,0:T(8,128)(2,1)}, f32[16,384]{1,0:T(8,128)}, bf16[64,128,1024]{2,1,0:T(8,128)(2,1)}) custom-call(f32[4,2,4,48,128]{4,3,2,1,0:T(8,128)} %bitcast.6, s32[2,512]{1,0:T(2,128)} %refs_1_.3, f32[2,3,8]{2,1,0:T(4,128)} %constant.11.clone.refs_2_, f32[2,8,128]{2,1,0:T(8,128)} %get-tuple-element.15.refs_1_.refs_3_, ...), custom_call_target="tpu_custom_call" | custom-call | tf_op jit(solution)/shard_map/exchange/pallas_call | solution.py:560
  104.9 16.3 %backward.3 = (f32[128,8,1024]{2,1,0:T(8,128)}, f32[16,384]{1,0:T(8,128)}) custom-call(s32[2,8,128]{2,1,0:T(8,128)} %get-tuple-element.14.refs_0_, f32[2,8,128]{2,1,0:T(8,128)} %get-tuple-element.15.refs_1_.refs_3_, s32[1,384]{1,0:T(1,128)} %get-tuple-element.16.refs_2_, f32[128,8,1024]{2,1,0:T(8,128)} %get-tuple-element.20.refs_3_, ...), custom_call_target="tpu_custom_call" | custom-call | tf_op jit(solution)/shard_map/backward/pallas_call | solution.py:619

commit v7 on v6

--- a/solution.py
+++ b/solution.py
@@ -27,7 +27,8 @@
 PAD = 32
 CHUNK = 32
 MADE = 4
-MADE_EARLY = (3, 8)
+MADE_EARLY = (0, 5)
+PARTS = 4
 DEPTH = 2
 EARLY = 3
 SPAN = 128
@@ -147,7 +148,7 @@
 
 
 def size_of(ref):
-    return min(CHUNK, ref.shape[0] // 2)
+    return min(CHUNK, ref.shape[0] // PARTS)
 
 
 def chunk_of(ref, c):
@@ -287,7 +288,7 @@
             lhs = jnp.concatenate([turned[g * 32:(g + 1) * 32], ones], axis=0).astype(jnp.bfloat16)
             at = slice(g * width, (g + 1) * width)
             if ready:
-                f = made[b - made.shape[0], :, at]
+                f = made[b - (vol_ref.shape[0] - made.shape[0]), :, at]
             else:
                 f = jnp.concatenate([footprint(e_scr[a * R:(a + 1) * R, at] + frac_ref[subset, a, b])
                                      for a in range(ANG_SUB)], axis=0)
@@ -310,10 +311,11 @@
         emit(c).start()
         return carry
 
-    lax.fori_loop(0, chunks // 2, lambda c, carry: chunk(c, carry, False), 0)
+    plain = chunks - chunks // PARTS
+    lax.fori_loop(0, plain, lambda c, carry: chunk(c, carry, False), 0)
     for c in range(made.shape[0] // MADE):
         load(c).wait()
-    lax.fori_loop(chunks // 2, chunks, lambda c, carry: chunk(c, carry, True), 0)
+    lax.fori_loop(plain, chunks, lambda c, carry: chunk(c, carry, True), 0)
     for c in range(chunks):
         emit(c).wait()
 
@@ -407,7 +409,7 @@
             put(i - 2).wait()
 
         for k in range(MADE):
-            b = frac_ref.shape[2] // 2 + i * MADE + k
+            b = frac_ref.shape[2] - made_hbm.shape[0] + i * MADE + k
             for a in range(ANG_SUB):
                 made[lax.rem(i, 2), k, a * R:(a + 1) * R, :] = footprint(
                     e_scr[a * R:(a + 1) * R, :] + frac_ref[subset, a, b])
@@ -563,7 +565,7 @@
         out_specs=[vmem, vmem, pl.BlockSpec(memory_space=pl.ANY)],
         out_shape=[jax.ShapeDtypeStruct(shape, jnp.bfloat16),
                    jax.ShapeDtypeStruct((rows, measured.shape[2]), jnp.float32),
-                   jax.ShapeDtypeStruct((frac.shape[2] // 2, LANES, VOX), jnp.bfloat16)],
+                   jax.ShapeDtypeStruct((frac.shape[2] // PARTS, LANES, VOX), jnp.bfloat16)],
         scratch_shapes=[pltpu.VMEM((pairs, groups, lines, LANES), jnp.float32),
                         pltpu.VMEM((pairs, groups, lines, LANES), jnp.float32),
                         pltpu.VMEM((pairs, groups, lines, LANES), wire),
@@ -605,7 +607,7 @@
                         pltpu.VMEM((ANG_SUB * TALL, LANES), jnp.float32),
                         pltpu.SMEM((ANG_SUB * TILES + 1,), jnp.int32),
                         pltpu.SMEM((ANG_SUB + 1,), jnp.int32),
-                        dma, dma((blocks // min(CHUNK, blocks // 2),))],
+                        dma, dma((blocks // min(CHUNK, blocks // PARTS),))],
         compiler_params=pltpu.CompilerParams(vmem_limit_bytes=VMEM_LIMIT),
         name="forward",
     )(lo, frac, win, volume, grid.T.astype(np.float32))
@@ -631,7 +633,7 @@
                         pltpu.VMEM((ANG_SUB * RAYS, LANES), jnp.float32),
                         pltpu.SMEM((ANG_SUB * TILES + 1,), jnp.int32),
                         pltpu.SMEM((ANG_SUB + 1,), jnp.int32),
-                        dma((blocks // min(CHUNK, blocks // 2),)), dma((blocks // min(CHUNK, blocks // 2),)),
+                        dma((blocks // min(CHUNK, blocks // PARTS),)), dma((blocks // min(CHUNK, blocks // PARTS),)),
                         dma((made.shape[0] // MADE,))],
         compiler_params=pltpu.CompilerParams(vmem_limit_bytes=VMEM_LIMIT),
         name="backward",

time: 122 us -> 117 us (0.959)
  Pallas kernels: 120 us -> 115 us
    pallas_call x2, Pallas kernels: 54.1 us -> 51.4 us  [exchange(): pl.pallas_call(lambda *refs: exchange_kernel(subset, tall, *refs), in_spe...]
    pallas_call x2, Pallas kernels: 32.5 us -> 30.2 us  [backward(): pl.pallas_call(lambda *refs: backward_kernel(subset, first, tall, *refs),...]
where the time goes in v7:
time: 117 us; the launch traced here: 116 us
  Pallas kernels  115 us (98%)
    pallas_call x2, Pallas kernels, exchange(): pl.pallas_call(lambda *refs: exchange_kernel(subset, tall, *refs), in_spe...  51.4 us
    pallas_call x2, Pallas kernels, forward(): pl.pallas_call(lambda *refs: forward_kernel(subset, first, tall, *refs),...  32.1 us
    pallas_call x2, Pallas kernels, backward(): pl.pallas_call(lambda *refs: backward_kernel(subset, first, tall, *refs),...  30.2 us

profile of v7, /device:TPU:1, one launch (start us, length us, event | category | flops | bytes accessed | tf_op | source)
XLA Modules:
  0.0 115.9 jit_solution(18196180714182449904)
XLA Ops:
  0.6 1.4 %placing.1 = (s32[2,8,128]{2,1,0:T(8,128)}, f32[2,8,128]{2,1,0:T(8,128)}, s32[1,384]{1,0:T(1,128)}) custom-call(s32[1,128]{1,0:T(1,128)} %bitcast.11), custom_call_target="tpu_custom_call" | custom-call | tf_op jit(solution)/shard_map/placing/pallas_call | solution.py:682
  2.1 16.0 %forward.2 = f32[1536,128]{1,0:T(8,128)} custom-call(s32[2,8,128]{2,1,0:T(8,128)} %get-tuple-element.14.refs_0_, f32[2,8,128]{2,1,0:T(8,128)} %get-tuple-element.15.refs_1_.refs_3_, s32[1,384]{1,0:T(1,128)} %get-tuple-element.16.refs_2_, f32[128,8,1024]{2,1,0:T(8,128)} %refs_3_.3, f32[1024,128]{1,0:T(8,128)} %constant.10.clone.refs_4_), custom_call_target="tpu_custom_call" | custom-call | tf_op jit(solution)/shard_map/forward/pallas_call | solution.py:599
  18.1 24.2 %exchange.2 = (bf16[4,2,4,48,128]{4,3,2,1,0:T(8,128)(2,1)}, f32[16,384]{1,0:T(8,128)}, bf16[32,128,1024]{2,1,0:T(8,128)(2,1)}) custom-call(f32[4,2,4,48,128]{4,3,2,1,0:T(8,128)} %bitcast.7, s32[2,512]{1,0:T(2,128)} %refs_1_.3, f32[2,3,8]{2,1,0:T(4,128)} %constant.11.clone.refs_2_, f32[2,8,128]{2,1,0:T(8,128)} %get-tuple-element.15.refs_1_.refs_3_, ...), custom_call_target="tpu_custom_call" | custom-call | tf_op jit(solution)/shard_map/exchange/pallas_call | solution.py:562
  42.3 15.1 %backward.2 = (f32[128,8,1024]{2,1,0:T(8,128)}, f32[16,384]{1,0:T(8,128)}) custom-call(s32[2,8,128]{2,1,0:T(8,128)} %get-tuple-element.14.refs_0_, f32[2,8,128]{2,1,0:T(8,128)} %get-tuple-element.15.refs_1_.refs_3_, s32[1,384]{1,0:T(1,128)} %get-tuple-element.16.refs_2_, f32[128,8,1024]{2,1,0:T(8,128)} %refs_3_.3, ...), custom_call_target="tpu_custom_call" | custom-call | tf_op jit(solution)/shard_map/backward/pallas_call | solution.py:621
  57.4 16.1 %forward.3 = f32[1536,128]{1,0:T(8,128)} custom-call(s32[2,8,128]{2,1,0:T(8,128)} %get-tuple-element.14.refs_0_, f32[2,8,128]{2,1,0:T(8,128)} %get-tuple-element.15.refs_1_.refs_3_, s32[1,384]{1,0:T(1,128)} %get-tuple-element.16.refs_2_, f32[128,8,1024]{2,1,0:T(8,128)} %get-tuple-element.20.refs_3_, f32[1024,128]{1,0:T(8,128)} %constant.13.clone.refs_4_), custom_call_target="tpu_custom_call" | custom-call | tf_op jit(solution)/shard_map/forward/pallas_call | solution.py:599
  73.4 27.2 %exchange.3 = (bf16[4,2,4,48,128]{4,3,2,1,0:T(8,128)(2,1)}, f32[16,384]{1,0:T(8,128)}, bf16[32,128,1024]{2,1,0:T(8,128)(2,1)}) custom-call(f32[4,2,4,48,128]{4,3,2,1,0:T(8,128)} %bitcast.6, s32[2,512]{1,0:T(2,128)} %refs_1_.3, f32[2,3,8]{2,1,0:T(4,128)} %constant.11.clone.refs_2_, f32[2,8,128]{2,1,0:T(8,128)} %get-tuple-element.15.refs_1_.refs_3_, ...), custom_call_target="tpu_custom_call" | custom-call | tf_op jit(solution)/shard_map/exchange/pallas_call | solution.py:562
  100.6 15.1 %backward.3 = (f32[128,8,1024]{2,1,0:T(8,128)}, f32[16,384]{1,0:T(8,128)}) custom-call(s32[2,8,128]{2,1,0:T(8,128)} %get-tuple-element.14.refs_0_, f32[2,8,128]{2,1,0:T(8,128)} %get-tuple-element.15.refs_1_.refs_3_, s32[1,384]{1,0:T(1,128)} %get-tuple-element.16.refs_2_, f32[128,8,1024]{2,1,0:T(8,128)} %get-tuple-element.20.refs_3_, ...), custom_call_target="tpu_custom_call" | custom-call | tf_op jit(solution)/shard_map/backward/pallas_call | solution.py:621

commit v8 on v7

--- a/solution.py
+++ b/solution.py
@@ -155,46 +155,24 @@
     return ref.at[pl.ds(c * size_of(ref), size_of(ref))]
 
 
-def forward_kernel(subset, first, tall, lo_ref, frac_ref, win_ref, vol_hbm, grid_hbm, out_ref,
-                   vol_ref, grid_ref, tot, acc, tiles, starts, grid_sem, vol_sem):
-    size = size_of(vol_ref)
-    chunks = vol_ref.shape[0] // size
-
-    def fetch(c):
-        return pltpu.make_async_copy(chunk_of(vol_hbm, c), chunk_of(vol_ref, c), vol_sem.at[c])
-
-    grid_copy = pltpu.make_async_copy(grid_hbm, grid_ref, grid_sem)
-    grid_copy.start()
-    for c in range(min(DEPTH, chunks)):
-        fetch(c).start()
-
-    zero = jnp.zeros((2 * SPAN, LANES), jnp.float32)
-    list_tiles(subset, win_ref, tiles, starts)
-
-    def clear(t, at):
-        acc[pl.ds(aligned(at // TILES * TALL + lax.rem(at, TILES) * SPAN, SPAN), 2 * SPAN), :] = zero
-
-    over_tiles(tiles, starts, clear)
-    out_ref[...] = jnp.zeros_like(out_ref)
-    grid_copy.wait()
-
+def forward_parts(subset, first, tall, lo_ref, frac_ref, win_ref, vol_ref, grid_ref, out_ref, tot, acc, tiles, starts):
     width = SUB * BLK_SIDE
     group = BLK_SIDE // SUB
     slices = vol_ref.shape[1]
     col_group = (lax.broadcasted_iota(jnp.int32, (group * slices, width), 1) % BLK_SIDE) // SUB
     mine = col_group == lax.broadcasted_iota(jnp.int32, (group * slices, width), 0) // slices
+    mine = jnp.where(mine, 1.0, 0.0).astype(jnp.bfloat16)
     angle = lax.broadcasted_iota(jnp.int32, (1, LANES), 1) // R
-    def chunk(c, carry):
-        fetch(c).wait()
-
-        @pl.when(c + DEPTH < chunks)
-        def _():
-            fetch(c + DEPTH).start()
-
-        for i in range(size):
-            block(c * size + i)
-        return carry
-
+
+    def prepare():
+        zero = jnp.zeros((2 * SPAN, LANES), jnp.float32)
+        list_tiles(subset, win_ref, tiles, starts)
+
+        def clear(t, at):
+            acc[pl.ds(aligned(at // TILES * TALL + lax.rem(at, TILES) * SPAN, SPAN), 2 * SPAN), :] = zero
+
+        over_tiles(tiles, starts, clear)
+        out_ref[...] = jnp.zeros_like(out_ref)
     def block(b):
         frac = jnp.zeros((1, LANES), jnp.float32)
         for a in range(ANG_SUB):
@@ -203,81 +181,67 @@
         for g in range(group):
             at = slice(g * width, (g + 1) * width)
             f = footprint(grid_ref[at, :] + frac)
-            wide = jnp.where(mine, jnp.tile(vol_ref[b, :, at], (group, 1)), 0.0)
-            parts.append(jnp.dot(wide.astype(jnp.bfloat16), f, preferred_element_type=jnp.float32))
+            pair = jnp.concatenate([vol_ref[b, :, at]] * 2, axis=0).astype(jnp.bfloat16)
+            wide = jnp.tile(pair, (group // 2, 1)) * mine
+            parts.append(jnp.dot(wide, f, preferred_element_type=jnp.float32))
         part = jnp.transpose(jnp.concatenate(parts, axis=0))
         for a in range(ANG_SUB):
             at = pl.ds(a * TALL + PAD + lo_ref[subset, a, b], R)
             acc[at, :] += part[a * R:(a + 1) * R, :]
 
-    lax.fori_loop(0, chunks, chunk, 0)
-    lane_q = lax.broadcasted_iota(jnp.int32, (1, LANES), 1) // 8
-
-    for a in range(ANG_SUB):
-        def merge(t, i, a=a):
-            base = aligned(a * TALL + PAD + i * SPAN, 32)
-            tot[pl.ds(aligned(t * SPAN, SPAN), SPAN), :] = shifted(
-                acc, base, [-int(o) for o in first[a]], lane_q)
-
-        over_angle(a, tiles, starts, merge)
-
-    def fold(t, at):
-        rows = [tot[sixteenth(aligned(t * SPAN, SPAN), r, tall), :] for r in range(16)]
-        for half in (1, 2, 4, 8):
-            low = lane_q % (2 * half) < half
-            rows = [jnp.where(low, x, y) + pltpu.roll(jnp.where(low, y, x), half * 8, 1)
-                    for x, y in zip(rows[0::2], rows[1::2])]
-        out_ref[pl.ds(aligned(at * 8, 8), 8), :] = rows[0]
-
-    over_tiles(tiles, starts, fold)
-
-
-def backward_kernel(subset, first, tall, lo_ref, frac_ref, win_ref, vol_hbm, made_hbm, base_ref, res_ref, own_ref,
-                    out_hbm, last_ref,
-                    vol_ref, out_ref, made, e_scr, res, rb, dd, tiles, starts, vol_sem, out_sem, made_sem):
-    size = size_of(vol_ref)
-    chunks = vol_ref.shape[0] // size
-
-    def fetch(c):
-        return pltpu.make_async_copy(chunk_of(vol_hbm, c), chunk_of(vol_ref, c), vol_sem.at[c])
-
-    def emit(c):
-        return pltpu.make_async_copy(chunk_of(out_ref, c), chunk_of(out_hbm, c), out_sem.at[c])
-
-    def load(c):
-        at = pl.ds(c * MADE, MADE)
-        return pltpu.make_async_copy(made_hbm.at[at], made.at[at], made_sem.at[c])
-
-    for c in range(min(DEPTH, chunks)):
-        fetch(c).start()
-    for c in range(made.shape[0] // MADE):
-        load(c).start()
-    fill_grid(base_ref, e_scr)
-    lane_q = lax.broadcasted_iota(jnp.int32, (1, LANES), 1) // 8
-    last_ref[...] = own_ref[...]
-    res[...] = res_ref[...].astype(jnp.float32)
-    list_tiles(subset, win_ref, tiles, starts)
-
-    def widen(t, at):
-        rows = spread_lanes(res[pl.ds(aligned(at * 8, 8), 8), :], lane_q)
-        base = aligned(at // TILES * TALL + PAD + lax.rem(at, TILES) * SPAN, 32)
-        for r in range(16):
-            rb[sixteenth(base, r, tall), :] = rows[r]
-
-    over_tiles(tiles, starts, widen)
-
-    for a in range(ANG_SUB):
-        def shift(t, i, a=a):
-            base = aligned(a * TALL + PAD + i * SPAN, 32)
-            dd[pl.ds(aligned(a * RAYS + i * SPAN, SPAN), SPAN), :] = shifted(
-                rb, base, [int(o) for o in first[a]], lane_q)
-
-        over_angle(a, tiles, starts, shift)
-
+    def finish():
+        lane_q = lax.broadcasted_iota(jnp.int32, (1, LANES), 1) // 8
+
+        for a in range(ANG_SUB):
+            def merge(t, i, a=a):
+                base = aligned(a * TALL + PAD + i * SPAN, 32)
+                tot[pl.ds(aligned(t * SPAN, SPAN), SPAN), :] = shifted(
+                    acc, base, [-int(o) for o in first[a]], lane_q)
+
+            over_angle(a, tiles, starts, merge)
+
+        def fold(t, at):
+            rows = [tot[sixteenth(aligned(t * SPAN, SPAN), r, tall), :] for r in range(16)]
+            for half in (1, 2, 4, 8):
+                low = lane_q % (2 * half) < half
+                rows = [jnp.where(low, x, y) + pltpu.roll(jnp.where(low, y, x), half * 8, 1)
+                        for x, y in zip(rows[0::2], rows[1::2])]
+            out_ref[pl.ds(aligned(at * 8, 8), 8), :] = rows[0]
+
+        over_tiles(tiles, starts, fold)
+
+    return prepare, block, finish
+
+
+def backward_parts(subset, first, tall, lo_ref, frac_ref, win_ref, vol_ref, base_ref, res_ref, out_ref,
+                   made, e_scr, res, rb, dd, tiles, starts):
     width = SUB * BLK_SIDE
     group = BLK_SIDE // SUB
     lane = lax.broadcasted_iota(jnp.int32, (8, width), 1)
     col_group = (lane % BLK_SIDE) // SUB
+
+
+    def prepare():
+        fill_grid(base_ref, e_scr)
+        lane_q = lax.broadcasted_iota(jnp.int32, (1, LANES), 1) // 8
+        res[...] = res_ref[...].astype(jnp.float32)
+        list_tiles(subset, win_ref, tiles, starts)
+
+        def widen(t, at):
+            rows = spread_lanes(res[pl.ds(aligned(at * 8, 8), 8), :], lane_q)
+            base = aligned(at // TILES * TALL + PAD + lax.rem(at, TILES) * SPAN, 32)
+            for r in range(16):
+                rb[sixteenth(base, r, tall), :] = rows[r]
+
+        over_tiles(tiles, starts, widen)
+
+        for a in range(ANG_SUB):
+            def shift(t, i, a=a):
+                base = aligned(a * TALL + PAD + i * SPAN, 32)
+                dd[pl.ds(aligned(a * RAYS + i * SPAN, SPAN), SPAN), :] = shifted(
+                    rb, base, [int(o) for o in first[a]], lane_q)
+
+            over_angle(a, tiles, starts, shift)
 
     def block(b, ready):
         rows = jnp.concatenate(
@@ -299,6 +263,48 @@
             col_sum = part[32:40]
             out_ref[b, :, at] = jnp.maximum(vol_ref[b, :, at] + relax * back / col_sum, 0.0)
 
+    return prepare, block
+
+
+def sweep_kernel(back, fore, tall, names, *refs):
+    ref = dict(zip(names, refs))
+    vol = ref["vol"]
+    size = size_of(vol)
+    chunks = vol.shape[0] // size
+    tables = ref["lo"], ref["frac"], ref["win"]
+
+    def fetch(c):
+        return pltpu.make_async_copy(chunk_of(ref["vol_hbm"], c), chunk_of(vol, c), ref["vol_sem"].at[c])
+
+    def emit(c):
+        return pltpu.make_async_copy(chunk_of(ref["out"], c), chunk_of(ref["out_hbm"], c), ref["out_sem"].at[c])
+
+    def load(c):
+        at = pl.ds(c * MADE, MADE)
+        return pltpu.make_async_copy(ref["made_hbm"].at[at], ref["made"].at[at], ref["made_sem"].at[c])
+
+    loads = 0 if back is None else ref["made"].shape[0] // MADE
+    if fore is not None:
+        grid_copy = pltpu.make_async_copy(ref["grid_hbm"], ref["grid"], ref["grid_sem"])
+        grid_copy.start()
+    for c in range(min(DEPTH, chunks)):
+        fetch(c).start()
+    for c in range(loads):
+        load(c).start()
+    if back is not None:
+        prepare, update = backward_parts(
+            back, geometry(back)[1], tall, *tables, vol, ref["base"], ref["residual"], ref["out"], ref["made"],
+            ref["edges"], ref["res"], ref["tall"], ref["flat"], ref["tiles"], ref["starts"])
+        prepare()
+    if fore is not None:
+        prepare, project, finish = forward_parts(
+            fore, geometry(fore)[1], tall, *tables, vol if back is None else ref["out"], ref["grid"], ref["part"],
+            ref["flat"], ref["tall"], ref["tiles"], ref["starts"])
+        prepare()
+        grid_copy.wait()
+    else:
+        ref["last"][...] = ref["own"][...]
+
     def chunk(c, carry, ready):
         fetch(c).wait()
 
@@ -306,18 +312,26 @@
         def _():
             fetch(c + DEPTH).start()
 
-        for i in range(size):
-            block(c * size + i, ready)
-        emit(c).start()
+        if back is not None:
+            for i in range(size):
+                update(c * size + i, ready)
+            emit(c).start()
+        if fore is not None:
+            for i in range(size):
+                project(c * size + i)
         return carry
 
-    plain = chunks - chunks // PARTS
+    plain = chunks if back is None else chunks - chunks // PARTS
     lax.fori_loop(0, plain, lambda c, carry: chunk(c, carry, False), 0)
-    for c in range(made.shape[0] // MADE):
+    for c in range(loads):
         load(c).wait()
-    lax.fori_loop(plain, chunks, lambda c, carry: chunk(c, carry, True), 0)
-    for c in range(chunks):
-        emit(c).wait()
+    if plain < chunks:
+        lax.fori_loop(plain, chunks, lambda c, carry: chunk(c, carry, True), 0)
+    if fore is not None:
+        finish()
+    if back is not None:
+        for c in range(chunks):
+            emit(c).wait()
 
 
 def ray_sums(shape, big, small, inv, ray):
@@ -589,55 +603,49 @@
     return pl.BlockSpec(memory_space=pltpu.SMEM)
 
 
-def forward(subset, tall, volume, lo, frac, win, base, first):
+def sweep(back, fore, tall, volume, lo, frac, win, made=None, residual=None, own=None):
     blocks = volume.shape[0]
+    chunks = blocks // min(CHUNK, blocks // PARTS)
     lines = ANG_SUB * RAYS // 16
-    grid = (np.repeat(base, R, axis=0) - np.tile(np.arange(R), ANG_SUB)[:, None]) * (1.0 / spread)
     vmem = pl.BlockSpec(memory_space=pltpu.VMEM)
     hbm = pl.BlockSpec(memory_space=pl.ANY)
     dma = pltpu.SemaphoreType.DMA
+    f32 = jnp.float32
+    given = [("lo", smem(), lo), ("frac", smem(), frac), ("win", smem(), win), ("vol_hbm", hbm, volume)]
+    made_here = []
+    scratch = [("vol", pltpu.VMEM(volume.shape, f32)),
+               ("tall", pltpu.VMEM((ANG_SUB * TALL, LANES), f32)),
+               ("flat", pltpu.VMEM((ANG_SUB * RAYS, LANES), f32)),
+               ("tiles", pltpu.SMEM((ANG_SUB * TILES + 1,), jnp.int32)),
+               ("starts", pltpu.SMEM((ANG_SUB + 1,), jnp.int32)),
+               ("vol_sem", dma((chunks,)))]
+    if fore is not None:
+        base = geometry(fore)[0]
+        grid = (np.repeat(base, R, axis=0) - np.tile(np.arange(R), ANG_SUB)[:, None]) * (1.0 / spread)
+        given.append(("grid_hbm", hbm, grid.T.astype(np.float32)))
+        made_here.append(("part", vmem, jax.ShapeDtypeStruct((lines, LANES), f32)))
+        scratch += [("grid", pltpu.VMEM((VOX, LANES), f32)), ("grid_sem", dma)]
+    if back is not None:
+        given += [("made_hbm", hbm, made), ("base", vmem, geometry(back)[0]), ("residual", vmem, residual)]
+        made_here.append(("out_hbm", hbm, jax.ShapeDtypeStruct(volume.shape, f32)))
+        scratch += [("out", pltpu.VMEM(volume.shape, f32)),
+                    ("made", pltpu.VMEM(made.shape, jnp.bfloat16)),
+                    ("edges", pltpu.VMEM((ANG_SUB * R, VOX), f32)),
+                    ("res", pltpu.VMEM(residual.shape, f32)),
+                    ("out_sem", dma((chunks,))), ("made_sem", dma((made.shape[0] // MADE,)))]
+    if fore is None:
+        given.append(("own", vmem, own))
+        made_here.append(("last", vmem, jax.ShapeDtypeStruct(own.shape, f32)))
+    names = [x[0] for x in given + made_here + scratch]
     return pl.pallas_call(
-        lambda *refs: forward_kernel(subset, first, tall, *refs),
-        in_specs=[smem(), smem(), smem(), hbm, hbm],
-        out_specs=vmem,
-        out_shape=jax.ShapeDtypeStruct((lines, LANES), jnp.float32),
-        scratch_shapes=[pltpu.VMEM(volume.shape, jnp.float32),
-                        pltpu.VMEM((VOX, LANES), jnp.float32),
-                        pltpu.VMEM((ANG_SUB * RAYS, LANES), jnp.float32),
-                        pltpu.VMEM((ANG_SUB * TALL, LANES), jnp.float32),
-                        pltpu.SMEM((ANG_SUB * TILES + 1,), jnp.int32),
-                        pltpu.SMEM((ANG_SUB + 1,), jnp.int32),
-                        dma, dma((blocks // min(CHUNK, blocks // PARTS),))],
+        lambda *refs: sweep_kernel(back, fore, tall, names, *refs),
+        in_specs=[x[1] for x in given],
+        out_specs=[x[1] for x in made_here],
+        out_shape=[x[2] for x in made_here],
+        scratch_shapes=[x[1] for x in scratch],
         compiler_params=pltpu.CompilerParams(vmem_limit_bytes=VMEM_LIMIT),
-        name="forward",
-    )(lo, frac, win, volume, grid.T.astype(np.float32))
-
-
-def backward(subset, tall, volume, made, residual, own, lo, frac, win, base, first):
-    blocks = volume.shape[0]
-    vmem = pl.BlockSpec(memory_space=pltpu.VMEM)
-    hbm = pl.BlockSpec(memory_space=pl.ANY)
-    dma = pltpu.SemaphoreType.DMA
-    return pl.pallas_call(
-        lambda *refs: backward_kernel(subset, first, tall, *refs),
-        in_specs=[smem(), smem(), smem(), hbm, hbm, vmem, vmem, vmem],
-        out_specs=[hbm, vmem],
-        out_shape=[jax.ShapeDtypeStruct(volume.shape, jnp.float32),
-                   jax.ShapeDtypeStruct(own.shape, jnp.float32)],
-        scratch_shapes=[pltpu.VMEM(volume.shape, jnp.float32),
-                        pltpu.VMEM(volume.shape, jnp.float32),
-                        pltpu.VMEM(made.shape, jnp.bfloat16),
-                        pltpu.VMEM((ANG_SUB * R, VOX), jnp.float32),
-                        pltpu.VMEM(residual.shape, jnp.float32),
-                        pltpu.VMEM((ANG_SUB * TALL, LANES), jnp.float32),
-                        pltpu.VMEM((ANG_SUB * RAYS, LANES), jnp.float32),
-                        pltpu.SMEM((ANG_SUB * TILES + 1,), jnp.int32),
-                        pltpu.SMEM((ANG_SUB + 1,), jnp.int32),
-                        dma((blocks // min(CHUNK, blocks // PARTS),)), dma((blocks // min(CHUNK, blocks // PARTS),)),
-                        dma((made.shape[0] // MADE,))],
-        compiler_params=pltpu.CompilerParams(vmem_limit_bytes=VMEM_LIMIT),
-        name="backward",
-    )(lo, frac, win, volume, made, base, residual, own)
+        name="sweep",
+    )(*[x[2] for x in given])
 
 
 def ray_table():
@@ -695,13 +703,14 @@
     table = ray_table()
     tall = rows * RAYS_TILE % (2 * LANES) == 0
     estimate = volume
-    own = None
+    (partial,) = sweep(None, 0, tall, estimate, lo, frac, win)
     for subset in range(SUBSETS):
-        base, first = geometry(subset)
-        partial = forward(subset, tall, estimate, lo, frac, win, base, first)
         full, own, made = exchange(
-            subset, tall, partial, live_rays, table, frac, measured, base, rows, groups, patches)
-        estimate, own = backward(subset, tall, estimate, made, full, own, lo, frac, win, base, first)
+            subset, tall, partial, live_rays, table, frac, measured, geometry(subset)[0], rows, groups, patches)
+        if subset < SUBSETS - 1:
+            partial, estimate = sweep(subset, subset + 1, tall, estimate, lo, frac, win, made, full)
+        else:
+            estimate, own = sweep(subset, None, tall, estimate, lo, frac, win, made, full, own)
     return (estimate, own[None])
 
 

time: 117 us -> 114 us (0.974)
  Pallas kernels: 115 us -> 113 us
    pallas_call x4 -> x3, Pallas kernels: 62.3 us -> 60.2 us  [sweep(): pl.pallas_call(lambda *refs: sweep_kernel(back, fore, tall, names, *refs)...]
where the time goes in v8:
time: 114 us; the launch traced here: 113 us
  Pallas kernels  113 us (99%)
    pallas_call x3, Pallas kernels, sweep(): pl.pallas_call(lambda *refs: sweep_kernel(back, fore, tall, names, *refs)...  60.2 us
    pallas_call x2, Pallas kernels, exchange(): pl.pallas_call(lambda *refs: exchange_kernel(subset, tall, *refs), in_spe...  50.9 us

profile of v8, /device:TPU:1, one launch (start us, length us, event | category | flops | bytes accessed | tf_op | source)
XLA Modules:
  0.0 113.4 jit_solution(3495344209154898578)
XLA Ops:
  0.6 1.4 %placing.1 = (s32[2,8,128]{2,1,0:T(8,128)}, f32[2,8,128]{2,1,0:T(8,128)}, s32[1,384]{1,0:T(1,128)}) custom-call(s32[1,128]{1,0:T(1,128)} %bitcast.11), custom_call_target="tpu_custom_call" | custom-call | tf_op jit(solution)/shard_map/placing/pallas_call | solution.py:690
  2.1 16.2 %sweep.3 = f32[1536,128]{1,0:T(8,128)} custom-call(s32[2,8,128]{2,1,0:T(8,128)} %get-tuple-element.14.refs_0_, f32[2,8,128]{2,1,0:T(8,128)} %get-tuple-element.15.refs_1_.refs_3_, s32[1,384]{1,0:T(1,128)} %get-tuple-element.16.refs_2_, f32[128,8,1024]{2,1,0:T(8,128)} %refs_3_.3, f32[1024,128]{1,0:T(8,128)} %constant.10.clone.refs_4_), custom_call_target="tpu_custom_call" | custom-call | tf_op jit(solution)/shard_map/sweep/pallas_call | solution.py:640
  18.3 24.8 %exchange.2 = (bf16[4,2,4,48,128]{4,3,2,1,0:T(8,128)(2,1)}, f32[16,384]{1,0:T(8,128)}, bf16[32,128,1024]{2,1,0:T(8,128)(2,1)}) custom-call(f32[4,2,4,48,128]{4,3,2,1,0:T(8,128)} %bitcast.6, s32[2,512]{1,0:T(2,128)} %refs_1_.3, f32[2,3,8]{2,1,0:T(4,128)} %constant.11.clone.refs_2_, f32[2,8,128]{2,1,0:T(8,128)} %get-tuple-element.15.refs_1_.refs_3_, ...), custom_call_target="tpu_custom_call" | custom-call | tf_op jit(solution)/shard_map/exchange/pallas_call | solution.py:576
  43.1 28.6 %sweep.4 = (f32[1536,128]{1,0:T(8,128)}, f32[128,8,1024]{2,1,0:T(8,128)}) custom-call(s32[2,8,128]{2,1,0:T(8,128)} %get-tuple-element.14.refs_0_, f32[2,8,128]{2,1,0:T(8,128)} %get-tuple-element.15.refs_1_.refs_3_, s32[1,384]{1,0:T(1,128)} %get-tuple-element.16.refs_2_, f32[128,8,1024]{2,1,0:T(8,128)} %refs_3_.3, f32[1024,128]{1,0:T(8,128)} %constant.13.clone.refs_4_, ...), custom_call_target="tpu_custom_call" | custom-call | tf_op jit(solution)/shard_map/sweep/pallas_call | solution.py:640
  71.7 26.1 %exchange.3 = (bf16[4,2,4,48,128]{4,3,2,1,0:T(8,128)(2,1)}, f32[16,384]{1,0:T(8,128)}, bf16[32,128,1024]{2,1,0:T(8,128)(2,1)}) custom-call(f32[4,2,4,48,128]{4,3,2,1,0:T(8,128)} %bitcast.7, s32[2,512]{1,0:T(2,128)} %refs_1_.3, f32[2,3,8]{2,1,0:T(4,128)} %constant.11.clone.refs_2_, f32[2,8,128]{2,1,0:T(8,128)} %get-tuple-element.15.refs_1_.refs_3_, ...), custom_call_target="tpu_custom_call" | custom-call | tf_op jit(solution)/shard_map/exchange/pallas_call | solution.py:576
  97.8 15.4 %sweep.5 = (f32[128,8,1024]{2,1,0:T(8,128)}, f32[16,384]{1,0:T(8,128)}) custom-call(s32[2,8,128]{2,1,0:T(8,128)} %get-tuple-element.14.refs_0_, f32[2,8,128]{2,1,0:T(8,128)} %get-tuple-element.15.refs_1_.refs_3_, s32[1,384]{1,0:T(1,128)} %get-tuple-element.16.refs_2_, f32[128,8,1024]{2,1,0:T(8,128)} %get-tuple-element.19.refs_3_, ...), custom_call_target="tpu_custom_call" | custom-call | tf_op jit(solution)/shard_map/sweep/pallas_call | solution.py:640

commit v9 on v8

--- a/solution.py
+++ b/solution.py
@@ -161,7 +161,6 @@
     slices = vol_ref.shape[1]
     col_group = (lax.broadcasted_iota(jnp.int32, (group * slices, width), 1) % BLK_SIDE) // SUB
     mine = col_group == lax.broadcasted_iota(jnp.int32, (group * slices, width), 0) // slices
-    mine = jnp.where(mine, 1.0, 0.0).astype(jnp.bfloat16)
     angle = lax.broadcasted_iota(jnp.int32, (1, LANES), 1) // R
 
     def prepare():
@@ -181,9 +180,8 @@
         for g in range(group):
             at = slice(g * width, (g + 1) * width)
             f = footprint(grid_ref[at, :] + frac)
-            pair = jnp.concatenate([vol_ref[b, :, at]] * 2, axis=0).astype(jnp.bfloat16)
-            wide = jnp.tile(pair, (group // 2, 1)) * mine
-            parts.append(jnp.dot(wide, f, preferred_element_type=jnp.float32))
+            wide = jnp.where(mine, jnp.tile(vol_ref[b, :, at], (group, 1)), 0.0)
+            parts.append(jnp.dot(wide.astype(jnp.bfloat16), f, preferred_element_type=jnp.float32))
         part = jnp.transpose(jnp.concatenate(parts, axis=0))
         for a in range(ANG_SUB):
             at = pl.ds(a * TALL + PAD + lo_ref[subset, a, b], R)

time: 114 us -> 113 us (level)
  no operation moved by 1% of the time
where the time goes in v9:
time: 113 us
  Pallas kernels  112 us (99%)
    pallas_call x3, Pallas kernels, sweep(): pl.pallas_call(lambda *refs: sweep_kernel(back, fore, tall, names, *refs)...  60.4 us
    pallas_call x2, Pallas kernels, exchange(): pl.pallas_call(lambda *refs: exchange_kernel(subset, tall, *refs), in_spe...  50.2 us

profile of v9, /device:TPU:1, one launch (start us, length us, event | category | flops | bytes accessed | tf_op | source)
XLA Modules:
  0.0 112.8 jit_solution(13489209327085908554)
XLA Ops:
  0.6 1.4 %placing.1 = (s32[2,8,128]{2,1,0:T(8,128)}, f32[2,8,128]{2,1,0:T(8,128)}, s32[1,384]{1,0:T(1,128)}) custom-call(s32[1,128]{1,0:T(1,128)} %bitcast.11), custom_call_target="tpu_custom_call" | custom-call | tf_op jit(solution)/shard_map/placing/pallas_call | solution.py:688
  2.1 16.2 %sweep.3 = f32[1536,128]{1,0:T(8,128)} custom-call(s32[2,8,128]{2,1,0:T(8,128)} %get-tuple-element.14.refs_0_, f32[2,8,128]{2,1,0:T(8,128)} %get-tuple-element.15.refs_1_.refs_3_, s32[1,384]{1,0:T(1,128)} %get-tuple-element.16.refs_2_, f32[128,8,1024]{2,1,0:T(8,128)} %refs_3_.3, f32[1024,128]{1,0:T(8,128)} %constant.10.clone.refs_4_), custom_call_target="tpu_custom_call" | custom-call | tf_op jit(solution)/shard_map/sweep/pallas_call | solution.py:638
  18.3 24.6 %exchange.2 = (bf16[4,2,4,48,128]{4,3,2,1,0:T(8,128)(2,1)}, f32[16,384]{1,0:T(8,128)}, bf16[32,128,1024]{2,1,0:T(8,128)(2,1)}) custom-call(f32[4,2,4,48,128]{4,3,2,1,0:T(8,128)} %bitcast.6, s32[2,512]{1,0:T(2,128)} %refs_1_.3, f32[2,3,8]{2,1,0:T(4,128)} %constant.11.clone.refs_2_, f32[2,8,128]{2,1,0:T(8,128)} %get-tuple-element.15.refs_1_.refs_3_, ...), custom_call_target="tpu_custom_call" | custom-call | tf_op jit(solution)/shard_map/exchange/pallas_call | solution.py:574
  42.9 28.7 %sweep.4 = (f32[1536,128]{1,0:T(8,128)}, f32[128,8,1024]{2,1,0:T(8,128)}) custom-call(s32[2,8,128]{2,1,0:T(8,128)} %get-tuple-element.14.refs_0_, f32[2,8,128]{2,1,0:T(8,128)} %get-tuple-element.15.refs_1_.refs_3_, s32[1,384]{1,0:T(1,128)} %get-tuple-element.16.refs_2_, f32[128,8,1024]{2,1,0:T(8,128)} %refs_3_.3, f32[1024,128]{1,0:T(8,128)} %constant.13.clone.refs_4_, ...), custom_call_target="tpu_custom_call" | custom-call | tf_op jit(solution)/shard_map/sweep/pallas_call | solution.py:638
  71.5 25.6 %exchange.3 = (bf16[4,2,4,48,128]{4,3,2,1,0:T(8,128)(2,1)}, f32[16,384]{1,0:T(8,128)}, bf16[32,128,1024]{2,1,0:T(8,128)(2,1)}) custom-call(f32[4,2,4,48,128]{4,3,2,1,0:T(8,128)} %bitcast.7, s32[2,512]{1,0:T(2,128)} %refs_1_.3, f32[2,3,8]{2,1,0:T(4,128)} %constant.11.clone.refs_2_, f32[2,8,128]{2,1,0:T(8,128)} %get-tuple-element.15.refs_1_.refs_3_, ...), custom_call_target="tpu_custom_call" | custom-call | tf_op jit(solution)/shard_map/exchange/pallas_call | solution.py:574
  97.1 15.5 %sweep.5 = (f32[128,8,1024]{2,1,0:T(8,128)}, f32[16,384]{1,0:T(8,128)}) custom-call(s32[2,8,128]{2,1,0:T(8,128)} %get-tuple-element.14.refs_0_, f32[2,8,128]{2,1,0:T(8,128)} %get-tuple-element.15.refs_1_.refs_3_, s32[1,384]{1,0:T(1,128)} %get-tuple-element.16.refs_2_, f32[128,8,1024]{2,1,0:T(8,128)} %get-tuple-element.19.refs_3_, ...), custom_call_target="tpu_custom_call" | custom-call | tf_op jit(solution)/shard_map/sweep/pallas_call | solution.py:638

commit v10 on v9

--- a/solution.py
+++ b/solution.py
@@ -27,7 +27,7 @@
 PAD = 32
 CHUNK = 32
 MADE = 4
-MADE_EARLY = (0, 5)
+MADE_EARLY = (2, 2)
 PARTS = 4
 DEPTH = 2
 EARLY = 3

time: 113 us -> 113 us (level)
  no operation moved by 1% of the time
where the time goes in v10:
time: 113 us
  Pallas kernels  112 us (99%)
    pallas_call x3, Pallas kernels, sweep(): pl.pallas_call(lambda *refs: sweep_kernel(back, fore, tall, names, *refs)...  59.8 us
    pallas_call x2, Pallas kernels, exchange(): pl.pallas_call(lambda *refs: exchange_kernel(subset, tall, *refs), in_spe...  50.8 us

profile of v10, /device:TPU:1, one launch (start us, length us, event | category | flops | bytes accessed | tf_op | source)
XLA Modules:
  0.0 112.9 jit_solution(13413273402622541527)
XLA Ops:
  0.6 1.4 %placing.1 = (s32[2,8,128]{2,1,0:T(8,128)}, f32[2,8,128]{2,1,0:T(8,128)}, s32[1,384]{1,0:T(1,128)}) custom-call(s32[1,128]{1,0:T(1,128)} %bitcast.11), custom_call_target="tpu_custom_call" | custom-call | tf_op jit(solution)/shard_map/placing/pallas_call | solution.py:688
  2.1 16.0 %sweep.3 = f32[1536,128]{1,0:T(8,128)} custom-call(s32[2,8,128]{2,1,0:T(8,128)} %get-tuple-element.14.refs_0_, f32[2,8,128]{2,1,0:T(8,128)} %get-tuple-element.15.refs_1_.refs_3_, s32[1,384]{1,0:T(1,128)} %get-tuple-element.16.refs_2_, f32[128,8,1024]{2,1,0:T(8,128)} %refs_3_.3, f32[1024,128]{1,0:T(8,128)} %constant.10.clone.refs_4_), custom_call_target="tpu_custom_call" | custom-call | tf_op jit(solution)/shard_map/sweep/pallas_call | solution.py:638
  18.1 24.5 %exchange.2 = (bf16[4,2,4,48,128]{4,3,2,1,0:T(8,128)(2,1)}, f32[16,384]{1,0:T(8,128)}, bf16[32,128,1024]{2,1,0:T(8,128)(2,1)}) custom-call(f32[4,2,4,48,128]{4,3,2,1,0:T(8,128)} %bitcast.6, s32[2,512]{1,0:T(2,128)} %refs_1_.3, f32[2,3,8]{2,1,0:T(4,128)} %constant.11.clone.refs_2_, f32[2,8,128]{2,1,0:T(8,128)} %get-tuple-element.15.refs_1_.refs_3_, ...), custom_call_target="tpu_custom_call" | custom-call | tf_op jit(solution)/shard_map/exchange/pallas_call | solution.py:574
  42.6 28.4 %sweep.4 = (f32[1536,128]{1,0:T(8,128)}, f32[128,8,1024]{2,1,0:T(8,128)}) custom-call(s32[2,8,128]{2,1,0:T(8,128)} %get-tuple-element.14.refs_0_, f32[2,8,128]{2,1,0:T(8,128)} %get-tuple-element.15.refs_1_.refs_3_, s32[1,384]{1,0:T(1,128)} %get-tuple-element.16.refs_2_, f32[128,8,1024]{2,1,0:T(8,128)} %refs_3_.3, f32[1024,128]{1,0:T(8,128)} %constant.13.clone.refs_4_, ...), custom_call_target="tpu_custom_call" | custom-call | tf_op jit(solution)/shard_map/sweep/pallas_call | solution.py:638
  71.0 26.3 %exchange.3 = (bf16[4,2,4,48,128]{4,3,2,1,0:T(8,128)(2,1)}, f32[16,384]{1,0:T(8,128)}, bf16[32,128,1024]{2,1,0:T(8,128)(2,1)}) custom-call(f32[4,2,4,48,128]{4,3,2,1,0:T(8,128)} %bitcast.7, s32[2,512]{1,0:T(2,128)} %refs_1_.3, f32[2,3,8]{2,1,0:T(4,128)} %constant.11.clone.refs_2_, f32[2,8,128]{2,1,0:T(8,128)} %get-tuple-element.15.refs_1_.refs_3_, ...), custom_call_target="tpu_custom_call" | custom-call | tf_op jit(solution)/shard_map/exchange/pallas_call | solution.py:574
  97.3 15.4 %sweep.5 = (f32[128,8,1024]{2,1,0:T(8,128)}, f32[16,384]{1,0:T(8,128)}) custom-call(s32[2,8,128]{2,1,0:T(8,128)} %get-tuple-element.14.refs_0_, f32[2,8,128]{2,1,0:T(8,128)} %get-tuple-element.15.refs_1_.refs_3_, s32[1,384]{1,0:T(1,128)} %get-tuple-element.16.refs_2_, f32[128,8,1024]{2,1,0:T(8,128)} %get-tuple-element.19.refs_3_, ...), custom_call_target="tpu_custom_call" | custom-call | tf_op jit(solution)/shard_map/sweep/pallas_call | solution.py:638
